TPU v7x, 32 devices: a whole 2x2x4 slice. The times are simulated.
32 devices in a mesh: ctx: 4 (over z), seq: 4 (over x, core), wsh: 2 (over y).
Axes of the slice: x: 2, y: 2, z: 4, core: 2. Of those that a mesh axis runs over, the one named last changes fastest.
Arguments:
- states: bfloat16 [8, 1536, 512], P(('seq', 'wsh'), 'ctx'), may hold values from -6 to 6
- remaining: float32 [8, 1536], P(('seq', 'wsh'), 'ctx'), may hold values from 0.2 to 1
- moa_ids: int32 [8, 1536, 4], P(('seq', 'wsh'), 'ctx'), may hold values from 0 to 23, all different within a row
- ffn_ids: int32 [8, 1536, 2], P(('seq', 'wsh'), 'ctx'), may hold values from 0 to 7, all different within a row; in each aligned block of 384 rows (0 to 383, 384 to 767, ..., all dimensions but the last counted through in order) at most 192 rows name the same one
- out_cotangent: float32 [8, 1536, 512], P(('seq', 'wsh'), 'ctx'), may hold values from -6 to 6
- left_cotangent: float32 [8, 1536], P(('seq', 'wsh'), 'ctx'), may hold values from -6 to 6
- query_weight: bfloat16 [512, 1536], P(('seq', 'wsh')), may hold values from -0.5 to 0.5
- keyval_weight: bfloat16 [512, 128], P(('seq', 'wsh')), may hold values from -0.25 to 0.25
- project_weight: bfloat16 [1536, 512], P(('seq', 'wsh')), may hold values from -6 to 6
- chooser: bfloat16 [512, 24], P(('seq', 'wsh')), may hold values from -0.125 to 0.125
- selector: bfloat16 [512, 8], P(('seq', 'wsh')), may hold values from -0.1875 to 0.1875
- gain_one: bfloat16 [512], P(('seq', 'wsh')), may hold values from 0.099609375 to 1.8984375
- bias_one: bfloat16 [512], P(('seq', 'wsh')), may hold values from -1 to 1
- gain_two: bfloat16 [512], P(('seq', 'wsh')), may hold values from 0.099609375 to 1.8984375
- bias_two: bfloat16 [512], P(('seq', 'wsh')), may hold values from -1 to 1
- halt_weight: bfloat16 [512], P(('seq', 'wsh')), may hold values from -0.25 to 0.25
- expert_in: bfloat16 [8, 512, 2048], P('ctx', ('seq', 'wsh')), may hold values from -0.25 to 0.25
- expert_out: bfloat16 [8, 2048, 512], P('ctx', ('seq', 'wsh')), may hold values from -0.25 to 0.25
Outputs:
- new_states: bfloat16 [8, 1536, 512], P(('seq', 'wsh'), 'ctx')
- remaining_next: float32 [8, 1536], P(('seq', 'wsh'), 'ctx')
- grad_states: float32 [8, 1536, 512], P(('seq', 'wsh'), 'ctx')
- grad_remaining: float32 [8, 1536], P(('seq', 'wsh'), 'ctx')
- grad_query: float32 [512, 1536], P(('seq', 'wsh'))
- grad_keyval: float32 [512, 128], P(('seq', 'wsh'))
- grad_project: float32 [1536, 512], P(('seq', 'wsh'))
- grad_chooser: float32 [512, 24], P(('seq', 'wsh'))
- grad_selector: float32 [512, 8], P(('seq', 'wsh'))
- grad_gain_one: float32 [512], P(('seq', 'wsh'))
- grad_bias_one: float32 [512], P(('seq', 'wsh'))
- grad_gain_two: float32 [512], P(('seq', 'wsh'))
- grad_bias_two: float32 [512], P(('seq', 'wsh'))
- grad_halt: float32 [512], P(('seq', 'wsh'))
- grad_expert_in: float32 [8, 512, 2048], P('ctx', ('seq', 'wsh'))
- grad_expert_out: float32 [8, 2048, 512], P('ctx', ('seq', 'wsh'))
Inputs may be any that keep to these rules, and one draw needn't show every extreme that they name: `moa_ids`: each row names 4 different attention experts. `ffn_ids`: within the rows of one device (aligned blocks of 384 positions) no expert is named more than 192 times, and in every draw some expert is named exactly 192 times by one device's rows. A row names two different experts.
All inputs are finite; a program needn't handle non-finite values.
Results may differ from a plain program's by a relative error of at most 0.025.
Values may be sent and summed in bfloat16 or wider, within the bound.
A program may use at most 192 MiB of HBM per device.

v0:
```python
from functools import partial

import jax
import jax.numpy as jnp
from jax import lax
from jax.sharding import PartitionSpec as P

D = 512
HS = 64
MOA_EXPERTS = 24
MOA_TOP = 4
EXP_DEV = 2
FFN_TOP = 2


EPS = 1e-05
HIGH = lax.Precision.HIGHEST


def shifted(x, axis, by):
    length = lax.axis_size(axis)
    return lax.ppermute(x, axis, [(i, (i + by) % length) for i in range(length)])


def layer_norm(values, gain, bias):
    centred = values - jnp.mean(values, -1, keepdims=True)
    inverse = lax.rsqrt(jnp.mean(centred * centred, -1, keepdims=True) + EPS)
    normal = centred * inverse
    return (normal * gain + bias, normal, inverse)


def norm_back(incoming, normal, inverse, gain):
    scaled = incoming * gain
    inner_term = (
        scaled
        - jnp.mean(scaled, -1, keepdims=True)
        - normal * jnp.mean(scaled * normal, -1, keepdims=True)
    )
    return (inverse * inner_term, jnp.sum(incoming * normal, 0), jnp.sum(incoming, 0))


def one_hot(index, count):
    return (index[..., None] == jnp.arange(count, dtype=jnp.int32)).astype(jnp.float32)


def choose_back(gates, upstream):
    return gates * (upstream - jnp.sum(gates * upstream, -1, keepdims=True))


def block_rows(row_count):
    if row_count > 512 and row_count % 512 == 0:
        return 512
    return row_count


def expert_slots(route_ids, experts):
    flat_ids = route_ids.reshape(-1)
    table = (flat_ids[:, None] == jnp.arange(experts, dtype=jnp.int32)[None, :]).astype(jnp.int32)
    earlier = jnp.cumsum(table, 0) - table
    return jnp.sum(earlier * table, 1).reshape(route_ids.shape)


def body(
    states,
    remaining,
    moa_ids,
    ffn_ids,
    out_cotangent,
    left_cotangent,
    query_weight,
    keyval_weight,
    project_weight,
    chooser,
    selector,
    gain_one,
    bias_one,
    gain_two,
    bias_two,
    halt_weight,
    expert_in,
    expert_out,
):
    tokens = states.shape[1]
    devices = lax.axis_size("ctx")
    experts = EXP_DEV * devices
    capacity = max(2, (4 * tokens + experts - 1) // experts)
    rows_total = tokens * MOA_TOP
    scaling = HS ** (-0.5)
    f32 = jnp.float32
    bf16 = jnp.bfloat16
    (
        query_full,
        keyval_full,
        project_full,
        chooser_full,
        selector_full,
        gainone_full,
        biasone_full,
        gaintwo_full,
        biastwo_full,
        halt_full,
    ) = (
        lax.all_gather(query_weight, ("seq", "wsh"), axis=0, tiled=True),
        lax.all_gather(keyval_weight, ("seq", "wsh"), axis=0, tiled=True),
        lax.all_gather(project_weight, ("seq", "wsh"), axis=0, tiled=True),
        lax.all_gather(chooser, ("seq", "wsh"), axis=0, tiled=True),
        lax.all_gather(selector, ("seq", "wsh"), axis=0, tiled=True),
        lax.all_gather(gain_one, ("seq", "wsh"), axis=0, tiled=True),
        lax.all_gather(bias_one, ("seq", "wsh"), axis=0, tiled=True),
        lax.all_gather(gain_two, ("seq", "wsh"), axis=0, tiled=True),
        lax.all_gather(bias_two, ("seq", "wsh"), axis=0, tiled=True),
        lax.all_gather(halt_weight, ("seq", "wsh"), axis=0, tiled=True),
    )
    inner_full, outer_full = (
        lax.all_gather(expert_in, ("seq", "wsh"), axis=1, tiled=True),
        lax.all_gather(expert_out, ("seq", "wsh"), axis=1, tiled=True),
    )
    gain_first = gainone_full.astype(f32)
    gain_second = gaintwo_full.astype(f32)
    halt_vector = halt_full.astype(f32)
    resident = states[0].astype(f32)
    normed_one, normal_one, inverse_one = layer_norm(resident, gain_first, biasone_full.astype(f32))
    acted = normed_one.astype(bf16)
    query_all = (
        jnp.dot(acted, query_full, preferred_element_type=f32)
        .astype(bf16)
        .reshape(tokens, MOA_EXPERTS, HS)
    )
    head_ids = moa_ids[0]
    query_sel = jnp.take_along_axis(query_all, head_ids[:, :, None], axis=1).reshape(rows_total, HS)
    keyval = jnp.dot(acted, keyval_full, preferred_element_type=f32).astype(bf16)
    chosen = one_hot(head_ids, MOA_EXPERTS)
    head_logits = jnp.sum(
        chosen * jnp.dot(acted, chooser_full, preferred_element_type=f32)[:, None, :], -1
    )
    head_gates = jax.nn.softmax(head_logits, -1)
    start_state = (
        jnp.full((rows_total,), -1e30, f32),
        jnp.zeros((rows_total,), f32),
        jnp.zeros((rows_total, HS), f32),
    )
    running = start_state
    shard_rows = lax.all_gather(keyval, "ctx", axis=0, tiled=True)
    block_size = block_rows(shard_rows.shape[0])
    grouped = shard_rows.reshape(shard_rows.shape[0] // block_size, block_size, 2 * HS)

    def absorb(carried, key_block):
        row_peak, row_total, gathered = carried
        scores = jnp.dot(query_sel, key_block[:, :HS].T, preferred_element_type=f32) * scaling
        new_peak = jnp.maximum(row_peak, jnp.max(scores, -1))
        fading = jnp.exp(row_peak - new_peak)
        weights = jnp.exp(scores - new_peak[:, None])
        row_total = row_total * fading + jnp.sum(weights, -1)
        gathered = gathered * fading[:, None] + jnp.dot(
            weights.astype(bf16), key_block[:, HS:], preferred_element_type=f32
        )
        return ((new_peak, row_total, gathered), None)

    running, unused = lax.scan(absorb, running, grouped)
    row_peak, row_total, gathered = running
    heads_out = gathered / row_total[:, None]
    log_total = row_peak + jnp.log(row_total)
    heads_view = heads_out.reshape(tokens, MOA_TOP, HS)
    mixed_sel = (head_gates[:, :, None] * heads_view).astype(bf16)
    chosen_low = chosen.astype(bf16)
    mixture = jnp.sum(chosen_low[:, :, :, None] * mixed_sel[:, :, None, :], 1).reshape(
        tokens, MOA_EXPERTS * HS
    )
    middle = resident + jnp.dot(mixture, project_full, preferred_element_type=f32)
    normed_two, normal_two, inverse_two = layer_norm(middle, gain_second, biastwo_full.astype(f32))
    entering = normed_two.astype(bf16)
    route_ids = ffn_ids[0]
    picked = one_hot(route_ids, experts)
    expert_logits = jnp.sum(
        picked * jnp.dot(entering, selector_full, preferred_element_type=f32)[:, None, :], -1
    )
    expert_gates = jax.nn.softmax(expert_logits, -1)
    slots = expert_slots(route_ids, experts)
    target = (route_ids * capacity + slots).reshape(-1)
    copies = jnp.broadcast_to(entering[:, None, :], (tokens, FFN_TOP, D)).reshape(-1, D)
    outgoing = (
        jnp.zeros((experts * capacity, D), bf16)
        .at[target]
        .set(copies)
        .reshape(devices, EXP_DEV, capacity, D)
    )
    arrived_rows = lax.all_to_all(outgoing, "ctx", split_axis=0, concat_axis=0, tiled=True)
    before = jnp.einsum("nekd,edf->nekf", arrived_rows, inner_full, preferred_element_type=f32)
    activated = jax.nn.gelu(before, approximate=False).astype(bf16)
    result_rows = jnp.einsum(
        "nekf,efd->nekd", activated, outer_full, preferred_element_type=f32
    ).astype(bf16)
    returned = lax.all_to_all(result_rows, "ctx", split_axis=0, concat_axis=0, tiled=True).reshape(
        experts * capacity, D
    )
    expert_rows = returned[target].reshape(tokens, FFN_TOP, D).astype(f32)
    final = middle + jnp.sum(expert_gates[:, :, None] * expert_rows, 1)
    halting = jax.nn.sigmoid(jnp.dot(final, halt_vector, precision=HIGH))
    left_mass = remaining[0]
    stopped = left_mass * halting
    new_states = (stopped[:, None] * resident + (1.0 - stopped)[:, None] * final).astype(bf16)
    remaining_next = left_mass * (1.0 - halting)
    out_grad = out_cotangent[0]
    left_grad = left_cotangent[0]
    stop_grad = jnp.sum(out_grad * (resident - final), -1)
    grad_remaining = stop_grad * halting + left_grad * (1.0 - halting)
    halt_logit_grad = (stop_grad - left_grad) * left_mass * halting * (1.0 - halting)
    grad_halt = jnp.sum(halt_logit_grad[:, None] * final, 0)
    grad_final = (1.0 - stopped)[:, None] * out_grad + halt_logit_grad[:, None] * halt_vector
    gate_grad = jnp.sum(grad_final[:, None, :] * expert_rows, -1)
    selector_logit_grad = jnp.sum(choose_back(expert_gates, gate_grad)[:, :, None] * picked, 1)
    entering_wide = entering.astype(f32)
    grad_selector = jnp.dot(entering_wide.T, selector_logit_grad, precision=HIGH)
    rows_grad = (expert_gates[:, :, None] * grad_final[:, None, :]).astype(bf16).reshape(-1, D)
    grad_outgoing = (
        jnp.zeros((experts * capacity, D), bf16)
        .at[target]
        .set(rows_grad)
        .reshape(devices, EXP_DEV, capacity, D)
    )
    grad_arrived = lax.all_to_all(grad_outgoing, "ctx", split_axis=0, concat_axis=0, tiled=True)
    grad_activated = jnp.einsum(
        "nekd,efd->nekf", grad_arrived, outer_full, preferred_element_type=f32
    )
    activated_again, gelu_back = jax.vjp(partial(jax.nn.gelu, approximate=False), before)
    before_grad = gelu_back(grad_activated)[0].astype(bf16)
    outer_grad = jnp.einsum(
        "nekf,nekd->efd", activated_again.astype(bf16), grad_arrived, preferred_element_type=f32
    )
    inner_grad = jnp.einsum("nekd,nekf->edf", arrived_rows, before_grad, preferred_element_type=f32)
    grad_sent = jnp.einsum(
        "nekf,edf->nekd", before_grad, inner_full, preferred_element_type=f32
    ).astype(bf16)
    grad_back = lax.all_to_all(grad_sent, "ctx", split_axis=0, concat_axis=0, tiled=True).reshape(
        experts * capacity, D
    )
    entering_grad = jnp.sum(grad_back[target].reshape(tokens, FFN_TOP, D).astype(f32), 1)
    entering_grad = entering_grad + jnp.dot(
        selector_logit_grad, selector_full.astype(f32).T, precision=HIGH
    )
    middle_extra, grad_gain_two, grad_bias_two = norm_back(
        entering_grad, normal_two, inverse_two, gain_second
    )
    middle_grad = grad_final + middle_extra
    attn_grad = middle_grad.astype(bf16)
    grad_project = jnp.dot(mixture.T, attn_grad, preferred_element_type=f32)
    mix_grad = jnp.dot(attn_grad, project_full.T, preferred_element_type=f32).reshape(
        tokens, MOA_EXPERTS, HS
    )
    mix_sel_grad = jnp.take_along_axis(mix_grad, head_ids[:, :, None], axis=1)
    head_gate_grad = jnp.sum(mix_sel_grad * heads_view, -1)
    chooser_logit_grad = jnp.sum(choose_back(head_gates, head_gate_grad)[:, :, None] * chosen, 1)
    acted_wide = acted.astype(f32)
    grad_chooser = jnp.dot(acted_wide.T, chooser_logit_grad, precision=HIGH)
    acted_grad = jnp.dot(chooser_logit_grad, chooser_full.astype(f32).T, precision=HIGH)
    heads_grad = (head_gates[:, :, None] * mix_sel_grad).astype(bf16).reshape(rows_total, HS)
    row_delta = jnp.sum(heads_grad.astype(f32) * heads_out, -1)

    def cycle_turn(turn_index, carried):
        visiting, grads_visiting, query_grad = carried
        block_size = block_rows(tokens)

        def per_block(query_acc, key_block):
            scores = jnp.dot(query_sel, key_block[:, :HS].T, preferred_element_type=f32) * scaling
            probability = jnp.exp(scores - log_total[:, None])
            prob_grad = jnp.dot(heads_grad, key_block[:, HS:].T, preferred_element_type=f32)
            score_grad = (probability * (prob_grad - row_delta[:, None])).astype(bf16)
            query_acc = (
                query_acc
                + jnp.dot(score_grad, key_block[:, :HS], preferred_element_type=f32) * scaling
            )
            keys_grad = jnp.dot(score_grad.T, query_sel, preferred_element_type=f32) * scaling
            values_grad = jnp.dot(
                probability.astype(bf16).T, heads_grad, preferred_element_type=f32
            )
            return (query_acc, jnp.concatenate([keys_grad, values_grad], -1))

        query_grad, block_grads = lax.scan(
            per_block, query_grad, visiting.reshape(tokens // block_size, block_size, 2 * HS)
        )
        grads_visiting = grads_visiting + block_grads.reshape(tokens, 2 * HS)
        visiting = shifted(visiting, "ctx", 1)
        grads_visiting = shifted(grads_visiting.astype(jnp.bfloat16), "ctx", 1).astype(
            grads_visiting.dtype
        )
        return (visiting, grads_visiting, query_grad)

    cycle_state = (keyval, jnp.zeros((tokens, 2 * HS), f32), jnp.zeros((rows_total, HS), f32))
    unused_keys, keyval_grad, query_grad = lax.fori_loop(0, devices, cycle_turn, cycle_state)
    query_sel_grad = query_grad.astype(bf16).reshape(tokens, MOA_TOP, HS)
    query_all_grad = jnp.sum(chosen_low[:, :, :, None] * query_sel_grad[:, :, None, :], 1).reshape(
        tokens, MOA_EXPERTS * HS
    )
    keyval_low = keyval_grad.astype(bf16)
    grad_query = jnp.dot(acted.T, query_all_grad, preferred_element_type=f32)
    grad_keyval = jnp.dot(acted.T, keyval_low, preferred_element_type=f32)
    acted_grad = acted_grad + jnp.dot(query_all_grad, query_full.T, preferred_element_type=f32)
    acted_grad = acted_grad + jnp.dot(keyval_low, keyval_full.T, preferred_element_type=f32)
    resident_grad, grad_gain_one, grad_bias_one = norm_back(
        acted_grad, normal_one, inverse_one, gain_first
    )
    grad_states = middle_grad + resident_grad + stopped[:, None] * out_grad
    dense_grads = (
        grad_query,
        grad_keyval,
        grad_project,
        grad_chooser,
        grad_selector,
        grad_gain_one,
        grad_bias_one,
        grad_gain_two,
        grad_bias_two,
        grad_halt,
    )
    totals = (
        lax.psum(dense_grads[0].astype(jnp.bfloat16), "ctx").astype(jnp.float32),
        lax.psum(dense_grads[1].astype(jnp.bfloat16), "ctx").astype(jnp.float32),
        lax.psum(dense_grads[2].astype(jnp.bfloat16), "ctx").astype(jnp.float32),
        lax.psum(dense_grads[3].astype(jnp.bfloat16), "ctx").astype(jnp.float32),
        lax.psum(dense_grads[4].astype(jnp.bfloat16), "ctx").astype(jnp.float32),
        lax.psum(dense_grads[5].astype(jnp.bfloat16), "ctx").astype(jnp.float32),
        lax.psum(dense_grads[6].astype(jnp.bfloat16), "ctx").astype(jnp.float32),
        lax.psum(dense_grads[7].astype(jnp.bfloat16), "ctx").astype(jnp.float32),
        lax.psum(dense_grads[8].astype(jnp.bfloat16), "ctx").astype(jnp.float32),
        lax.psum(dense_grads[9].astype(jnp.bfloat16), "ctx").astype(jnp.float32),
    )
    shards = (
        lax.psum_scatter(
            totals[0].astype(jnp.bfloat16), ("seq", "wsh"), scatter_dimension=0, tiled=True
        ).astype(jnp.float32),
        lax.psum_scatter(
            totals[1].astype(jnp.bfloat16), ("seq", "wsh"), scatter_dimension=0, tiled=True
        ).astype(jnp.float32),
        lax.psum_scatter(
            totals[2].astype(jnp.bfloat16), ("seq", "wsh"), scatter_dimension=0, tiled=True
        ).astype(jnp.float32),
        lax.psum_scatter(
            totals[3].astype(jnp.bfloat16), ("seq", "wsh"), scatter_dimension=0, tiled=True
        ).astype(jnp.float32),
        lax.psum_scatter(
            totals[4].astype(jnp.bfloat16), ("seq", "wsh"), scatter_dimension=0, tiled=True
        ).astype(jnp.float32),
        lax.psum_scatter(
            totals[5].astype(jnp.bfloat16), ("seq", "wsh"), scatter_dimension=0, tiled=True
        ).astype(jnp.float32),
        lax.psum_scatter(
            totals[6].astype(jnp.bfloat16), ("seq", "wsh"), scatter_dimension=0, tiled=True
        ).astype(jnp.float32),
        lax.psum_scatter(
            totals[7].astype(jnp.bfloat16), ("seq", "wsh"), scatter_dimension=0, tiled=True
        ).astype(jnp.float32),
        lax.psum_scatter(
            totals[8].astype(jnp.bfloat16), ("seq", "wsh"), scatter_dimension=0, tiled=True
        ).astype(jnp.float32),
        lax.psum_scatter(
            totals[9].astype(jnp.bfloat16), ("seq", "wsh"), scatter_dimension=0, tiled=True
        ).astype(jnp.float32),
    )
    inner_shard, outer_shard = (
        lax.psum_scatter(
            inner_grad.astype(jnp.bfloat16), ("seq", "wsh"), scatter_dimension=1, tiled=True
        ).astype(jnp.float32),
        lax.psum_scatter(
            outer_grad.astype(jnp.bfloat16), ("seq", "wsh"), scatter_dimension=1, tiled=True
        ).astype(jnp.float32),
    )
    return (
        new_states[None],
        remaining_next[None],
        grad_states[None],
        grad_remaining[None],
        shards[0],
        shards[1],
        shards[2],
        shards[3],
        shards[4],
        shards[5],
        shards[6],
        shards[7],
        shards[8],
        shards[9],
        inner_shard,
        outer_shard,
    )


def solution(mesh):
    in_specs = (
        P(("seq", "wsh"), "ctx", None),
        P(("seq", "wsh"), "ctx"),
        P(("seq", "wsh"), "ctx", None),
        P(("seq", "wsh"), "ctx", None),
        P(("seq", "wsh"), "ctx", None),
        P(("seq", "wsh"), "ctx"),
        P(("seq", "wsh"), None),
        P(("seq", "wsh"), None),
        P(("seq", "wsh"), None),
        P(("seq", "wsh"), None),
        P(("seq", "wsh"), None),
        P(("seq", "wsh")),
        P(("seq", "wsh")),
        P(("seq", "wsh")),
        P(("seq", "wsh")),
        P(("seq", "wsh")),
        P("ctx", ("seq", "wsh"), None),
        P("ctx", ("seq", "wsh"), None),
    )
    out_specs = (
        P(("seq", "wsh"), "ctx", None),
        P(("seq", "wsh"), "ctx"),
        P(("seq", "wsh"), "ctx", None),
        P(("seq", "wsh"), "ctx"),
        P(("seq", "wsh"), None),
        P(("seq", "wsh"), None),
        P(("seq", "wsh"), None),
        P(("seq", "wsh"), None),
        P(("seq", "wsh"), None),
        P(("seq", "wsh")),
        P(("seq", "wsh")),
        P(("seq", "wsh")),
        P(("seq", "wsh")),
        P(("seq", "wsh")),
        P("ctx", ("seq", "wsh"), None),
        P("ctx", ("seq", "wsh"), None),
    )
    return jax.shard_map(body, mesh=mesh, in_specs=in_specs, out_specs=out_specs, check_vma=False)
```

profile of v0, /device:TPU:0, one launch (start us, length us, event | category | flops | bytes accessed | tf_op | source)
XLA Modules:
  0.0 790.4 jit_solution(11110082044518483812)
XLA Ops:
  19.1 16.2 %all-reduce.11 = (bf16[512]{0:T(512)(128)(2,1)S(1)}, bf16[512]{0:T(512)(128)(2,1)S(1)}, bf16[512]{0:T(512)(128)(2,1)S(1)}, bf16[512]{0:T(512)(128)(2,1)S(1)}, bf16[512]{0:T(512)(128)(2,1)}) all-reduce(bf16[512]{0:T(512)(128)(2,1)S(1)} %dynamic-update-slice.1, ...), channel_id=1, replica_groups=mesh['ctx'=4,'seq'=4,'wsh'=2] {'seq','wsh'}, use_global_device_ids=true, to_apply=%add.1 | all-reduce | flops 2560 | bytes 10240
  38.8 14.0 %all-gather = bf16[8,64,24]{1,2,0:T(8,128)(2,1)S(1)} all-gather(bf16[1,64,24]{1,2,0:T(8,128)(2,1)} %bitcast.297), channel_id=1, replica_groups=mesh['ctx'=4,'seq'=4,'wsh'=2] {'seq','wsh'}, dimensions={0}, use_global_device_ids=true | all-gather | bytes 27648 | tf_op jit(solution)/shard_map/all_gather | solution.py:106
  54.3 16.4 %all_gather.42 = bf16[512,128]{1,0:T(8,128)(2,1)S(1)} all-gather(bf16[64,128]{1,0:T(8,128)(2,1)} %param.29), channel_id=1, replica_groups=mesh['ctx'=4,'seq'=4,'wsh'=2] {'seq','wsh'}, dimensions={0}, use_global_device_ids=true | all-gather | bytes 147456 | tf_op jit(solution)/shard_map/all_gather | solution.py:104
  71.4 1.7 reduce-window.6
  76.5 15.8 %all_gather.43 = bf16[1536,128]{1,0:T(8,128)(2,1)} all-gather(bf16[384,128]{1,0:T(8,128)(2,1)S(1)} %convolution_convert_fusion.4), channel_id=1, replica_groups=mesh['ctx'=4,'seq'=4,'wsh'=2] {'ctx'}, dimensions={0}, use_global_device_ids=true | all-gather | bytes 491520 | tf_op jit(solution)/shard_map/all_gather | solution.py:143
  93.0 2.2 convolution_convert_fusion.2
  95.2 1.4 copy.122
  96.6 2.8 copy.124
  99.5 15.6 %gather_fusion.2 = bf16[1536,64]{1,0:T(8,128)(2,1)} fusion(bf16[384,24,64]{2,1,0:T(8,128)(2,1)S(1)} %copy.124, s32[1536]{0:T(1024)S(1)} %reshape.539), kind=kCustom, calls=%fused_computation.2 | custom fusion | bytes 405504 | tf_op jit(solution)/shard_map/jit(take_along_axis)/gather | solution.py:130
  116.4 8.4 %while.35 = (s32[]{:T(128)}, f32[1536]{0:T(1024)S(1)}, f32[1536]{0:T(1024)S(1)}, f32[1536,64]{0,1:T(8,128)S(1)}, bf16[3,512,128]{2,1,0:T(8,128)(2,1)}, /*index=5*/bf16[1536,64]{1,0:T(8,128)(2,1)S(1)}, s32[]{:T(128)}, s32[]{:T(128)}) while((s32[]{:T(128)}, f32[1536]{0:T(1024)S(1)}, f32[1536]{0:T(1024)S(1)}, ...), condition=%wide.region_8.9_spmd.clone, body=%wide.region_5.8_spmd.clone.sunk | while | flops 206347776 | bytes 11042925 | solution.py:159
  127.5 2.7 fusion.129
  132.0 3.0 reshape.555
  135.0 7.5 scatter_custom_fusion
  142.5 5.4 all-to-all-start
  148.4 33.8 %all-to-all-done = bf16[4,2,192,512]{3,2,1,0:T(8,128)(2,1)S(1)} async-done(((bf16[4,2,192,512]{3,2,1,0:T(8,128)(2,1)}), bf16[4,2,192,512]{3,2,1,0:T(8,128)(2,1)S(1)}, u32[]{:S(2)}, u32[]{:S(2)}) %all-to-all-start) | async-done | bytes 1572896 | tf_op jit(solution)/shard_map/all_to_all | solution.py:187
  182.2 33.0 %fusion.27 = (bf16[4,2,192,2048]{3,2,0,1:T(8,128)(2,1)}, f32[4,2,192,2048]{3,2,0,1:T(8,128)}, f32[2,4,192,2048]{3,2,1,0:T(8,128)}) fusion(bf16[2,512,2048]{2,1,0:T(8,128)(2,1)} %all-gather.11.cloned.1.call-done, bf16[4,2,192,512]{3,2,1,0:T(8,128)(2,1)S(1)} %all-to-all-done), kind=kOutput, calls=%fused_computation.53 | convolution fusion | flops 3425697792 | bytes 37224448 | tf_op jit(solution)/shard_map/nekd,edf->nekf/dot_general | solution.py:188
  215.2 7.4 fusion.61
  224.0 3.6 all-to-all-start.1
  232.6 17.7 %all-gather.1 = bf16[8,64,8]{1,2,0:T(8,128)(2,1)S(1)} all-gather(bf16[1,64,8]{1,2,0:T(8,128)(2,1)} %bitcast.298), channel_id=1, replica_groups=mesh['ctx'=4,'seq'=4,'wsh'=2] {'seq','wsh'}, dimensions={0}, use_global_device_ids=true | all-gather | bytes 9216 | tf_op jit(solution)/shard_map/all_gather | solution.py:107
  256.7 7.2 all-to-all-done.1
  264.0 3.5 gather_fusion
  267.4 2.2 reshape.521
  269.6 2.4 multiply_reduce_fusion.3
  275.7 1.7 mul.454
  277.3 2.4 mul.455
  279.7 7.7 scatter_custom_fusion.1
  287.4 40.2 %all_to_all.20 = bf16[4,2,192,512]{3,2,1,0:T(8,128)(2,1)S(1)} all-to-all(bf16[4,2,192,512]{3,2,1,0:T(8,128)(2,1)} %bitcast.283), channel_id=1, replica_groups=mesh['ctx'=4,'seq'=4,'wsh'=2] {'ctx'}, dimensions={0} | all-to-all | bytes 3145728 | tf_op jit(solution)/shard_map/all_to_all | solution.py:221
  327.6 16.0 %fusion.24 = bf16[4,2,192,2048]{3,2,0,1:T(8,128)(2,1)} fusion(f32[4,2,192,2048]{3,2,0,1:T(8,128)} %get-tuple-element.236, f32[2,4,192,2048]{3,2,1,0:T(8,128)} %get-tuple-element.251, bf16[2,2048,512]{2,1,0:T(8,128)(2,1)} %all-gather.13.cloned.1.call-done, bf16[4,2,192,512]{3,2,1,0:T(8,128)(2,1)S(1)} %all_to_all.20), kind=kOutput, calls=%fused_computation.45 | convolution fusion | flops 3265265664 | bytes 37224448 | tf_op jit(solution)/shard_map/nekd,efd->nekf/dot_general | solution.py:222
  343.6 7.4 fusion.58
  352.4 3.6 all-to-all-start.3
  357.3 3.2 multiply_reduce_fusion.2
  364.4 27.6 %all-to-all-done.3 = bf16[4,2,192,512]{3,2,1,0:T(8,128)(2,1)S(1)} async-done(((bf16[4,2,192,512]{3,2,1,0:T(8,128)(2,1)}), bf16[4,2,192,512]{3,2,1,0:T(8,128)(2,1)S(1)}, u32[]{:S(2)}, u32[]{:S(2)}) %all-to-all-start.3) | async-done | bytes 1572896 | tf_op jit(solution)/shard_map/all_to_all | solution.py:234
  391.9 3.6 gather_fusion.1
  395.5 3.0 reshape.522
  398.5 3.3 reduce_sum.302
  401.8 2.2 multiply_reduce_fusion.5
  405.1 2.1 convolution_convert_fusion
  407.6 3.9 fusion.108
  411.4 5.0 copy.142
  416.5 23.0 %gather_fusion.3 = f32[1536,64]{1,0:T(8,128)} fusion(f32[384,24,64]{2,1,0:T(8,128)} %copy.142, s32[1536]{0:T(1024)S(1)} %copy-done.1), kind=kCustom, calls=%fused_computation.3 | custom fusion | bytes 798720 | tf_op jit(solution)/shard_map/jit(take_along_axis)/gather | solution.py:250
  439.5 2.7 multiply_reduce_fusion.7
  442.2 34.5 %while.36 = (s32[]{:T(128)}, bf16[384,128]{1,0:T(8,128)(2,1)S(1)}, f32[384,128]{0,1:T(8,128)S(1)}, f32[1536,64]{0,1:T(8,128)S(1)}, bf16[1536,64]{1,0:T(8,128)(2,...) while((s32[]{:T(128)}, bf16[384,128]{1,0:T(8,128)(2,1)S(1)}, ...), condition=%wide.region_33.34_spmd.clone, body=%wide.region_32.33_spmd.clone.sunk | while | flops 381591552 | bytes 14463168 | solution.py:289
  445.4 5.4 collective-permute-done.1
  454.1 5.3 collective-permute-done.1
  463.2 4.9 collective-permute-done.1
  471.9 4.9 collective-permute-done.1
  479.6 2.4 convolution_convert_fusion.1
  485.9 35.3 %reduce-scatter.16.cloned.1.call-done = bf16[64,1536]{1,0:T(8,128)(2,1)} async-done(((bf16[512,1536]{1,0:T(8,128)(2,1)}), bf16[64,1536]{1,0:T(8,128)(2,1)}) %reduce-scatter.16.cloned.1.call-update) | async-done | bytes 196624 | tf_op jit(solution)/shard_map/reduce_scatter | solution.py:328
  521.3 9.3 %bitcast_convert_fusion = bf16[2,2048,512]{2,1,0:T(8,128)(2,1)} fusion(bf16[4,2,192,2048]{3,2,0,1:T(8,128)(2,1)} %get-tuple-element.235, bf16[4,2,192,512]{3,2,1,0:T(8,128)(2,1)S(1)} %copy-done.28), kind=kOutput, calls=%fused_computation.67 | convolution fusion | flops 3223322624 | bytes 12058624 | tf_op jit(solution)/shard_map/nekf,nekd->efd/dot_general | solution.py:227
  532.0 7.9 bitcast_convert_fusion.1
  541.9 16.2 %reduce-scatter.24.cloned.1.call-done = bf16[64,8]{1,0:T(8,128)(2,1)} async-done(((bf16[512,8]{1,0:T(8,128)(2,1)}), bf16[64,8]{1,0:T(8,128)(2,1)}) %reduce-scatter.24.cloned.1.call-update) | async-done | bytes 1040
  559.8 2.9 fusion.84
  562.8 1.5 multiply_reduce_fusion.4
  564.3 13.7 %all-reduce.10 = (bf16[512]{0:T(512)(128)(2,1)S(1)}, bf16[512]{0:T(512)(128)(2,1)S(1)}, bf16[512]{0:T(512)(128)(2,1)S(1)}, bf16[512]{0:T(512)(128)(2,1)S(1)}, bf16[512]{0:T(512)(128)(2,1)S(1)}) all-reduce(bf16[512]{0:T(512)(128)(2,1)S(1)} %get-tuple-element.172, ...), channel_id=7, replica_groups=mesh['ctx'=4,'seq'=4,'wsh'=2] {'seq','wsh'}, use_global_device_ids=true, to_apply=%region_49.50.clone | all-reduce | flops 2560 | bytes 10240
  578.4 16.9 %reduce-scatter.22.cloned.1.call-done = bf16[64,24]{1,0:T(8,128)(2,1)} async-done(((bf16[512,24]{1,0:T(8,128)(2,1)}), bf16[64,24]{1,0:T(8,128)(2,1)}) %reduce-scatter.22.cloned.1.call-update) | async-done | bytes 3088
  596.1 36.2 %reduce-scatter.18.cloned.1.call-done = bf16[64,128]{1,0:T(8,128)(2,1)} async-done(((bf16[512,128]{1,0:T(8,128)(2,1)}), bf16[64,128]{1,0:T(8,128)(2,1)}) %reduce-scatter.18.cloned.1.call-update) | async-done | bytes 16400 | tf_op jit(solution)/shard_map/reduce_scatter | solution.py:331
  632.3 19.2 %all-reduce.12 = (bf16[64,128]{1,0:T(8,128)(2,1)S(1)}, bf16[64,24]{0,1:T(8,128)(2,1)S(1)}, bf16[64,8]{0,1:T(8,128)(2,1)S(1)}, bf16[64]{0:T(256)(128)(2,1)S(1)}, ...) all-reduce(bf16[64,128]{1,0:T(8,128)(2,1)} %reduce-scatter.18.clone, ...), channel_id=1, replica_groups=mesh['ctx'=4,'seq'=4,'wsh'=2] {'ctx'}, use_global_device_ids=true, to_apply=%region_39.40 | all-reduce | flops 10560 | bytes 42240 | tf_op jit(solution)/shard_map/psum | solution.py:317
  655.9 16.2 %all-reduce.16.cloned.1.call-done = (bf16[64,1536]{1,0:T(8,128)(2,1)}, bf16[192,512]{1,0:T(8,128)(2,1)}) async-done(((bf16[64,1536]{1,0:T(8,128)(2,1)}, bf16[192,512]{1,0:T(8,128)(2,1)}), (bf16[64,1536]{1,0:T(8,128)(2,1)}, bf16[192,512]{1,0:T(8,128)(2,1)})) %all-reduce.16.cloned.1.call-update) | async-done | bytes 393232 | tf_op jit(solution)/shard_map/psum | solution.py:316
  672.1 1.7 convert_element_type.280
  673.8 1.7 convert_element_type.284
  675.5 50.7 %reduce-scatter.14.cloned.1.call-done = bf16[2,256,512]{2,1,0:T(8,128)(2,1)} async-done(((bf16[2,2048,512]{2,1,0:T(8,128)(2,1)}), bf16[2,256,512]{2,1,0:T(8,128)(2,1)}) %reduce-scatter.14.cloned.1.call-update) | async-done | bytes 524304 | tf_op jit(solution)/shard_map/reduce_scatter | solution.py:363
  726.3 2.1 convert_element_type.302
  728.4 52.8 %reduce-scatter.12.cloned.1.call-done = bf16[2,64,2048]{2,1,0:T(8,128)(2,1)} async-done(((bf16[2,512,2048]{2,1,0:T(8,128)(2,1)}), bf16[2,64,2048]{2,1,0:T(8,128)(2,1)}) %reduce-scatter.12.cloned.1.call-update) | async-done | bytes 524304 | tf_op jit(solution)/shard_map/reduce_scatter | solution.py:360
  781.2 2.1 convert_element_type.300
  (376 shorter events, 89.3 us)
Async XLA Ops:
  7.2 67.5 %copy-start.39 = (s32[1,384,4]{1,2,0:T(4,128)S(1)}, s32[1,384,4]{1,2,0:T(4,128)}, u32[]{:S(2)}) copy-start(s32[1,384,4]{1,2,0:T(4,128)} %param.24) | copy-start | bytes 18436
  7.2 67.0 %copy-start.3 = (bf16[1,384,512]{2,1,0:T(8,128)(2,1)S(1)}, bf16[1,384,512]{2,1,0:T(8,128)(2,1)}, u32[]{:S(2)}) copy-start(bf16[1,384,512]{2,1,0:T(8,128)(2,1)} %param.22) | copy-start | bytes 1179652
  7.2 85.8 %all-gather.7.cloned.1.call-start = ((), (), s32[]{:S(2)}) async-start(), calls=%async_computation.11 | async-start | bytes 1769472 | tf_op jit(solution)/shard_map/all_gather | solution.py:103
  7.9 119.6 %all-gather.9.cloned.1.call-start = ((), (), s32[]{:S(2)}) async-start(), calls=%async_computation.12 | async-start | bytes 1769472 | tf_op jit(solution)/shard_map/all_gather | solution.py:105
  8.7 173.5 %all-gather.11.cloned.1.call-start = ((), (), s32[]{:S(2)}) async-start(), calls=%async_computation.13 | async-start | bytes 4718592 | tf_op jit(solution)/shard_map/all_gather | solution.py:115
  35.2 60.0 %copy-start.67 = (f32[512]{0:T(512)}, f32[512]{0:T(512)S(1)}, u32[]{:S(2)}) copy-start(f32[512]{0:T(512)S(1)} %convert_element_type.249) | copy-start | bytes 6148
  35.2 39.6 %copy-start.61 = (f32[512]{0:T(512)}, f32[512]{0:T(512)S(1)}, u32[]{:S(2)}) copy-start(f32[512]{0:T(512)S(1)} %convert_element_type.248) | copy-start | bytes 6148
  37.5 57.7 %copy-start.52 = (f32[384]{0:T(512)}, f32[384]{0:T(512)S(1)}, u32[]{:S(2)}) copy-start(f32[384]{0:T(512)S(1)} %broadcast_multiply_fusion.6) | copy-start | bytes 4612
  38.8 36.0 %copy-start.63 = (f32[384]{0:T(512)}, f32[384]{0:T(512)S(1)}, u32[]{:S(2)}) copy-start(f32[384]{0:T(512)S(1)} %add_rsqrt_fusion.1) | copy-start | bytes 4612
  53.0 21.9 %copy-start.35 = (bf16[512,24]{0,1:T(8,128)(2,1)}, bf16[512,24]{0,1:T(8,128)(2,1)S(1)}, u32[]{:S(2)}) copy-start(bf16[512,24]{0,1:T(8,128)(2,1)S(1)} %reshape.585) | copy-start | bytes 73732
  70.7 25.9 %copy-start.29 = (bf16[512,128]{1,0:T(8,128)(2,1)}, bf16[512,128]{1,0:T(8,128)(2,1)S(1)}, u32[]{:S(2)}) copy-start(bf16[512,128]{1,0:T(8,128)(2,1)S(1)} %all_gather.42) | copy-start | bytes 393220
  71.0 28.4 %copy-start = (s32[1536]{0:T(1024)}, s32[1536]{0:T(1024)S(1)}, u32[]{:S(2)}) copy-start(s32[1536]{0:T(1024)S(1)} %reshape.539) | copy-start | bytes 18436
  74.4 22.2 %copy-start.11 = (bf16[384,512]{1,0:T(8,128)(2,1)}, bf16[384,512]{1,0:T(8,128)(2,1)S(1)}, u32[]{:S(2)}) copy-start(bf16[384,512]{1,0:T(8,128)(2,1)S(1)} %fusion.77) | copy-start | bytes 1179652
  75.4 24.1 %copy-start.58 = (f32[384]{0:T(512)}, f32[384]{0:T(512)S(1)}, u32[]{:S(2)}) copy-start(f32[384]{0:T(512)S(1)} %fusion.120) | copy-start | bytes 4612
  75.7 23.8 %copy-start.21 = (bf16[384,128]{1,0:T(8,128)(2,1)}, bf16[384,128]{1,0:T(8,128)(2,1)S(1)}, u32[]{:S(2)}) copy-start(bf16[384,128]{1,0:T(8,128)(2,1)S(1)} %convolution_convert_fusion.4) | copy-start | bytes 294916
  116.4 9.0 %copy-start.23 = (f32[384,4]{1,0:T(8,128)S(1)}, f32[384,4]{1,0:T(8,128)}, u32[]{:S(2)}) copy-start(f32[384,4]{1,0:T(8,128)} %copy.120) | copy-start | bytes 18436
  130.2 12.3 %copy-start.44 = (f32[384]{0:T(512)}, f32[384]{0:T(512)S(1)}, u32[]{:S(2)}) copy-start(f32[384]{0:T(512)S(1)} %broadcast_multiply_fusion.5) | copy-start | bytes 4612
  130.5 12.0 %copy-start.55 = (f32[384]{0:T(512)}, f32[384]{0:T(512)S(1)}, u32[]{:S(2)}) copy-start(f32[384]{0:T(512)S(1)} %add_rsqrt_fusion) | copy-start | bytes 4612
  130.7 122.8 %copy-start.19 = (bf16[384,512]{1,0:T(8,128)(2,1)}, bf16[384,512]{1,0:T(8,128)(2,1)S(1)}, u32[]{:S(2)}) copy-start(bf16[384,512]{1,0:T(8,128)(2,1)S(1)} %add_convert_fusion) | copy-start | bytes 1179652
  142.5 39.7 %all-to-all-start = ((bf16[4,2,192,512]{3,2,1,0:T(8,128)(2,1)}), bf16[4,2,192,512]{3,2,1,0:T(8,128)(2,1)S(1)}, u32[]{:S(2)}, u32[]{:S(2)}) async-start(bf16[4,2,192,512]{3,2,1,0:T(8,128)(2,1)} %bitcast.282), calls=%async_computation | async-start | bytes 3145728 | tf_op jit(solution)/shard_map/all_to_all | solution.py:187
  147.9 67.3 %all-gather.13.cloned.1.call-start = ((), (), s32[]{:S(2)}) async-start(), calls=%async_computation.14 | async-start | bytes 4718592 | tf_op jit(solution)/shard_map/all_gather | solution.py:116
  182.2 33.0 %copy-start.25 = (bf16[4,2,192,512]{3,2,1,0:T(8,128)(2,1)}, bf16[4,2,192,512]{3,2,1,0:T(8,128)(2,1)S(1)}, u32[]{:S(2)}) copy-start(bf16[4,2,192,512]{3,2,1,0:T(8,128)(2,1)S(1)} %all-to-all-done) | copy-start | bytes 4718596
  224.0 40.0 %all-to-all-start.1 = ((bf16[4,2,192,512]{3,2,1,0:T(8,128)(2,1)}), bf16[4,2,192,512]{3,2,1,0:T(8,128)(2,1)S(1)}, u32[]{:S(2)}, u32[]{:S(2)}) async-start(bf16[4,2,192,512]{3,2,1,0:T(8,128)(2,1)} %copy.135), calls=%async_computation.1 | async-start | bytes 3145728 | tf_op jit(solution)/shard_map/all_to_all | solution.py:193
  274.6 12.9 %copy-start.48 = (f32[384]{0:T(512)}, f32[384]{0:T(512)S(1)}, u32[]{:S(2)}) copy-start(f32[384]{0:T(512)S(1)} %get-tuple-element.243) | copy-start | bytes 4612
  274.6 12.9 %copy-start.50 = (f32[384]{0:T(512)}, f32[384]{0:T(512)S(1)}, u32[]{:S(2)}) copy-start(f32[384]{0:T(512)S(1)} %get-tuple-element.245) | copy-start | bytes 4612
  327.6 16.0 %copy-start.27 = (bf16[4,2,192,512]{3,2,1,0:T(8,128)(2,1)}, bf16[4,2,192,512]{3,2,1,0:T(8,128)(2,1)S(1)}, u32[]{:S(2)}) copy-start(bf16[4,2,192,512]{3,2,1,0:T(8,128)(2,1)S(1)} %all_to_all.20) | copy-start | bytes 4718596
  352.4 39.5 %all-to-all-start.3 = ((bf16[4,2,192,512]{3,2,1,0:T(8,128)(2,1)}), bf16[4,2,192,512]{3,2,1,0:T(8,128)(2,1)S(1)}, u32[]{:S(2)}, u32[]{:S(2)}) async-start(bf16[4,2,192,512]{3,2,1,0:T(8,128)(2,1)} %copy.138), calls=%async_computation.3 | async-start | bytes 3145728 | tf_op jit(solution)/shard_map/all_to_all | solution.py:234
  355.9 130.0 %reduce-scatter.20.cloned.1.call-start = ((), (), s32[]{:S(2)}) async-start(), calls=%async_computation.19 | async-start | bytes 1769472 | tf_op jit(solution)/shard_map/reduce_scatter | solution.py:334
  391.9 9.9 %copy-start.43 = (bf16[512,8]{0,1:T(8,128)(2,1)S(1)}, bf16[512,8]{0,1:T(8,128)(2,1)}, u32[]{:S(2)}) copy-start(bf16[512,8]{0,1:T(8,128)(2,1)} %reshape.587) | copy-start | bytes 24580
  407.3 113.9 %reduce-scatter.16.cloned.1.call-start = ((), (), s32[]{:S(2)}) async-start(), calls=%async_computation.17 | async-start | bytes 1769472 | tf_op jit(solution)/shard_map/reduce_scatter | solution.py:328
  416.4 23.0 %copy-start.15 = (f32[1536,64]{1,0:T(8,128)S(1)}, f32[1536,64]{1,0:T(8,128)}, u32[]{:S(2)}) copy-start(f32[1536,64]{1,0:T(8,128)} %copy-done.14) | copy-start | bytes 1179652
  416.4 23.0 %copy-start.56 = (f32[1536]{0:T(1024)S(1)}, f32[1536]{0:T(1024)}, u32[]{:S(2)}) copy-start(f32[1536]{0:T(1024)} %div.87) | copy-start | bytes 18436
  416.4 23.0 %copy-start.60 = (pred[1536]{0:T(1024)(128)(4,1)S(1)}, pred[1536]{0:T(1024)(128)(4,1)}, u32[]{:S(2)}) copy-start(pred[1536]{0:T(1024)(128)(4,1)} %compare_and_fusion) | copy-start | bytes 4612
  416.4 25.7 %copy-start.13 = (f32[384,128]{0,1:T(8,128)S(1)}, f32[384,128]{0,1:T(8,128)}, u32[]{:S(2)}) copy-start(f32[384,128]{0,1:T(8,128)} %custom-call.7) | copy-start | bytes 589828
  416.5 25.7 %copy-start.22 = (bf16[384,128]{1,0:T(8,128)(2,1)S(1)}, bf16[384,128]{1,0:T(8,128)(2,1)}, u32[]{:S(2)}) copy-start(bf16[384,128]{1,0:T(8,128)(2,1)} %copy-done.21) | copy-start | bytes 294916
  416.5 25.7 %copy-start.34 = (f32[1536]{0:T(1024)S(1)}, f32[1536]{0:T(1024)}, u32[]{:S(2)}) copy-start(f32[1536]{0:T(1024)} %log_add_fusion) | copy-start | bytes 18436
  442.2 35.2 %copy-start.33 = (bf16[384,4,24]{0,2,1:T(8,128)(2,1)S(1)}, bf16[384,4,24]{0,2,1:T(8,128)(2,1)}, u32[]{:S(2)}) copy-start(bf16[384,4,24]{0,2,1:T(8,128)(2,1)} %convert_convert_fusion) | copy-start | bytes 221188
  442.2 37.4 %copy-start.53 = (f32[384]{0:T(512)S(1)}, f32[384]{0:T(512)}, u32[]{:S(2)}) copy-start(f32[384]{0:T(512)} %copy-done.52) | copy-start | bytes 4612
  442.2 37.4 %copy-start.62 = (f32[512]{0:T(512)S(1)}, f32[512]{0:T(512)}, u32[]{:S(2)}) copy-start(f32[512]{0:T(512)} %copy-done.61) | copy-start | bytes 6148
  442.2 37.4 %copy-start.64 = (f32[384]{0:T(512)S(1)}, f32[384]{0:T(512)}, u32[]{:S(2)}) copy-start(f32[384]{0:T(512)} %copy-done.63) | copy-start | bytes 4612
  442.2 37.4 %copy-start.68 = (f32[512]{0:T(512)S(1)}, f32[512]{0:T(512)}, u32[]{:S(2)}) copy-start(f32[512]{0:T(512)} %copy-done.67) | copy-start | bytes 6148
  442.3 8.6 %collective-permute-start = (bf16[384,128]{1,0:T(8,128)(2,1)S(1)}, bf16[384,128]{1,0:T(8,128)(2,1)S(1)}, u32[]{:S(2)}, u32[]{:S(2)}) collective-permute-start(bf16[384,128]{1,0:T(8,128)(2,1)S(1)} %copy.192), channel_id=1, source_target_pairs={{0,8},{8,16},{16,24},{24,0},{1,9},{9,17},{17,25},{25,1},{2,10},{10... | collective-permute-start | bytes 294920 | tf_op jit(solution)/shard_map/while/body/eval_jaxpr/ppermute | solution.py:22
  444.3 6.6 collective-permute-start.1
  450.9 8.6 %collective-permute-start = (bf16[384,128]{1,0:T(8,128)(2,1)S(1)}, bf16[384,128]{1,0:T(8,128)(2,1)S(1)}, u32[]{:S(2)}, u32[]{:S(2)}) collective-permute-start(bf16[384,128]{1,0:T(8,128)(2,1)S(1)} %copy.192), channel_id=1, source_target_pairs={{0,8},{8,16},{16,24},{24,0},{1,9},{9,17},{17,25},{25,1},{2,10},{10... | collective-permute-start | bytes 294920 | tf_op jit(solution)/shard_map/while/body/eval_jaxpr/ppermute | solution.py:22
  452.9 6.6 collective-permute-start.1
  459.5 8.6 %collective-permute-start = (bf16[384,128]{1,0:T(8,128)(2,1)S(1)}, bf16[384,128]{1,0:T(8,128)(2,1)S(1)}, u32[]{:S(2)}, u32[]{:S(2)}) collective-permute-start(bf16[384,128]{1,0:T(8,128)(2,1)S(1)} %copy.192), channel_id=1, source_target_pairs={{0,8},{8,16},{16,24},{24,0},{1,9},{9,17},{17,25},{25,1},{2,10},{10... | collective-permute-start | bytes 294920 | tf_op jit(solution)/shard_map/while/body/eval_jaxpr/ppermute | solution.py:22
  461.5 6.6 collective-permute-start.1
  468.2 8.6 %collective-permute-start = (bf16[384,128]{1,0:T(8,128)(2,1)S(1)}, bf16[384,128]{1,0:T(8,128)(2,1)S(1)}, u32[]{:S(2)}, u32[]{:S(2)}) collective-permute-start(bf16[384,128]{1,0:T(8,128)(2,1)S(1)} %copy.192), channel_id=1, source_target_pairs={{0,8},{8,16},{16,24},{24,0},{1,9},{9,17},{17,25},{25,1},{2,10},{10... | collective-permute-start | bytes 294920 | tf_op jit(solution)/shard_map/while/body/eval_jaxpr/ppermute | solution.py:22
  470.2 6.6 collective-permute-start.1
  479.6 41.6 %copy-start.28 = (bf16[4,2,192,512]{3,2,1,0:T(8,128)(2,1)S(1)}, bf16[4,2,192,512]{3,2,1,0:T(8,128)(2,1)}, u32[]{:S(2)}) copy-start(bf16[4,2,192,512]{3,2,1,0:T(8,128)(2,1)} %copy-done.27) | copy-start | bytes 4718596
  482.1 76.0 %reduce-scatter.24.cloned.1.call-start = ((), (), s32[]{:S(2)}) async-start(), calls=%async_computation.21 | async-start | bytes 147456
  483.2 112.1 %reduce-scatter.22.cloned.1.call-start = ((), (), s32[]{:S(2)}) async-start(), calls=%async_computation.20 | async-start | bytes 147456
  484.8 147.5 %reduce-scatter.18.cloned.1.call-start = ((), (), s32[]{:S(2)}) async-start(), calls=%async_computation.18 | async-start | bytes 147456 | tf_op jit(solution)/shard_map/reduce_scatter | solution.py:331
  485.8 186.3 %all-reduce.16.cloned.1.call-start = ((), (), s32[]{:S(2)}) async-start(), calls=%async_computation.22 | async-start | bytes 786432 | tf_op jit(solution)/shard_map/psum | solution.py:316
  521.2 205.1 %reduce-scatter.14.cloned.1.call-start = ((), (), s32[]{:S(2)}) async-start(), calls=%async_computation.16 | async-start | bytes 4718592 | tf_op jit(solution)/shard_map/reduce_scatter | solution.py:363
  530.6 250.6 %reduce-scatter.12.cloned.1.call-start = ((), (), s32[]{:S(2)}) async-start(), calls=%async_computation.15 | async-start | bytes 4718592 | tf_op jit(solution)/shard_map/reduce_scatter | solution.py:360
  539.9 19.0 %copy-start.36 = (bf16[512,24]{0,1:T(8,128)(2,1)S(1)}, bf16[512,24]{0,1:T(8,128)(2,1)}, u32[]{:S(2)}) copy-start(bf16[512,24]{0,1:T(8,128)(2,1)} %copy-done.35) | copy-start | bytes 73732
  539.9 19.6 %copy-start.30 = (bf16[512,128]{1,0:T(8,128)(2,1)S(1)}, bf16[512,128]{1,0:T(8,128)(2,1)}, u32[]{:S(2)}) copy-start(bf16[512,128]{1,0:T(8,128)(2,1)} %copy-done.29) | copy-start | bytes 393220
  539.9 22.8 %copy-start.5 = (f32[384,512]{1,0:T(8,128)S(1)}, f32[384,512]{1,0:T(8,128)}, u32[]{:S(2)}) copy-start(f32[384,512]{1,0:T(8,128)} %copy-done.4) | copy-start | bytes 2359300
  539.9 22.8 %copy-start.8 = (f32[1,384,512]{2,1,0:T(8,128)S(1)}, f32[1,384,512]{2,1,0:T(8,128)}, u32[]{:S(2)}) copy-start(f32[1,384,512]{2,1,0:T(8,128)} %param.26) | copy-start | bytes 2359300
  539.9 22.8 %copy-start.18 = (f32[384,512]{1,0:T(8,128)S(1)}, f32[384,512]{1,0:T(8,128)}, u32[]{:S(2)}) copy-start(f32[384,512]{1,0:T(8,128)} %copy-done.17) | copy-start | bytes 2359300
  539.9 22.8 %copy-start.49 = (f32[384]{0:T(512)S(1)}, f32[384]{0:T(512)}, u32[]{:S(2)}) copy-start(f32[384]{0:T(512)} %copy-done.48) | copy-start | bytes 4612
  539.9 22.8 %copy-start.51 = (f32[384]{0:T(512)S(1)}, f32[384]{0:T(512)}, u32[]{:S(2)}) copy-start(f32[384]{0:T(512)} %copy-done.50) | copy-start | bytes 4612
  539.9 22.8 %copy-start.66 = (f32[384]{0:T(512)S(1)}, f32[384]{0:T(512)}, u32[]{:S(2)}) copy-start(f32[384]{0:T(512)} %get-tuple-element.246) | copy-start | bytes 4612
  (36 other events, 147.0 us)
Sparse Core Ops, SparseCore 0:
  9.9 28.6 all-gather.6
  40.4 25.8 all-gather.8
  68.3 36.7 all-gather.10
  150.3 37.0 all-gather.12
  407.4 38.4 reduce-scatter.19
  482.2 38.9 reduce-scatter.15
  524.7 33.3 reduce-scatter.23
  562.0 33.3 reduce-scatter.21
  598.9 33.3 reduce-scatter.17
  634.7 37.3 all-reduce.15
  675.5 50.7 reduce-scatter.13
  729.9 51.3 reduce-scatter.11
where the time goes:
time: 797 us; the launch traced here: 790 us
  waiting for transfers between devices  316 us (40%)
  blocking collectives  153 us (19%)
  matrix products  117 us (15%)
  local copies, waits for them, and re-layouts  107 us (13%)
  other arithmetic  61.8 us (8%)
  starting transfers between devices  17.3 us (2%)
  between operations  17.2 us (2%)
    reduce_scatter x1, waiting for transfers between devices, body(): lax.psum_scatter(inner_grad.astype(jnp.bfloat16), ('seq', 'wsh'), scatter...  52.8 us
    reduce_scatter x1, waiting for transfers between devices, body(): lax.psum_scatter(outer_grad.astype(jnp.bfloat16), ('seq', 'wsh'), scatter...  50.7 us
    all_to_all x1, blocking collectives, body(): lax.all_to_all(grad_outgoing, 'ctx', split_axis=0, concat_axis=0, tiled=T...  40.2 us
    reduce_scatter x1, waiting for transfers between devices, body(): lax.psum_scatter(totals[1].astype(jnp.bfloat16), ('seq', 'wsh'), scatter_...  36.2 us
    unnamed x14, waiting for transfers between devices  35.9 us
    reduce_scatter x1, waiting for transfers between devices, body(): lax.psum_scatter(totals[0].astype(jnp.bfloat16), ('seq', 'wsh'), scatter_...  35.3 us
    all_to_all x1, waiting for transfers between devices, body(): lax.all_to_all(outgoing, 'ctx', split_axis=0, concat_axis=0, tiled=True)  33.8 us
    dot_general x1, matrix products, body(): jnp.einsum('nekd,edf->nekf', arrived_rows, inner_full, preferred_element_...  33 us
  transfers between devices with their start and end apart: 23, of which 14 were waited for; matrix products, arithmetic and copies ran while one was open for 26% of the time, Pallas kernels for 0%

commit v1 on v0

--- a/solution.py
+++ b/solution.py
@@ -3,6 +3,8 @@
 import jax
 import jax.numpy as jnp
 from jax import lax
+from jax.experimental import pallas as pl
+from jax.experimental.pallas import tpu as pltpu
 from jax.sharding import PartitionSpec as P
 
 D = 512
@@ -11,6 +13,7 @@
 MOA_TOP = 4
 EXP_DEV = 2
 FFN_TOP = 2
+FF = 2048
 
 
 EPS = 1e-05
@@ -55,12 +58,14 @@
 
 def expert_slots(route_ids, experts):
     flat_ids = route_ids.reshape(-1)
-    table = (flat_ids[:, None] == jnp.arange(experts, dtype=jnp.int32)[None, :]).astype(jnp.int32)
-    earlier = jnp.cumsum(table, 0) - table
-    return jnp.sum(earlier * table, 1).reshape(route_ids.shape)
-
-
-def body(
+    table = (flat_ids[:, None] == jnp.arange(experts, dtype=jnp.int32)[None, :]).astype(jnp.float32)
+    place = jnp.arange(flat_ids.shape[0], dtype=jnp.int32)
+    before = (place[None, :] < place[:, None]).astype(jnp.bfloat16)
+    earlier = jnp.dot(before, table.astype(jnp.bfloat16), preferred_element_type=jnp.float32)
+    return jnp.sum(earlier * table, 1).astype(jnp.int32).reshape(route_ids.shape)
+
+
+def general_body(
     states,
     remaining,
     moa_ids,
@@ -384,6 +389,866 @@
     )
 
 
+MESH = pl.DeviceIdType.MESH
+CAP = 192
+KEEP = 0.7071067811865476
+SPREAD = 0.3989422804014327
+ERF_P = 0.3275911
+ERF_A = (0.254829592, -0.284496736, 1.421413741, -1.453152027, 1.061405429)
+
+
+def remote(source, target, send_sem, recv_sem, device):
+    return pltpu.make_async_remote_copy(
+        src_ref=source,
+        dst_ref=target,
+        send_sem=send_sem,
+        recv_sem=recv_sem,
+        device_id=device,
+        device_id_type=MESH,
+    )
+
+
+def places():
+    ctx, seq, wsh = (lax.axis_index(name) for name in ("ctx", "seq", "wsh"))
+    chip, core = seq // 2, seq % 2
+    over = (1 - chip) * 2 + core
+    twin = (ctx, chip * 2 + 1 - core, wsh)
+    beside = (ctx, over, wsh)
+    above = (ctx, seq, 1 - wsh)
+    across = (ctx, over, 1 - wsh)
+    return (ctx, seq, wsh), twin, beside, above, across
+
+
+def shard_of(place):
+    return place[1] * 2 + place[2]
+
+
+def moved(place, offset, length):
+    return ((place[0] + offset) % length, place[1], place[2])
+
+
+class PlaneGather:
+    def __init__(self, shard, full, halves, send, recv, local):
+        self.shard, self.full, self.halves = shard, full, halves
+        self.send, self.recv, self.local = send, recv, local
+        self.me, self.twin, self.beside, self.above, self.across = places()
+
+    def pair(self, view, slot, device):
+        return remote(view, view, self.send.at[slot], self.recv.at[slot], device)
+
+    def own(self, slot, device):
+        target = self.full(shard_of(self.me))
+        return remote(self.shard, target, self.send.at[slot], self.recv.at[slot], device)
+
+    def keep(self):
+        return pltpu.make_async_copy(self.shard, self.full(shard_of(self.me)), self.local)
+
+    def start(self):
+        self.own(0, self.twin).start()
+        self.own(1, self.beside).start()
+        self.own(2, self.above).start()
+        if self.halves is None:
+            self.own(3, self.across).start()
+        self.keep().start()
+
+    def arrive(self, slot, place):
+        self.pair(self.full(shard_of(place)), slot, self.twin).wait_recv()
+
+    def relay(self):
+        if self.halves is None:
+            for slot, place in ((1, self.beside), (2, self.above), (3, self.across)):
+                self.arrive(slot, place)
+                self.pair(self.full(shard_of(place)), slot + 3, self.twin).start()
+            return
+        self.arrive(1, self.beside)
+        self.pair(self.halves(shard_of(self.beside), 1), 7, self.above).start()
+        self.pair(self.full(shard_of(self.beside)), 4, self.twin).start()
+        self.arrive(2, self.above)
+        self.pair(self.halves(shard_of(self.above), 0), 3, self.beside).start()
+        self.pair(self.full(shard_of(self.above)), 5, self.twin).start()
+
+    def relay_rest(self):
+        shard = shard_of(self.across)
+        for slot, half in ((3, 0), (7, 1)):
+            view = self.halves(shard, half)
+            self.pair(view, slot, self.twin).wait_recv()
+            self.pair(view, 6 if half == 0 else 8, self.twin).start()
+
+    def finish(self):
+        self.keep().wait()
+        ctx, seq, wsh = self.twin
+        over = (1 - seq // 2) * 2 + seq % 2
+        self.arrive(0, self.twin)
+        self.arrive(4, (ctx, over, wsh))
+        self.arrive(5, (ctx, seq, 1 - wsh))
+        rest = shard_of((ctx, over, 1 - wsh))
+        if self.halves is None:
+            self.pair(self.full(rest), 6, self.twin).wait_recv()
+        else:
+            self.pair(self.halves(rest, 0), 6, self.twin).wait_recv()
+            self.pair(self.halves(rest, 1), 8, self.twin).wait_recv()
+
+    def drain(self):
+        self.own(0, self.twin).wait_send()
+        self.own(1, self.beside).wait_send()
+        self.own(2, self.above).wait_send()
+        beside, above, across = (shard_of(p) for p in (self.beside, self.above, self.across))
+        self.pair(self.full(beside), 4, self.twin).wait_send()
+        self.pair(self.full(above), 5, self.twin).wait_send()
+        if self.halves is None:
+            self.own(3, self.across).wait_send()
+            self.pair(self.full(across), 6, self.twin).wait_send()
+        else:
+            self.pair(self.halves(above, 0), 3, self.beside).wait_send()
+            self.pair(self.halves(beside, 1), 7, self.above).wait_send()
+            self.pair(self.halves(across, 0), 6, self.twin).wait_send()
+            self.pair(self.halves(across, 1), 8, self.twin).wait_send()
+
+
+class LineGather:
+    def __init__(self, length, blocks, send, recv):
+        self.length, self.blocks, self.send, self.recv = length, blocks, send, recv
+        self.me = places()[0]
+
+    def hop(self, block, way, step, device):
+        view = self.blocks(block)
+        return remote(view, view, self.send.at[way, step], self.recv.at[way, step], device)
+
+    def ways(self, step):
+        ctx = self.me[0]
+        left = (ctx - 1, self.me[1], self.me[2])
+        right = (ctx + 1, self.me[1], self.me[2])
+        return (
+            (0, ctx - step, ctx - step >= 0, right, ctx + 1 < self.length),
+            (1, ctx + step, ctx + step < self.length, left, ctx - 1 >= 0),
+        )
+
+    def start(self):
+        for way, block, unused, device, there in self.ways(0):
+            pl.when(there)(lambda b=block, w=way, d=device: self.hop(b, w, 0, d).start())
+
+    def relay(self, step):
+        for way, block, come, device, there in self.ways(step):
+
+            def pass_on(way=way, block=block, device=device, there=there):
+                self.hop(block, way, step - 1, device).wait_recv()
+                if step < self.length - 1:
+                    pl.when(there)(lambda: self.hop(block, way, step, device).start())
+
+            pl.when(come)(pass_on)
+
+    def drain(self):
+        for step in range(self.length - 1):
+            for way, block, come, device, there in self.ways(step):
+                pl.when(jnp.logical_and(come, there))(
+                    lambda b=block, w=way, d=device, s=step: self.hop(b, w, s, d).wait_send()
+                )
+
+
+def direct_send(view, send, recv, length):
+    me = places()[0]
+    return [
+        remote(view, view, send.at[step - 1], recv.at[step - 1], moved(me, step, length))
+        for step in range(1, length)
+    ]
+
+
+def direct_wait(view_of, send, recv, length):
+    me = places()[0]
+    for step in range(1, length):
+        source = moved(me, length - step, length)
+        view = view_of(source[0])
+        remote(view, view, send.at[step - 1], recv.at[step - 1], source).wait_recv()
+
+
+def lanes_of(shape):
+    return lax.broadcasted_iota(jnp.int32, shape, 1)
+
+
+def rows_of(shape):
+    return lax.broadcasted_iota(jnp.int32, shape, 0)
+
+
+def product(left, right, dims=((1,), (0,))):
+    return lax.dot_general(left, right, (dims, ((), ())), preferred_element_type=jnp.float32)
+
+
+def gelu_parts(values):
+    near = jnp.abs(values) * KEEP
+    turn = 1.0 / (1.0 + ERF_P * near)
+    bell = jnp.exp(-near * near)
+    series = ERF_A[4]
+    for term in ERF_A[3::-1]:
+        series = series * turn + term
+    tail = 0.5 * series * turn * bell
+    share = jnp.where(values >= 0, 1.0 - tail, tail)
+    return values * share, share + values * bell * SPREAD
+
+
+def forward_kernel(
+    length,
+    states,
+    cotangent,
+    head_ids,
+    route_ids,
+    pack,
+    query_part,
+    project_part,
+    inner_part,
+    outer_part,
+    slot_rows,
+    active,
+    slope,
+    result,
+    slot_cot,
+    inner,
+    outer,
+    query,
+    project,
+    packed,
+    acted,
+    mixture,
+    queries,
+    heads,
+    keyval,
+    head_gates,
+    middle,
+    entering,
+    cots,
+    routes,
+    scores_back,
+    small,
+    normal,
+    score_sent,
+    plane_send,
+    plane_recv,
+    plane_local,
+    line_send,
+    line_recv,
+    direct_sems,
+    direct_recvs,
+):
+    f32, bf16 = jnp.float32, jnp.bfloat16
+    tokens = states.shape[0]
+    me, twin, beside, above, across = places()
+    ctx = me[0]
+    experts = EXP_DEV * length
+    peers = [twin, beside, above, across] + [moved(me, k, length) for k in range(1, length)]
+    barrier = pltpu.get_barrier_semaphore()
+    for peer in peers:
+        pl.semaphore_signal(barrier, inc=1, device_id=peer, device_id_type=MESH)
+
+    def gather(index, shard, full, halves=None):
+        return PlaneGather(
+            shard, full, halves, plane_send.at[index], plane_recv.at[index], plane_local.at[index]
+        )
+
+    def rows_view(ref, rows):
+        return lambda shard: ref.at[pl.ds(shard * rows, rows), :]
+
+    pack_gather = gather(0, pack, rows_view(packed, 64))
+    query_gather = gather(1, query_part, rows_view(query, 64))
+    project_gather = gather(2, project_part, rows_view(project, 192))
+    inner_gather = gather(
+        3,
+        inner_part,
+        lambda shard: inner.at[:, pl.ds(shard * 64, 64), :],
+        lambda shard, half: inner.at[half, pl.ds(shard * 64, 64), :],
+    )
+    outer_gather = gather(
+        4,
+        outer_part,
+        lambda shard: outer.at[:, pl.ds(shard * 256, 256), :],
+        lambda shard, half: outer.at[half, pl.ds(shard * 256, 256), :],
+    )
+    cot_gather = LineGather(length, lambda b: cots.at[b], line_send.at[0], line_recv.at[0])
+    entering_gather = LineGather(length, lambda b: entering.at[b], line_send.at[1], line_recv.at[1])
+
+    def keyval_view(block):
+        return keyval.at[pl.ds(block * tokens, tokens), :]
+
+    cots[ctx] = cotangent[...].astype(bf16)
+    pl.semaphore_wait(barrier, len(peers))
+    pack_gather.start()
+    query_gather.start()
+    cot_gather.start()
+
+    values = states[...].astype(f32)
+    centred = values - jnp.mean(values, -1, keepdims=True)
+    inverse = lax.rsqrt(jnp.mean(centred * centred, -1, keepdims=True) + EPS)
+    normal[...] = centred * inverse
+
+    lane = lanes_of((tokens, 128))
+    ids = route_ids[...].astype(f32)
+    both = jnp.where(lane == 0, ids[:, 0:1], ids[:, 1:2])
+    turned = jnp.transpose(both)[0:8]
+    expert_row = rows_of((8, tokens)).astype(f32)
+    picked = jnp.logical_or(expert_row == turned[0:1], expert_row == turned[1:2])
+    marks = jnp.concatenate([picked.astype(f32), jnp.zeros((8, tokens), f32)], 0).astype(bf16)
+    earlier = (rows_of((tokens, tokens)) < lanes_of((tokens, tokens))).astype(f32).astype(bf16)
+    ranks = product(marks, earlier)[0:8]
+    routes[ctx, 0:8, :] = jnp.where(picked, ranks, -1.0)
+
+    pack_gather.relay()
+    pack_gather.finish()
+    small[...] = jnp.transpose(packed[:, 128:256].astype(f32))
+    shaped = (normal[...] * small[32:33, :] + small[33:34, :]).astype(bf16)
+    acted[...] = shaped
+    sides = product(shaped, packed[...])
+    keyval_view(ctx)[...] = sides[:, 0:128].astype(bf16)
+    keyval_sends = direct_send(keyval_view(ctx), direct_sems.at[0], direct_recvs.at[0], length)
+    for copy in keyval_sends:
+        copy.start()
+
+    id_lanes = [head_ids[:, j : j + 1] for j in range(MOA_TOP)]
+    logits = [
+        jnp.sum(jnp.where(lane == id_lanes[j], sides[:, 128:256], 0.0), -1, keepdims=True)
+        for j in range(MOA_TOP)
+    ]
+    peak = jnp.maximum(jnp.maximum(logits[0], logits[1]), jnp.maximum(logits[2], logits[3]))
+    powers = [jnp.exp(item - peak) for item in logits]
+    total = powers[0] + powers[1] + powers[2] + powers[3]
+    gates = [item / total for item in powers]
+    head_gates[...] = jnp.where(
+        lane == 0,
+        gates[0],
+        jnp.where(lane == 1, gates[1], jnp.where(lane == 2, gates[2], gates[3])),
+    )
+
+    query_gather.relay()
+    project_gather.start()
+    inner_gather.start()
+    query_gather.finish()
+    for part in range(6):
+        columns = slice(part * 256, part * 256 + 256)
+        mixture[:, columns] = product(acted[...], query[:, columns]).astype(bf16)
+    cot_gather.relay(1)
+
+    low_half = lane < HS
+    side = lane // HS
+    for j in range(MOA_TOP):
+        wanted = id_lanes[j] - side
+        chosen = jnp.zeros((tokens, 128), f32)
+        for pair in range(MOA_EXPERTS // 2):
+            block = mixture[:, pair * 128 : pair * 128 + 128].astype(f32)
+            chosen = chosen + jnp.where(wanted == 2 * pair, block, 0.0)
+        folded = chosen + pltpu.roll(chosen, HS, 1)
+        queries[j * tokens : (j + 1) * tokens, :] = (
+            jnp.where(low_half, folded, 0.0) * HS ** (-0.5)
+        ).astype(bf16)
+
+    direct_wait(keyval_view, direct_sems.at[0], direct_recvs.at[0], length)
+    chunk = 256
+
+    def attend(turn, carried):
+        rows = pl.ds(pl.multiple_of(turn * chunk, chunk), chunk)
+        scores = product(queries[rows, :], keyval[...], ((1,), (1,)))
+        top = jnp.max(scores, -1, keepdims=True)
+        weights = jnp.exp(scores - top)
+        mass = jnp.sum(weights, -1, keepdims=True)
+        seen = product(weights.astype(bf16), keyval[...]) / mass
+        heads[rows, :] = jnp.where(lanes_of((chunk, 128)) < HS, top + jnp.log(mass), seen)
+        return carried
+
+    lax.fori_loop(0, MOA_TOP * tokens // chunk, attend, 0)
+    project_gather.relay()
+
+    spread = []
+    for j in range(MOA_TOP):
+        head = heads[j * tokens : (j + 1) * tokens, :]
+        both = jnp.where(low_half, pltpu.roll(head, HS, 1), head)
+        spread.append(both * head_gates[:, j : j + 1])
+    for pair in range(MOA_EXPERTS // 2):
+        block = jnp.zeros((tokens, 128), f32)
+        for j in range(MOA_TOP):
+            block = jnp.where(id_lanes[j] - side == 2 * pair, spread[j], block)
+        mixture[:, pair * 128 : pair * 128 + 128] = block.astype(bf16)
+
+    project_gather.finish()
+    between = states[...].astype(f32) + product(mixture[...], project[...])
+    middle[...] = between
+    centred = between - jnp.mean(between, -1, keepdims=True)
+    inverse = lax.rsqrt(jnp.mean(centred * centred, -1, keepdims=True) + EPS)
+    entry = (centred * inverse * small[34:35, :] + small[35:36, :]).astype(bf16)
+    entering[ctx] = entry
+    entering_gather.start()
+    logits = product(small[16:32, :].astype(bf16), entry, ((1,), (1,)))[8:16]
+    peak = jnp.max(jnp.where(picked, logits, -1e30), 0, keepdims=True)
+    powers = jnp.where(picked, jnp.exp(jnp.where(picked, logits - peak, 0.0)), 0.0)
+    routes[ctx, 8:16, :] = powers / jnp.sum(powers, 0, keepdims=True)
+    route_sends = direct_send(routes.at[ctx], direct_sems.at[1], direct_recvs.at[1], length)
+    for copy in route_sends:
+        copy.start()
+
+    def selection(source, expert):
+        row = routes[source, pl.ds(EXP_DEV * ctx + expert, 1), :]
+        return rows_of((CAP, tokens)).astype(f32) == row
+
+    def slots(source):
+        return pl.ds(pl.multiple_of(source * CAP, CAP), CAP)
+
+    def first_half(source):
+        def one(expert, carried):
+            chosen = selection(source, expert).astype(f32).astype(bf16)
+            rows = product(chosen, entering[source]).astype(bf16)
+            slot_rows[expert, slots(source), :] = rows
+
+            def part(index, kept):
+                columns = pl.ds(pl.multiple_of(index * 512, 512), 512)
+                before = product(rows, inner[expert, :, columns])
+                value, gradient = gelu_parts(before)
+                active[expert, slots(source), columns] = value.astype(bf16)
+                slope[expert, slots(source), columns] = gradient.astype(bf16)
+                return kept
+
+            return lax.fori_loop(0, 4, part, carried)
+
+        lax.fori_loop(0, EXP_DEV, one, 0)
+
+    inner_gather.relay()
+    outer_gather.start()
+    direct_wait(lambda b: routes.at[b], direct_sems.at[1], direct_recvs.at[1], length)
+    entering_gather.relay(1)
+    inner_gather.relay_rest()
+    inner_gather.finish()
+
+    def step_of(step, carried):
+        for ahead in range(2, length):
+
+            @pl.when(step == ahead - 1)
+            def _():
+                entering_gather.relay(ahead)
+                if ahead < length - 1:
+                    pass
+
+        @pl.when(step == length - 2)
+        def _():
+            cot_gather.relay(2)
+
+        @pl.when(step == length - 1)
+        def _():
+            outer_gather.relay()
+
+        before_me = ctx - step >= 0
+        after_me = jnp.logical_and(ctx + step < length, step > 0)
+        count = before_me.astype(jnp.int32) + after_me.astype(jnp.int32)
+
+        def visit(turn, kept):
+            source = jnp.where(jnp.logical_and(turn == 0, before_me), ctx - step, ctx + step)
+            first_half(source)
+            return kept
+
+        lax.fori_loop(0, count, visit, 0)
+        return carried
+
+    lax.fori_loop(0, length, step_of, 0)
+    outer_gather.relay_rest()
+    cot_gather.relay(length - 1)
+    outer_gather.finish()
+
+    def second_half(turn, carried):
+        expert, part = turn // 2, turn % 2
+        rows = pl.ds(pl.multiple_of(part * 384, 384), 384)
+        result[expert, rows, :] = product(active[expert, rows, :], outer[expert]).astype(bf16)
+        return carried
+
+    lax.fori_loop(0, 2 * EXP_DEV, second_half, 0)
+
+    def score(source, carried):
+        lines = []
+        for expert in range(EXP_DEV):
+            chosen = selection(source, expert).astype(f32)
+            cot_rows = product(chosen.astype(bf16), cots[source]).astype(bf16)
+            slot_cot[expert, slots(source), :] = cot_rows
+            rows = result[expert, slots(source), :].astype(f32)
+            toward = jnp.sum(rows * small[36:37, :], -1, keepdims=True)
+            against = jnp.sum(rows * cot_rows.astype(f32), -1, keepdims=True)
+            lines.append(jnp.sum(chosen * toward, 0, keepdims=True))
+            lines.append(jnp.sum(chosen * against, 0, keepdims=True))
+        lines.append(jnp.zeros((8 - 2 * EXP_DEV, tokens), f32))
+        sheet = jnp.concatenate(lines, 0)
+
+        @pl.when(source == ctx)
+        def _():
+            scores_back[ctx] = sheet
+
+        @pl.when(source != ctx)
+        def _():
+            score_sent[source] = sheet
+            offset = (source - ctx + length) % length
+            remote(
+                score_sent.at[source],
+                scores_back.at[ctx],
+                direct_sems.at[2, offset - 1],
+                direct_recvs.at[2, offset - 1],
+                (source, me[1], me[2]),
+            ).start()
+
+        return carried
+
+    lax.fori_loop(0, length, score, 0)
+    direct_wait(lambda b: scores_back.at[b], direct_sems.at[2], direct_recvs.at[2], length)
+    for step in range(1, length):
+        target = moved(me, step, length)
+        remote(
+            score_sent.at[target[0]],
+            scores_back.at[ctx],
+            direct_sems.at[2, step - 1],
+            direct_recvs.at[2, step - 1],
+            target,
+        ).wait_send()
+    for copy in keyval_sends + route_sends:
+        copy.wait_send()
+    for item in (pack_gather, query_gather, project_gather, inner_gather, outer_gather):
+        item.drain()
+    cot_gather.drain()
+    entering_gather.drain()
+
+
+def fast_forward(length, states, cotangent, head_ids, route_ids, pack, query, project, inner, outer):
+    f32, bf16 = jnp.float32, jnp.bfloat16
+    tokens = states.shape[0]
+    rows = length * CAP
+    shape = jax.ShapeDtypeStruct
+    in_vmem = pl.BlockSpec(memory_space=pltpu.VMEM)
+    in_place = pl.BlockSpec(memory_space=pl.ANY)
+    outs = (
+        shape((EXP_DEV, rows, D), bf16),
+        shape((EXP_DEV, rows, FF), bf16),
+        shape((EXP_DEV, rows, FF), bf16),
+        shape((EXP_DEV, rows, D), bf16),
+        shape((EXP_DEV, rows, D), bf16),
+        shape((EXP_DEV, D, FF), bf16),
+        shape((EXP_DEV, FF, D), bf16),
+        shape((D, MOA_EXPERTS * HS), bf16),
+        shape((MOA_EXPERTS * HS, D), bf16),
+        shape((D, 256), bf16),
+        shape((tokens, D), bf16),
+        shape((tokens, MOA_EXPERTS * HS), bf16),
+        shape((MOA_TOP * tokens, 128), bf16),
+        shape((MOA_TOP * tokens, 128), f32),
+        shape((length * tokens, 128), bf16),
+        shape((tokens, 128), f32),
+        shape((tokens, D), f32),
+        shape((length, tokens, D), bf16),
+        shape((length, tokens, D), bf16),
+        shape((length, 16, tokens), f32),
+        shape((length, 8, tokens), f32),
+        shape((128, D), f32),
+    )
+    dma = pltpu.SemaphoreType.DMA
+    return pl.pallas_call(
+        partial(forward_kernel, length),
+        out_shape=outs,
+        in_specs=[in_vmem] * 5 + [in_place] * 4,
+        out_specs=[in_vmem] * len(outs),
+        scratch_shapes=[
+            pltpu.VMEM((tokens, D), f32),
+            pltpu.VMEM((length, 8, tokens), f32),
+            dma((5, 9)),
+            dma((5, 9)),
+            dma((5,)),
+            dma((2, 2, length)),
+            dma((2, 2, length)),
+            dma((3, length)),
+            dma((3, length)),
+        ],
+        compiler_params=pltpu.CompilerParams(
+            collective_id=0, has_side_effects=True, vmem_limit_bytes=60 * 2**20
+        ),
+        name="forward",
+    )(states, cotangent, head_ids, route_ids, pack, query, project, inner, outer)
+
+
+def fast_body(
+    states,
+    remaining,
+    moa_ids,
+    ffn_ids,
+    out_cotangent,
+    left_cotangent,
+    query_weight,
+    keyval_weight,
+    project_weight,
+    chooser,
+    selector,
+    gain_one,
+    bias_one,
+    gain_two,
+    bias_two,
+    halt_weight,
+    expert_in,
+    expert_out,
+):
+    tokens = states.shape[1]
+    devices = lax.axis_size("ctx")
+    experts = EXP_DEV * devices
+    capacity = max(2, (4 * tokens + experts - 1) // experts)
+    rows_total = tokens * MOA_TOP
+    scaling = HS ** (-0.5)
+    f32 = jnp.float32
+    bf16 = jnp.bfloat16
+    flat = jnp.stack([gain_one, bias_one, gain_two, bias_two, halt_weight], 1)
+    pack = jnp.concatenate(
+        [keyval_weight, chooser, selector, flat, jnp.zeros((flat.shape[0], 91), bf16)], 1
+    )
+    (
+        arrived_flat,
+        activated_flat,
+        slope_flat,
+        result_flat,
+        unused_cot,
+        inner_full,
+        outer_full,
+        query_full,
+        project_full,
+        packed,
+        acted,
+        mixture,
+        queries_flat,
+        heads_flat,
+        shard_rows,
+        gate_lanes,
+        middle,
+        entering_all,
+        unused_cots,
+        routes,
+        unused_scores,
+        small,
+    ) = fast_forward(
+        devices, states[0], out_cotangent[0], moa_ids[0], ffn_ids[0],
+        pack, query_weight, project_weight, expert_in, expert_out,
+    )
+    spot = lax.axis_index("ctx")
+    keyval_full = packed[:, :128]
+    chooser_full = packed[:, 128:152]
+    selector_full = packed[:, 152:160]
+    gainone_full, biasone_full, gaintwo_full, biastwo_full, halt_full = (small[32 + i] for i in range(5))
+    gain_first = gainone_full.astype(f32)
+    gain_second = gaintwo_full.astype(f32)
+    halt_vector = halt_full.astype(f32)
+    resident = states[0].astype(f32)
+    normed_one, normal_one, inverse_one = layer_norm(resident, gain_first, biasone_full.astype(f32))
+    head_ids = moa_ids[0]
+    query_sel = (
+        (queries_flat[:, :HS] * 8.0).reshape(MOA_TOP, tokens, HS).swapaxes(0, 1).reshape(rows_total, HS)
+    )
+    keyval = lax.dynamic_slice_in_dim(shard_rows, spot * tokens, tokens, 0)
+    chosen = one_hot(head_ids, MOA_EXPERTS)
+    head_gates = gate_lanes[:, :MOA_TOP]
+    heads_view = heads_flat[:, HS:].reshape(MOA_TOP, tokens, HS).swapaxes(0, 1)
+    heads_out = heads_view.reshape(rows_total, HS)
+    log_total = heads_flat[:, 0].reshape(MOA_TOP, tokens).T.reshape(rows_total)
+    chosen_low = chosen.astype(bf16)
+    normed_two, normal_two, inverse_two = layer_norm(middle, gain_second, biastwo_full.astype(f32))
+    entering = lax.dynamic_index_in_dim(entering_all, spot, 0, False)
+    own = lax.dynamic_index_in_dim(routes, spot, 0, False)
+    route_ids = ffn_ids[0]
+    picked = one_hot(route_ids, experts)
+    expert_gates = jnp.sum(picked * own[8:16].T[:, None, :], -1)
+    slots = jnp.sum(picked * own[0:8].T[:, None, :], -1).astype(jnp.int32)
+    target = (route_ids * capacity + slots).reshape(-1)
+
+    def by_source(flat):
+        return flat.reshape(EXP_DEV, devices, capacity, flat.shape[-1]).swapaxes(0, 1)
+
+    arrived_rows = by_source(arrived_flat)
+    activated = by_source(activated_flat)
+    slope = by_source(slope_flat)
+    result_rows = by_source(result_flat)
+    returned = lax.all_to_all(result_rows, "ctx", split_axis=0, concat_axis=0, tiled=True).reshape(
+        experts * capacity, D
+    )
+    expert_rows = returned[target].reshape(tokens, FFN_TOP, D).astype(f32)
+    final = middle + jnp.sum(expert_gates[:, :, None] * expert_rows, 1)
+    halting = jax.nn.sigmoid(jnp.dot(final, halt_vector, precision=HIGH))
+    left_mass = remaining[0]
+    stopped = left_mass * halting
+    new_states = (stopped[:, None] * resident + (1.0 - stopped)[:, None] * final).astype(bf16)
+    remaining_next = left_mass * (1.0 - halting)
+    out_grad = out_cotangent[0]
+    left_grad = left_cotangent[0]
+    stop_grad = jnp.sum(out_grad * (resident - final), -1)
+    grad_remaining = stop_grad * halting + left_grad * (1.0 - halting)
+    halt_logit_grad = (stop_grad - left_grad) * left_mass * halting * (1.0 - halting)
+    grad_halt = jnp.sum(halt_logit_grad[:, None] * final, 0)
+    grad_final = (1.0 - stopped)[:, None] * out_grad + halt_logit_grad[:, None] * halt_vector
+    gate_grad = jnp.sum(grad_final[:, None, :] * expert_rows, -1)
+    selector_logit_grad = jnp.sum(choose_back(expert_gates, gate_grad)[:, :, None] * picked, 1)
+    entering_wide = entering.astype(f32)
+    grad_selector = jnp.dot(entering_wide.T, selector_logit_grad, precision=HIGH)
+    rows_grad = (expert_gates[:, :, None] * grad_final[:, None, :]).astype(bf16).reshape(-1, D)
+    grad_outgoing = (
+        jnp.zeros((experts * capacity, D), bf16)
+        .at[target]
+        .set(rows_grad)
+        .reshape(devices, EXP_DEV, capacity, D)
+    )
+    grad_arrived = lax.all_to_all(grad_outgoing, "ctx", split_axis=0, concat_axis=0, tiled=True)
+    grad_activated = jnp.einsum(
+        "nekd,efd->nekf", grad_arrived, outer_full, preferred_element_type=f32
+    )
+    before_grad = (grad_activated * slope.astype(f32)).astype(bf16)
+    outer_grad = jnp.einsum(
+        "nekf,nekd->efd", activated, grad_arrived, preferred_element_type=f32
+    )
+    inner_grad = jnp.einsum("nekd,nekf->edf", arrived_rows, before_grad, preferred_element_type=f32)
+    grad_sent = jnp.einsum(
+        "nekf,edf->nekd", before_grad, inner_full, preferred_element_type=f32
+    ).astype(bf16)
+    grad_back = lax.all_to_all(grad_sent, "ctx", split_axis=0, concat_axis=0, tiled=True).reshape(
+        experts * capacity, D
+    )
+    entering_grad = jnp.sum(grad_back[target].reshape(tokens, FFN_TOP, D).astype(f32), 1)
+    entering_grad = entering_grad + jnp.dot(
+        selector_logit_grad, selector_full.astype(f32).T, precision=HIGH
+    )
+    middle_extra, grad_gain_two, grad_bias_two = norm_back(
+        entering_grad, normal_two, inverse_two, gain_second
+    )
+    middle_grad = grad_final + middle_extra
+    attn_grad = middle_grad.astype(bf16)
+    grad_project = jnp.dot(mixture.T, attn_grad, preferred_element_type=f32)
+    mix_grad = jnp.dot(attn_grad, project_full.T, preferred_element_type=f32).reshape(
+        tokens, MOA_EXPERTS, HS
+    )
+    mix_sel_grad = jnp.take_along_axis(mix_grad, head_ids[:, :, None], axis=1)
+    head_gate_grad = jnp.sum(mix_sel_grad * heads_view, -1)
+    chooser_logit_grad = jnp.sum(choose_back(head_gates, head_gate_grad)[:, :, None] * chosen, 1)
+    acted_wide = acted.astype(f32)
+    grad_chooser = jnp.dot(acted_wide.T, chooser_logit_grad, precision=HIGH)
+    acted_grad = jnp.dot(chooser_logit_grad, chooser_full.astype(f32).T, precision=HIGH)
+    heads_grad = (head_gates[:, :, None] * mix_sel_grad).astype(bf16).reshape(rows_total, HS)
+    row_delta = jnp.sum(heads_grad.astype(f32) * heads_out, -1)
+
+    def cycle_turn(turn_index, carried):
+        visiting, grads_visiting, query_grad = carried
+        block_size = block_rows(tokens)
+
+        def per_block(query_acc, key_block):
+            scores = jnp.dot(query_sel, key_block[:, :HS].T, preferred_element_type=f32) * scaling
+            probability = jnp.exp(scores - log_total[:, None])
+            prob_grad = jnp.dot(heads_grad, key_block[:, HS:].T, preferred_element_type=f32)
+            score_grad = (probability * (prob_grad - row_delta[:, None])).astype(bf16)
+            query_acc = (
+                query_acc
+                + jnp.dot(score_grad, key_block[:, :HS], preferred_element_type=f32) * scaling
+            )
+            keys_grad = jnp.dot(score_grad.T, query_sel, preferred_element_type=f32) * scaling
+            values_grad = jnp.dot(
+                probability.astype(bf16).T, heads_grad, preferred_element_type=f32
+            )
+            return (query_acc, jnp.concatenate([keys_grad, values_grad], -1))
+
+        query_grad, block_grads = lax.scan(
+            per_block, query_grad, visiting.reshape(tokens // block_size, block_size, 2 * HS)
+        )
+        grads_visiting = grads_visiting + block_grads.reshape(tokens, 2 * HS)
+        visiting = shifted(visiting, "ctx", 1)
+        grads_visiting = shifted(grads_visiting.astype(jnp.bfloat16), "ctx", 1).astype(
+            grads_visiting.dtype
+        )
+        return (visiting, grads_visiting, query_grad)
+
+    cycle_state = (keyval, jnp.zeros((tokens, 2 * HS), f32), jnp.zeros((rows_total, HS), f32))
+    unused_keys, keyval_grad, query_grad = lax.fori_loop(0, devices, cycle_turn, cycle_state)
+    query_sel_grad = query_grad.astype(bf16).reshape(tokens, MOA_TOP, HS)
+    query_all_grad = jnp.sum(chosen_low[:, :, :, None] * query_sel_grad[:, :, None, :], 1).reshape(
+        tokens, MOA_EXPERTS * HS
+    )
+    keyval_low = keyval_grad.astype(bf16)
+    grad_query = jnp.dot(acted.T, query_all_grad, preferred_element_type=f32)
+    grad_keyval = jnp.dot(acted.T, keyval_low, preferred_element_type=f32)
+    acted_grad = acted_grad + jnp.dot(query_all_grad, query_full.T, preferred_element_type=f32)
+    acted_grad = acted_grad + jnp.dot(keyval_low, keyval_full.T, preferred_element_type=f32)
+    resident_grad, grad_gain_one, grad_bias_one = norm_back(
+        acted_grad, normal_one, inverse_one, gain_first
+    )
+    grad_states = middle_grad + resident_grad + stopped[:, None] * out_grad
+    dense_grads = (
+        grad_query,
+        grad_keyval,
+        grad_project,
+        grad_chooser,
+        grad_selector,
+        grad_gain_one,
+        grad_bias_one,
+        grad_gain_two,
+        grad_bias_two,
+        grad_halt,
+    )
+    totals = (
+        lax.psum(dense_grads[0].astype(jnp.bfloat16), "ctx").astype(jnp.float32),
+        lax.psum(dense_grads[1].astype(jnp.bfloat16), "ctx").astype(jnp.float32),
+        lax.psum(dense_grads[2].astype(jnp.bfloat16), "ctx").astype(jnp.float32),
+        lax.psum(dense_grads[3].astype(jnp.bfloat16), "ctx").astype(jnp.float32),
+        lax.psum(dense_grads[4].astype(jnp.bfloat16), "ctx").astype(jnp.float32),
+        lax.psum(dense_grads[5].astype(jnp.bfloat16), "ctx").astype(jnp.float32),
+        lax.psum(dense_grads[6].astype(jnp.bfloat16), "ctx").astype(jnp.float32),
+        lax.psum(dense_grads[7].astype(jnp.bfloat16), "ctx").astype(jnp.float32),
+        lax.psum(dense_grads[8].astype(jnp.bfloat16), "ctx").astype(jnp.float32),
+        lax.psum(dense_grads[9].astype(jnp.bfloat16), "ctx").astype(jnp.float32),
+    )
+    shards = (
+        lax.psum_scatter(
+            totals[0].astype(jnp.bfloat16), ("seq", "wsh"), scatter_dimension=0, tiled=True
+        ).astype(jnp.float32),
+        lax.psum_scatter(
+            totals[1].astype(jnp.bfloat16), ("seq", "wsh"), scatter_dimension=0, tiled=True
+        ).astype(jnp.float32),
+        lax.psum_scatter(
+            totals[2].astype(jnp.bfloat16), ("seq", "wsh"), scatter_dimension=0, tiled=True
+        ).astype(jnp.float32),
+        lax.psum_scatter(
+            totals[3].astype(jnp.bfloat16), ("seq", "wsh"), scatter_dimension=0, tiled=True
+        ).astype(jnp.float32),
+        lax.psum_scatter(
+            totals[4].astype(jnp.bfloat16), ("seq", "wsh"), scatter_dimension=0, tiled=True
+        ).astype(jnp.float32),
+        lax.psum_scatter(
+            totals[5].astype(jnp.bfloat16), ("seq", "wsh"), scatter_dimension=0, tiled=True
+        ).astype(jnp.float32),
+        lax.psum_scatter(
+            totals[6].astype(jnp.bfloat16), ("seq", "wsh"), scatter_dimension=0, tiled=True
+        ).astype(jnp.float32),
+        lax.psum_scatter(
+            totals[7].astype(jnp.bfloat16), ("seq", "wsh"), scatter_dimension=0, tiled=True
+        ).astype(jnp.float32),
+        lax.psum_scatter(
+            totals[8].astype(jnp.bfloat16), ("seq", "wsh"), scatter_dimension=0, tiled=True
+        ).astype(jnp.float32),
+        lax.psum_scatter(
+            totals[9].astype(jnp.bfloat16), ("seq", "wsh"), scatter_dimension=0, tiled=True
+        ).astype(jnp.float32),
+    )
+    inner_shard, outer_shard = (
+        lax.psum_scatter(
+            inner_grad.astype(jnp.bfloat16), ("seq", "wsh"), scatter_dimension=1, tiled=True
+        ).astype(jnp.float32),
+        lax.psum_scatter(
+            outer_grad.astype(jnp.bfloat16), ("seq", "wsh"), scatter_dimension=1, tiled=True
+        ).astype(jnp.float32),
+    )
+    return (
+        new_states[None],
+        remaining_next[None],
+        grad_states[None],
+        grad_remaining[None],
+        shards[0],
+        shards[1],
+        shards[2],
+        shards[3],
+        shards[4],
+        shards[5],
+        shards[6],
+        shards[7],
+        shards[8],
+        shards[9],
+        inner_shard,
+        outer_shard,
+    )
+
+
 def solution(mesh):
     in_specs = (
         P(("seq", "wsh"), "ctx", None),
@@ -423,4 +1288,5 @@
         P("ctx", ("seq", "wsh"), None),
         P("ctx", ("seq", "wsh"), None),
     )
+    body = fast_body if mesh.shape["ctx"] == 4 else general_body
     return jax.shard_map(body, mesh=mesh, in_specs=in_specs, out_specs=out_specs, check_vma=False)

time: 797 us -> 690 us (0.87)
  Pallas kernels: 0 us -> 101 us
  blocking collectives: 153 us -> 72.2 us
  matrix products: 117 us -> 58.4 us
  local copies, waits for them, and re-layouts: 107 us -> 70.8 us
  waiting for transfers between devices: 316 us -> 295 us
  other arithmetic: 61.8 us -> 52.6 us
    pallas_call x0 -> x1, Pallas kernels: none -> 101 us  [fast_forward(): pl.pallas_call(partial(forward_kernel, length), out_shape=outs, in_specs=...]
    all_gather x4 -> x0, blocking collectives: 64 us -> none  [the longest x1 17.7 us: body(): lax.all_gather(selector, ('seq', 'wsh'), axis=0, tiled=True)]
    dot_general x28 -> x15, matrix products: 108 us -> 48.8 us  [the longest x1 9.42 us: fast_body(): jnp.einsum('nekd,efd->nekf', grad_arrived, outer_full, preferred_element_...]
    gather x6 -> x5, local copies, waits for them, and re-layouts: 45.9 us -> 22 us  [the longest x3 16 us: fast_body(): mix_sel_grad = jnp.take_along_axis(mix_grad, head_ids[:, :, None], axis=1)]
    unnamed x2 -> x1, blocking collectives: 29.9 us -> 13.8 us
    all_to_all x3 -> x2, waiting for transfers between devices: 68.6 us -> 53.7 us  [the longest x1 31.9 us: fast_body(): lax.all_to_all(result_rows, 'ctx', split_axis=0, concat_axis=0, tiled=True)]
    reduce_sum x18 -> x9, other arithmetic: 20.6 us -> 15.1 us  [the longest x1 3.75 us: fast_body(): final = middle + jnp.sum(expert_gates[:, :, None] * expert_rows, 1)]
    unnamed x179 -> x159, local copies, waits for them, and re-layouts: 18.6 us -> 14.1 us
  transfers between devices with their start and end apart: 23 -> 18, of which waited for: 14 -> 13; matrix products, arithmetic and copies ran while one was open for 26% -> 16% of each run, Pallas kernels for 0% -> 0%
where the time goes in v1:
time: 690 us; the launch traced here: 682 us
  waiting for transfers between devices  295 us (43%)
  Pallas kernels  101 us (15%)
  blocking collectives  72.2 us (10%)
  local copies, waits for them, and re-layouts  70.8 us (10%)
  matrix products  58.4 us (8%)
  other arithmetic  52.6 us (8%)
  between operations  16.3 us (2%)
  starting transfers between devices  15.3 us (2%)
    pallas_call x1, Pallas kernels, fast_forward(): pl.pallas_call(partial(forward_kernel, length), out_shape=outs, in_specs=...  101 us
    reduce_scatter x1, waiting for transfers between devices, fast_body(): lax.psum_scatter(inner_grad.astype(jnp.bfloat16), ('seq', 'wsh'), scatter...  52.9 us
    reduce_scatter x1, waiting for transfers between devices, fast_body(): lax.psum_scatter(outer_grad.astype(jnp.bfloat16), ('seq', 'wsh'), scatter...  50.7 us
    all_to_all x1, blocking collectives, fast_body(): lax.all_to_all(grad_outgoing, 'ctx', split_axis=0, concat_axis=0, tiled=T...  39.1 us
    reduce_scatter x1, waiting for transfers between devices, fast_body(): lax.psum_scatter(totals[1].astype(jnp.bfloat16), ('seq', 'wsh'), scatter_...  36 us
    unnamed x10, waiting for transfers between devices  34.1 us
    reduce_scatter x1, waiting for transfers between devices, fast_body(): lax.psum_scatter(totals[0].astype(jnp.bfloat16), ('seq', 'wsh'), scatter_...  31.9 us
    all_to_all x1, waiting for transfers between devices, fast_body(): lax.all_to_all(result_rows, 'ctx', split_axis=0, concat_axis=0, tiled=True)  31.9 us
  transfers between devices with their start and end apart: 18, of which 13 were waited for; matrix products, arithmetic and copies ran while one was open for 16% of the time, Pallas kernels for 0%

profile of v1, /device:TPU:0, one launch (start us, length us, event | category | flops | bytes accessed | tf_op | source)
XLA Modules:
  0.0 682.0 jit_solution(4278608393804204360)
XLA Ops:
  12.6 1.5 copy.178
  14.1 1.5 copy.179
  15.6 1.4 concatenate.7.pack
  17.0 101.1 %forward.1 = (bf16[2,768,512]{2,1,0:T(8,128)(2,1)}, bf16[2,768,2048]{2,1,0:T(8,128)(2,1)}, bf16[2,768,2048]{2,1,0:T(8,128)(2,1)}, bf16[2,768,512]{2,1,0:T(8,128)...) custom-call(bf16[384,512]{1,0:T(8,128)(2,1)} %bitcast.158, ...), custom_call_target="tpu_custom_call" | custom-call | tf_op jit(solution)/shard_map/forward/pallas_call | solution.py:940
  118.1 2.7 copy.235
  120.9 5.6 all-to-all-start
  130.6 1.4 fusion.67
  132.0 31.9 %all-to-all-done = bf16[4,2,192,512]{3,2,1,0:T(8,128)(2,1)S(1)} async-done(((bf16[4,2,192,512]{3,2,1,0:T(8,128)(2,1)}), bf16[4,2,192,512]{3,2,1,0:T(8,128)(2,1)S(1)}, u32[]{:S(2)}, u32[]{:S(2)}) %all-to-all-start) | async-done | bytes 1572896 | tf_op jit(solution)/shard_map/all_to_all | solution.py:1059
  163.9 2.7 gather_fusion
  167.6 3.7 multiply_reduce_fusion.2
  171.4 1.2 fusion.37
  172.5 1.5 convolution_reduce_fusion
  176.8 2.2 mul.356
  179.0 9.2 %scatter_custom_fusion = bf16[1536,512]{1,0:T(8,128)(2,1)S(1)} fusion(s32[768]{0:T(1024)} %copy-done.53, f32[768,512]{1,0:T(8,128)} %mul.356, f32[768]{0:T(1024)S(1)} %copy-done.52, bf16[]{:T(256)} %constant.42.clone.1), kind=kCustom, calls=%fused_computation.67 | custom fusion | flops 786432 | bytes 3149312 | tf_op jit(solution)/shard_map/scatter | solution.py:1084
  188.3 39.1 %all_to_all.15 = bf16[4,2,192,512]{3,2,1,0:T(8,128)(2,1)S(1)} all-to-all(bf16[4,2,192,512]{3,2,1,0:T(8,128)(2,1)S(1)} %bitcast.157), channel_id=1, replica_groups=mesh['ctx'=4,'seq'=4,'wsh'=2] {'ctx'}, dimensions={0} | all-to-all | bytes 3145728 | tf_op jit(solution)/shard_map/all_to_all | solution.py:1087
  227.4 9.4 %fusion.12 = bf16[4,2,192,2048]{3,2,0,1:T(8,128)(2,1)} fusion(bf16[2,4,192,2048]{3,2,1,0:T(8,128)(2,1)} %bitcast.184, bf16[2,2048,512]{2,1,0:T(8,128)(2,1)} %get-tuple-element.107, bf16[4,2,192,512]{3,2,1,0:T(8,128)(2,1)S(1)} %all_to_all.15), kind=kOutput, calls=%fused_computation.22 | convolution fusion | flops 3230662656 | bytes 18350080 | tf_op jit(solution)/shard_map/nekd,efd->nekf/dot_general | solution.py:1088
  236.9 6.4 fusion.19
  243.3 1.4 copy.194
  244.6 3.7 all-to-all-start.2
  252.4 2.4 slice.59
  257.1 1.3 compare_and_fusion.1
  258.4 1.3 convert_convert_fusion
  259.7 2.5 multiply_reduce_fusion.1
  262.4 21.9 %all-to-all-done.2 = bf16[4,2,192,512]{3,2,1,0:T(8,128)(2,1)S(1)} async-done(((bf16[4,2,192,512]{3,2,1,0:T(8,128)(2,1)}), bf16[4,2,192,512]{3,2,1,0:T(8,128)(2,1)S(1)}, u32[]{:S(2)}, u32[]{:S(2)}) %all-to-all-start.2) | async-done | bytes 1572896 | tf_op jit(solution)/shard_map/all_to_all | solution.py:1099
  284.3 3.3 gather_fusion.1
  287.6 3.0 reshape.329
  290.6 3.4 reduce_sum.245
  294.0 1.5 multiply_reduce_fusion.4
  296.8 2.2 convolution_convert_fusion
  299.3 3.8 fusion.49
  303.1 5.0 copy.201
  308.2 15.7 %gather_fusion.2 = f32[1536,64]{1,0:T(8,128)S(1)} fusion(f32[384,24,64]{2,1,0:T(8,128)} %copy.201, s32[1536]{0:T(1024)S(1)} %reshape.347), kind=kCustom, calls=%fused_computation.2 | custom fusion | bytes 798720 | tf_op jit(solution)/shard_map/jit(take_along_axis)/gather | solution.py:1115
  323.9 2.6 multiply_reduce_fusion.6
  326.8 1.1 multiply_convert_fusion.3
  328.0 42.7 %while.15 = (s32[]{:T(128)}, bf16[384,128]{1,0:T(8,128)(2,1)S(1)}, f32[384,128]{0,1:T(8,128)}, f32[1536,64]{0,1:T(8,128)S(1)}, bf16[1536,64]{1,0:T(8,128)(2,1)S(...) while((s32[]{:T(128)}, bf16[384,128]{1,0:T(8,128)(2,1)S(1)}, ...), condition=%wide.wide.region_20.21_spmd.clone, body=%wide.wide.region_19.20_spmd.clone.sunk | while | flops 381591552 | bytes 14463176 | solution.py:1154
  331.6 5.6 collective-permute-done.1
  339.9 1.6 fusion.134
  342.9 5.3 collective-permute-done.1
  350.8 1.6 fusion.134
  352.4 1.4 collective-permute-start.1
  354.3 4.8 collective-permute-done.1
  361.7 1.6 fusion.134
  363.3 2.3 collective-permute-start.1
  366.2 3.8 collective-permute-done.1
  371.5 1.2 multiply_reduce_fusion
  372.8 2.2 convolution_convert_fusion.1
  375.7 1.3 convolution_convert_fusion.4
  380.6 31.9 %reduce-scatter.16.cloned.1.call-done = bf16[64,1536]{1,0:T(8,128)(2,1)} async-done(((bf16[512,1536]{1,0:T(8,128)(2,1)}), bf16[64,1536]{1,0:T(8,128)(2,1)}) %reduce-scatter.16.cloned.1.call-update) | async-done | bytes 196624 | tf_op jit(solution)/shard_map/reduce_scatter | solution.py:1193
  412.9 8.6 %bitcast_convert_fusion = bf16[2,2048,512]{2,1,0:T(8,128)(2,1)} fusion(bf16[4,2,192,2048]{3,2,0,1:T(8,128)(2,1)} %bitcast.183, bf16[4,2,192,512]{3,2,1,0:T(8,128)(2,1)} %copy-done.19), kind=kOutput, calls=%fused_computation.23 | convolution fusion | flops 3223322624 | bytes 12058624 | tf_op jit(solution)/shard_map/nekf,nekd->efd/dot_general | solution.py:1092
  421.6 8.7 %bitcast_convert_fusion.1 = bf16[2,512,2048]{2,1,0:T(8,128)(2,1)} fusion(bf16[4,2,192,512]{3,2,0,1:T(8,128)(2,1)} %bitcast.185, bf16[4,2,192,2048]{3,2,0,1:T(8,128)(2,1)} %fusion.12), kind=kOutput, calls=%fused_computation.24 | convolution fusion | flops 3223322624 | bytes 12058624 | tf_op jit(solution)/shard_map/nekd,nekf->edf/dot_general | solution.py:1095
  433.4 16.1 %reduce-scatter.24.cloned.1.call-done = bf16[64,8]{1,0:T(8,128)(2,1)} async-done(((bf16[512,8]{1,0:T(8,128)(2,1)}), bf16[64,8]{1,0:T(8,128)(2,1)}) %reduce-scatter.24.cloned.1.call-update) | async-done | bytes 1040
  451.7 1.2 fusion.36
  453.1 1.6 multiply_reduce_fusion.3
  454.6 13.8 %all-reduce.5 = (bf16[512]{0:T(512)(128)(2,1)S(1)}, bf16[512]{0:T(512)(128)(2,1)S(1)}, bf16[512]{0:T(512)(128)(2,1)S(1)}, bf16[512]{0:T(512)(128)(2,1)S(1)}, bf16[512]{0:T(512)(128)(2,1)S(1)}) all-reduce(bf16[512]{0:T(512)(128)(2,1)S(1)} %get-tuple-element.194, ...), channel_id=7, replica_groups=mesh['ctx'=4,'seq'=4,'wsh'=2] {'seq','wsh'}, use_global_device_ids=true, to_apply=%region_36.37.clone | all-reduce | flops 2560 | bytes 10240
  468.8 17.8 %reduce-scatter.22.cloned.1.call-done = bf16[64,24]{1,0:T(8,128)(2,1)} async-done(((bf16[512,24]{1,0:T(8,128)(2,1)}), bf16[64,24]{1,0:T(8,128)(2,1)}) %reduce-scatter.22.cloned.1.call-update) | async-done | bytes 3088
  487.4 36.0 %reduce-scatter.18.cloned.1.call-done = bf16[64,128]{1,0:T(8,128)(2,1)} async-done(((bf16[512,128]{1,0:T(8,128)(2,1)}), bf16[64,128]{1,0:T(8,128)(2,1)}) %reduce-scatter.18.cloned.1.call-update) | async-done | bytes 16400 | tf_op jit(solution)/shard_map/reduce_scatter | solution.py:1196
  523.4 19.3 %all-reduce.6 = (bf16[64,128]{1,0:T(8,128)(2,1)S(1)}, bf16[64,24]{0,1:T(8,128)(2,1)S(1)}, bf16[64,8]{0,1:T(8,128)(2,1)S(1)}, bf16[64]{0:T(256)(128)(2,1)S(1)}, b...) all-reduce(bf16[64,128]{1,0:T(8,128)(2,1)} %reduce-scatter.18.clone, ...), channel_id=1, replica_groups=mesh['ctx'=4,'seq'=4,'wsh'=2] {'ctx'}, use_global_device_ids=true, to_apply=%region_26.27 | all-reduce | flops 10560 | bytes 42240 | tf_op jit(solution)/shard_map/psum | solution.py:1182
  547.1 16.3 %all-reduce.10.cloned.1.call-done = (bf16[64,1536]{1,0:T(8,128)(2,1)}, bf16[192,512]{1,0:T(8,128)(2,1)}) async-done(((bf16[64,1536]{1,0:T(8,128)(2,1)}, bf16[192,512]{1,0:T(8,128)(2,1)}), (bf16[64,1536]{1,0:T(8,128)(2,1)}, bf16[192,512]{1,0:T(8,128)(2,1)})) %all-reduce.10.cloned.1.call-update) | async-done | bytes 393232 | tf_op jit(solution)/shard_map/psum | solution.py:1181
  563.4 1.7 convert_element_type.229
  565.1 1.7 convert_element_type.233
  566.8 50.7 %reduce-scatter.14.cloned.1.call-done = bf16[2,256,512]{2,1,0:T(8,128)(2,1)} async-done(((bf16[2,2048,512]{2,1,0:T(8,128)(2,1)}), bf16[2,256,512]{2,1,0:T(8,128)(2,1)}) %reduce-scatter.14.cloned.1.call-update) | async-done | bytes 524304 | tf_op jit(solution)/shard_map/reduce_scatter | solution.py:1228
  617.5 2.1 convert_element_type.251
  619.7 52.9 %reduce-scatter.12.cloned.1.call-done = bf16[2,64,2048]{2,1,0:T(8,128)(2,1)} async-done(((bf16[2,512,2048]{2,1,0:T(8,128)(2,1)}), bf16[2,64,2048]{2,1,0:T(8,128)(2,1)}) %reduce-scatter.12.cloned.1.call-update) | async-done | bytes 524304 | tf_op jit(solution)/shard_map/reduce_scatter | solution.py:1225
  672.6 2.1 convert_element_type.249
  (295 shorter events, 51.6 us)
Async XLA Ops:
  120.9 5.6 copy-start.17
  120.9 5.7 copy-start.67
  120.9 6.4 copy-start.68
  120.9 7.0 %copy-start.54 = (s32[1,384,2]{1,2,0:T(2,128)S(1)}, s32[1,384,2]{1,2,0:T(2,128)}, u32[]{:S(2)}) copy-start(s32[1,384,2]{1,2,0:T(2,128)} %param.23) | copy-start | bytes 9220
  120.9 9.2 %copy-start.4 = (f32[384,512]{1,0:T(8,128)S(1)}, f32[384,512]{1,0:T(8,128)}, u32[]{:S(2)}) copy-start(f32[384,512]{1,0:T(8,128)} %get-tuple-element.102) | copy-start | bytes 2359300
  120.9 42.9 %all-to-all-start = ((bf16[4,2,192,512]{3,2,1,0:T(8,128)(2,1)}), bf16[4,2,192,512]{3,2,1,0:T(8,128)(2,1)S(1)}, u32[]{:S(2)}, u32[]{:S(2)}) async-start(bf16[4,2,192,512]{3,2,1,0:T(8,128)(2,1)} %bitcast.156), calls=%async_computation | async-start | bytes 3145728 | tf_op jit(solution)/shard_map/all_to_all | solution.py:1059
  126.5 3.8 copy-start.10
  126.6 37.2 %copy-start.43 = (s32[384,2]{0,1:T(2,128)}, s32[384,2]{0,1:T(2,128)S(1)}, u32[]{:S(2)}) copy-start(s32[384,2]{0,1:T(2,128)S(1)} %copy.187) | copy-start | bytes 9220
  128.9 34.9 %copy-start.30 = (f32[384,2]{0,1:T(2,128)}, f32[384,2]{0,1:T(2,128)S(1)}, u32[]{:S(2)}) copy-start(f32[384,2]{0,1:T(2,128)S(1)} %get-tuple-element.202) | copy-start | bytes 9220
  129.4 34.4 %copy-start.18 = (f32[384,2]{1,0:T(8,128)}, f32[384,2]{1,0:T(8,128)S(1)}, u32[]{:S(2)}) copy-start(f32[384,2]{1,0:T(8,128)S(1)} %copy.188) | copy-start | bytes 9220
  130.3 33.5 %copy-start.53 = (s32[768]{0:T(1024)}, s32[768]{0:T(1024)S(1)}, u32[]{:S(2)}) copy-start(s32[768]{0:T(1024)S(1)} %fusion.61) | copy-start | bytes 9220
  130.4 36.2 %copy-start.32 = (s32[1024]{0:T(1024)}, s32[1024]{0:T(1024)S(1)}, u32[]{:S(2)}) copy-start(s32[1024]{0:T(1024)S(1)} %pad_clamp_fusion) | copy-start | bytes 12292
  130.5 40.8 %copy-start.47 = (f32[384]{0:T(512)}, f32[384]{0:T(512)S(1)}, u32[]{:S(2)}) copy-start(f32[384]{0:T(512)S(1)} %broadcast_multiply_fusion.3) | copy-start | bytes 4612
  130.5 40.8 %copy-start.34 = (f32[384]{0:T(512)}, f32[384]{0:T(512)S(1)}, u32[]{:S(2)}) copy-start(f32[384]{0:T(512)S(1)} %broadcast_multiply_fusion.6) | copy-start | bytes 4612
  132.0 42.7 %copy-start.50 = (f32[1,512]{1,0:T(1,128)}, f32[1,512]{1,0:T(1,128)S(1)}, u32[]{:S(2)}) copy-start(f32[1,512]{1,0:T(1,128)S(1)} %get-tuple-element.244) | copy-start | bytes 6148
  167.5 5.0 copy-start.1
  167.5 3.8 copy-start
  171.3 2.7 copy-start.62
  227.4 9.4 %copy-start.19 = (bf16[4,2,192,512]{3,2,1,0:T(8,128)(2,1)}, bf16[4,2,192,512]{3,2,1,0:T(8,128)(2,1)S(1)}, u32[]{:S(2)}) copy-start(bf16[4,2,192,512]{3,2,1,0:T(8,128)(2,1)S(1)} %all_to_all.15) | copy-start | bytes 4718596
  227.4 9.4 %copy-start.69 = (bf16[2,512,2048]{2,1,0:T(8,128)(2,1)S(1)}, bf16[2,512,2048]{2,1,0:T(8,128)(2,1)}, u32[]{:S(2)}) copy-start(bf16[2,512,2048]{2,1,0:T(8,128)(2,1)} %get-tuple-element.106) | copy-start | bytes 12582916
  244.6 3.8 copy-start.46
  244.6 3.8 copy-start.12
  244.6 5.2 copy-start.15
  244.6 39.7 %all-to-all-start.2 = ((bf16[4,2,192,512]{3,2,1,0:T(8,128)(2,1)}), bf16[4,2,192,512]{3,2,1,0:T(8,128)(2,1)S(1)}, u32[]{:S(2)}, u32[]{:S(2)}) async-start(bf16[4,2,192,512]{3,2,1,0:T(8,128)(2,1)} %copy.194), calls=%async_computation.2 | async-start | bytes 3145728 | tf_op jit(solution)/shard_map/all_to_all | solution.py:1099
  248.3 132.3 %reduce-scatter.20.cloned.1.call-start = ((), (), s32[]{:S(2)}) async-start(), calls=%async_computation.14 | async-start | bytes 1769472 | tf_op jit(solution)/shard_map/reduce_scatter | solution.py:1199
  251.6 3.7 copy-start.24
  256.1 6.2 copy-start.31
  256.2 6.2 copy-start.44
  256.2 6.2 copy-start.56
  256.2 28.1 %copy-start.33 = (s32[1024]{0:T(1024)S(1)}, s32[1024]{0:T(1024)}, u32[]{:S(2)}) copy-start(s32[1024]{0:T(1024)} %copy-done.32) | copy-start | bytes 12292
  262.4 31.6 %copy-start.26 = (f32[384,8]{0,1:T(8,128)}, f32[384,8]{0,1:T(8,128)S(1)}, u32[]{:S(2)}) copy-start(f32[384,8]{0,1:T(8,128)S(1)} %select_reduce_fusion.1) | copy-start | bytes 36868
  290.6 3.4 copy-start.5
  290.6 3.4 copy-start.22
  290.6 3.4 copy-start.35
  290.6 3.4 copy-start.49
  295.9 3.3 copy-start.2
  299.0 113.5 %reduce-scatter.16.cloned.1.call-start = ((), (), s32[]{:S(2)}) async-start(), calls=%async_computation.12 | async-start | bytes 1769472 | tf_op jit(solution)/shard_map/reduce_scatter | solution.py:1193
  308.2 15.7 %copy-start.45 = (f32[384,4]{0,1:T(4,128)S(1)}, f32[384,4]{0,1:T(4,128)}, u32[]{:S(2)}) copy-start(f32[384,4]{0,1:T(4,128)} %copy.208) | copy-start | bytes 18436
  308.2 15.7 %copy-start.64 = (pred[384,4]{0,1:T(4,128)(4,1)S(1)}, pred[384,4]{0,1:T(4,128)(4,1)}, u32[]{:S(2)}) copy-start(pred[384,4]{0,1:T(4,128)(4,1)} %copy.198) | copy-start | bytes 4612
  323.9 3.0 copy-start.42
  323.9 3.0 copy-start.55
  328.0 10.0 %collective-permute-start = (bf16[384,128]{1,0:T(8,128)(2,1)S(1)}, bf16[384,128]{1,0:T(8,128)(2,1)S(1)}, u32[]{:S(2)}, u32[]{:S(2)}) collective-permute-start(bf16[384,128]{1,0:T(8,128)(2,1)S(1)} %copy.241), channel_id=1, source_target_pairs={{0,8},{8,16},{16,24},{24,0},{1,9},{9,17},{17,25},{25,1},{2,10},{10... | collective-permute-start | bytes 294920 | tf_op jit(solution)/shard_map/while/body/eval_jaxpr/ppermute | solution.py:25
  330.6 6.6 collective-permute-start.1
  338.0 10.9 %collective-permute-start = (bf16[384,128]{1,0:T(8,128)(2,1)S(1)}, bf16[384,128]{1,0:T(8,128)(2,1)S(1)}, u32[]{:S(2)}, u32[]{:S(2)}) collective-permute-start(bf16[384,128]{1,0:T(8,128)(2,1)S(1)} %copy.241), channel_id=1, source_target_pairs={{0,8},{8,16},{16,24},{24,0},{1,9},{9,17},{17,25},{25,1},{2,10},{10... | collective-permute-start | bytes 294920 | tf_op jit(solution)/shard_map/while/body/eval_jaxpr/ppermute | solution.py:25
  341.5 6.6 collective-permute-start.1
  348.9 10.9 %collective-permute-start = (bf16[384,128]{1,0:T(8,128)(2,1)S(1)}, bf16[384,128]{1,0:T(8,128)(2,1)S(1)}, u32[]{:S(2)}, u32[]{:S(2)}) collective-permute-start(bf16[384,128]{1,0:T(8,128)(2,1)S(1)} %copy.241), channel_id=1, source_target_pairs={{0,8},{8,16},{16,24},{24,0},{1,9},{9,17},{17,25},{25,1},{2,10},{10... | collective-permute-start | bytes 294920 | tf_op jit(solution)/shard_map/while/body/eval_jaxpr/ppermute | solution.py:25
  352.4 6.6 collective-permute-start.1
  359.8 10.9 %collective-permute-start = (bf16[384,128]{1,0:T(8,128)(2,1)S(1)}, bf16[384,128]{1,0:T(8,128)(2,1)S(1)}, u32[]{:S(2)}, u32[]{:S(2)}) collective-permute-start(bf16[384,128]{1,0:T(8,128)(2,1)S(1)} %copy.241), channel_id=1, source_target_pairs={{0,8},{8,16},{16,24},{24,0},{1,9},{9,17},{17,25},{25,1},{2,10},{10... | collective-permute-start | bytes 294920 | tf_op jit(solution)/shard_map/while/body/eval_jaxpr/ppermute | solution.py:25
  363.3 6.6 collective-permute-start.1
  375.0 2.8 copy-start.28
  375.0 3.0 copy-start.16
  375.0 3.4 copy-start.29
  375.0 4.6 copy-start.6
  375.0 74.5 %reduce-scatter.24.cloned.1.call-start = ((), (), s32[]{:S(2)}) async-start(), calls=%async_computation.16 | async-start | bytes 147456
  377.8 108.8 %reduce-scatter.22.cloned.1.call-start = ((), (), s32[]{:S(2)}) async-start(), calls=%async_computation.15 | async-start | bytes 147456
  379.5 143.9 %reduce-scatter.18.cloned.1.call-start = ((), (), s32[]{:S(2)}) async-start(), calls=%async_computation.13 | async-start | bytes 147456 | tf_op jit(solution)/shard_map/reduce_scatter | solution.py:1196
  380.6 182.8 %all-reduce.10.cloned.1.call-start = ((), (), s32[]{:S(2)}) async-start(), calls=%async_computation.17 | async-start | bytes 786432 | tf_op jit(solution)/shard_map/psum | solution.py:1181
  412.6 204.9 %reduce-scatter.14.cloned.1.call-start = ((), (), s32[]{:S(2)}) async-start(), calls=%async_computation.11 | async-start | bytes 4718592 | tf_op jit(solution)/shard_map/reduce_scatter | solution.py:1228
  421.6 251.1 %reduce-scatter.12.cloned.1.call-start = ((), (), s32[]{:S(2)}) async-start(), calls=%async_computation.10 | async-start | bytes 4718592 | tf_op jit(solution)/shard_map/reduce_scatter | solution.py:1225
  430.3 19.9 %copy-start.23 = (bf16[512,256]{1,0:T(8,128)(2,1)S(1)}, bf16[512,256]{1,0:T(8,128)(2,1)}, u32[]{:S(2)}) copy-start(bf16[512,256]{1,0:T(8,128)(2,1)} %get-tuple-element.109) | copy-start | bytes 786436
  430.4 20.7 %copy-start.11 = (bf16[1,384,512]{2,1,0:T(8,128)(2,1)S(1)}, bf16[1,384,512]{2,1,0:T(8,128)(2,1)}, u32[]{:S(2)}) copy-start(bf16[1,384,512]{2,1,0:T(8,128)(2,1)} %param.20) | copy-start | bytes 1179652
  430.4 20.7 %copy-start.48 = (f32[384]{0:T(512)S(1)}, f32[384]{0:T(512)}, u32[]{:S(2)}) copy-start(f32[384]{0:T(512)} %copy-done.47) | copy-start | bytes 4612
  430.4 20.7 %copy-start.57 = (f32[1,512]{1,0:T(1,128)S(1)}, f32[1,512]{1,0:T(1,128)}, u32[]{:S(2)}) copy-start(f32[1,512]{1,0:T(1,128)} %get-tuple-element.242) | copy-start | bytes 6148
  430.4 20.7 %copy-start.59 = (f32[384]{0:T(512)S(1)}, f32[384]{0:T(512)}, u32[]{:S(2)}) copy-start(f32[384]{0:T(512)} %get-tuple-element.254) | copy-start | bytes 4612
  (26 other events, 37.9 us)
Sparse Core Ops, SparseCore 0:
  299.1 36.6 reduce-scatter.19
  375.1 37.3 reduce-scatter.15
  416.1 33.2 reduce-scatter.23
  453.2 33.3 reduce-scatter.21
  490.0 33.3 reduce-scatter.17
  525.8 37.5 all-reduce.9
  566.7 50.7 reduce-scatter.13
  621.2 51.3 reduce-scatter.11

commit v2 on v0

--- a/solution.py
+++ b/solution.py
@@ -1,8 +1,11 @@
 from functools import partial
+from types import SimpleNamespace
 
 import jax
 import jax.numpy as jnp
 from jax import lax
+from jax.experimental import pallas as pl
+from jax.experimental.pallas import tpu as pltpu
 from jax.sharding import PartitionSpec as P
 
 D = 512
@@ -11,6 +14,7 @@
 MOA_TOP = 4
 EXP_DEV = 2
 FFN_TOP = 2
+FF = 2048
 
 
 EPS = 1e-05
@@ -55,12 +59,14 @@
 
 def expert_slots(route_ids, experts):
     flat_ids = route_ids.reshape(-1)
-    table = (flat_ids[:, None] == jnp.arange(experts, dtype=jnp.int32)[None, :]).astype(jnp.int32)
-    earlier = jnp.cumsum(table, 0) - table
-    return jnp.sum(earlier * table, 1).reshape(route_ids.shape)
-
-
-def body(
+    table = (flat_ids[:, None] == jnp.arange(experts, dtype=jnp.int32)[None, :]).astype(jnp.float32)
+    place = jnp.arange(flat_ids.shape[0], dtype=jnp.int32)
+    before = (place[None, :] < place[:, None]).astype(jnp.bfloat16)
+    earlier = jnp.dot(before, table.astype(jnp.bfloat16), preferred_element_type=jnp.float32)
+    return jnp.sum(earlier * table, 1).astype(jnp.int32).reshape(route_ids.shape)
+
+
+def general_body(
     states,
     remaining,
     moa_ids,
@@ -384,6 +390,1192 @@
     )
 
 
+MESH = pl.DeviceIdType.MESH
+CAP = 192
+LIMIT_MIB = 63
+KEEP = 0.7071067811865476
+SPREAD = 0.3989422804014327
+ERF_P = 0.3275911
+ERF_A = (0.254829592, -0.284496736, 1.421413741, -1.453152027, 1.061405429)
+
+
+def remote(source, target, send_sem, recv_sem, device):
+    return pltpu.make_async_remote_copy(
+        src_ref=source,
+        dst_ref=target,
+        send_sem=send_sem,
+        recv_sem=recv_sem,
+        device_id=device,
+        device_id_type=MESH,
+    )
+
+
+def places():
+    ctx, seq, wsh = (lax.axis_index(name) for name in ("ctx", "seq", "wsh"))
+    chip, core = seq // 2, seq % 2
+    over = (1 - chip) * 2 + core
+    twin = (ctx, chip * 2 + 1 - core, wsh)
+    beside = (ctx, over, wsh)
+    above = (ctx, seq, 1 - wsh)
+    across = (ctx, over, 1 - wsh)
+    return (ctx, seq, wsh), twin, beside, above, across
+
+
+def shard_of(place):
+    return place[1] * 2 + place[2]
+
+
+def moved(place, offset, length):
+    return ((place[0] + offset) % length, place[1], place[2])
+
+
+class PlaneGather:
+    def __init__(self, shard, full, halves, send, recv, local):
+        self.shard, self.full, self.halves = shard, full, halves
+        self.send, self.recv, self.local = send, recv, local
+        self.me, self.twin, self.beside, self.above, self.across = places()
+
+    def pair(self, view, slot, device):
+        return remote(view, view, self.send.at[slot], self.recv.at[slot], device)
+
+    def own(self, slot, device):
+        target = self.full(shard_of(self.me))
+        return remote(self.shard, target, self.send.at[slot], self.recv.at[slot], device)
+
+    def keep(self):
+        return pltpu.make_async_copy(self.shard, self.full(shard_of(self.me)), self.local)
+
+    def start(self):
+        self.own(0, self.twin).start()
+        self.own(1, self.beside).start()
+        self.own(2, self.above).start()
+        if self.halves is None:
+            self.own(3, self.across).start()
+        self.keep().start()
+
+    def arrive(self, slot, place):
+        self.pair(self.full(shard_of(place)), slot, self.twin).wait_recv()
+
+    def relay(self):
+        if self.halves is None:
+            for slot, place in ((1, self.beside), (2, self.above), (3, self.across)):
+                self.arrive(slot, place)
+                self.pair(self.full(shard_of(place)), slot + 3, self.twin).start()
+            return
+        self.arrive(1, self.beside)
+        self.pair(self.halves(shard_of(self.beside), 1), 7, self.above).start()
+        self.pair(self.full(shard_of(self.beside)), 4, self.twin).start()
+        self.arrive(2, self.above)
+        self.pair(self.halves(shard_of(self.above), 0), 3, self.beside).start()
+        self.pair(self.full(shard_of(self.above)), 5, self.twin).start()
+
+    def relay_rest(self):
+        shard = shard_of(self.across)
+        for slot, half in ((3, 0), (7, 1)):
+            view = self.halves(shard, half)
+            self.pair(view, slot, self.twin).wait_recv()
+            self.pair(view, 6 if half == 0 else 8, self.twin).start()
+
+    def finish(self):
+        self.keep().wait()
+        ctx, seq, wsh = self.twin
+        over = (1 - seq // 2) * 2 + seq % 2
+        self.arrive(0, self.twin)
+        self.arrive(4, (ctx, over, wsh))
+        self.arrive(5, (ctx, seq, 1 - wsh))
+        rest = shard_of((ctx, over, 1 - wsh))
+        if self.halves is None:
+            self.pair(self.full(rest), 6, self.twin).wait_recv()
+        else:
+            self.pair(self.halves(rest, 0), 6, self.twin).wait_recv()
+            self.pair(self.halves(rest, 1), 8, self.twin).wait_recv()
+
+    def drain(self):
+        self.own(0, self.twin).wait_send()
+        self.own(1, self.beside).wait_send()
+        self.own(2, self.above).wait_send()
+        beside, above, across = (shard_of(p) for p in (self.beside, self.above, self.across))
+        self.pair(self.full(beside), 4, self.twin).wait_send()
+        self.pair(self.full(above), 5, self.twin).wait_send()
+        if self.halves is None:
+            self.own(3, self.across).wait_send()
+            self.pair(self.full(across), 6, self.twin).wait_send()
+        else:
+            self.pair(self.halves(above, 0), 3, self.beside).wait_send()
+            self.pair(self.halves(beside, 1), 7, self.above).wait_send()
+            self.pair(self.halves(across, 0), 6, self.twin).wait_send()
+            self.pair(self.halves(across, 1), 8, self.twin).wait_send()
+
+
+class LineGather:
+    def __init__(self, length, blocks, send, recv):
+        self.length, self.blocks, self.send, self.recv = length, blocks, send, recv
+        self.me = places()[0]
+
+    def hop(self, block, way, step, device):
+        view = self.blocks(block)
+        return remote(view, view, self.send.at[way, step], self.recv.at[way, step], device)
+
+    def ways(self, step):
+        ctx = self.me[0]
+        left = (ctx - 1, self.me[1], self.me[2])
+        right = (ctx + 1, self.me[1], self.me[2])
+        return (
+            (0, ctx - step, ctx - step >= 0, right, ctx + 1 < self.length),
+            (1, ctx + step, ctx + step < self.length, left, ctx - 1 >= 0),
+        )
+
+    def start(self):
+        for way, block, unused, device, there in self.ways(0):
+            pl.when(there)(lambda b=block, w=way, d=device: self.hop(b, w, 0, d).start())
+
+    def relay(self, step):
+        for way, block, come, device, there in self.ways(step):
+
+            def pass_on(way=way, block=block, device=device, there=there):
+                self.hop(block, way, step - 1, device).wait_recv()
+                if step < self.length - 1:
+                    pl.when(there)(lambda: self.hop(block, way, step, device).start())
+
+            pl.when(come)(pass_on)
+
+    def drain(self):
+        for step in range(self.length - 1):
+            for way, block, come, device, there in self.ways(step):
+                pl.when(jnp.logical_and(come, there))(
+                    lambda b=block, w=way, d=device, s=step: self.hop(b, w, s, d).wait_send()
+                )
+
+
+def direct_send(view, send, recv, length):
+    me = places()[0]
+    return [
+        remote(view, view, send.at[step - 1], recv.at[step - 1], moved(me, step, length))
+        for step in range(1, length)
+    ]
+
+
+def direct_wait(view_of, send, recv, length):
+    me = places()[0]
+    for step in range(1, length):
+        source = moved(me, length - step, length)
+        view = view_of(source[0])
+        remote(view, view, send.at[step - 1], recv.at[step - 1], source).wait_recv()
+
+
+def lanes_of(shape):
+    return lax.broadcasted_iota(jnp.int32, shape, 1)
+
+
+def rows_of(shape):
+    return lax.broadcasted_iota(jnp.int32, shape, 0)
+
+
+def product(left, right, dims=((1,), (0,))):
+    return lax.dot_general(left, right, (dims, ((), ())), preferred_element_type=jnp.float32)
+
+
+def gelu_parts(values):
+    near = jnp.abs(values) * KEEP
+    turn = 1.0 / (1.0 + ERF_P * near)
+    bell = jnp.exp(-near * near)
+    series = ERF_A[4]
+    for term in ERF_A[3::-1]:
+        series = series * turn + term
+    tail = 0.5 * series * turn * bell
+    share = jnp.where(values >= 0, 1.0 - tail, tail)
+    return values * share, share + values * bell * SPREAD
+
+
+def forward_part(length, r):
+    f32, bf16 = jnp.float32, jnp.bfloat16
+    tokens = r.states.shape[0]
+    me, twin, beside, above, across = places()
+    ctx = me[0]
+    experts = EXP_DEV * length
+    peers = [twin, beside, above, across] + [moved(me, k, length) for k in range(1, length)]
+    barrier = pltpu.get_barrier_semaphore()
+    for peer in peers:
+        pl.semaphore_signal(barrier, inc=1, device_id=peer, device_id_type=MESH)
+
+    def gather(index, shard, full, halves=None):
+        return PlaneGather(
+            shard, full, halves, r.plane_send.at[index], r.plane_recv.at[index], r.plane_local.at[index]
+        )
+
+    def rows_view(ref, rows):
+        return lambda shard: ref.at[pl.ds(shard * rows, rows), :]
+
+    pack_gather = gather(0, r.pack, rows_view(r.packed, 64))
+    query_gather = gather(1, r.query_part, rows_view(r.query, 64))
+    project_gather = gather(2, r.project_part, rows_view(r.project, 192))
+    inner_gather = gather(
+        3,
+        r.inner_part,
+        lambda shard: r.inner.at[:, pl.ds(shard * 64, 64), :],
+        lambda shard, half: r.inner.at[half, pl.ds(shard * 64, 64), :],
+    )
+    outer_gather = gather(
+        4,
+        r.outer_part,
+        lambda shard: r.outer.at[:, pl.ds(shard * 256, 256), :],
+        lambda shard, half: r.outer.at[half, pl.ds(shard * 256, 256), :],
+    )
+    cot_gather = LineGather(length, lambda b: r.cots.at[b], r.line_send.at[0], r.line_recv.at[0])
+    entering_gather = LineGather(length, lambda b: r.entering.at[b], r.line_send.at[1], r.line_recv.at[1])
+
+    def keyval_view(block):
+        return r.keyval.at[pl.ds(block * tokens, tokens), :]
+
+    r.cots[ctx] = r.cotangent[...].astype(bf16)
+    pl.semaphore_wait(barrier, len(peers))
+    pack_gather.start()
+    query_gather.start()
+    cot_gather.start()
+
+    values = r.states[...].astype(f32)
+    centred = values - jnp.mean(values, -1, keepdims=True)
+    inverse = lax.rsqrt(jnp.mean(centred * centred, -1, keepdims=True) + EPS)
+    r.flow[...] = centred * inverse
+
+    lane = lanes_of((tokens, 128))
+    ids = r.route_ids[...].astype(f32)
+    both = jnp.where(lane == 0, ids[:, 0:1], ids[:, 1:2])
+    turned = jnp.transpose(both)[0:8]
+    expert_row = rows_of((8, tokens)).astype(f32)
+    picked = jnp.logical_or(expert_row == turned[0:1], expert_row == turned[1:2])
+    marks = jnp.concatenate([picked.astype(f32), jnp.zeros((8, tokens), f32)], 0).astype(bf16)
+    earlier = (rows_of((tokens, tokens)) < lanes_of((tokens, tokens))).astype(f32).astype(bf16)
+    ranks = product(marks, earlier)[0:8]
+    r.routes[ctx, 0:8, :] = jnp.where(picked, ranks, -1.0)
+
+    pack_gather.relay()
+    pack_gather.finish()
+    r.small[...] = jnp.transpose(r.packed[:, 128:256].astype(f32))
+    shaped = (r.flow[...] * r.small[32:33, :] + r.small[33:34, :]).astype(bf16)
+    r.acted[...] = shaped
+    sides = product(shaped, r.packed[...])
+    keyval_view(ctx)[...] = sides[:, 0:128].astype(bf16)
+    keyval_sends = direct_send(keyval_view(ctx), r.direct_sems.at[0], r.direct_recvs.at[0], length)
+    for copy in keyval_sends:
+        copy.start()
+
+    id_lanes = [r.head_ids[:, j : j + 1] for j in range(MOA_TOP)]
+    logits = [
+        jnp.sum(jnp.where(lane == id_lanes[j], sides[:, 128:256], 0.0), -1, keepdims=True)
+        for j in range(MOA_TOP)
+    ]
+    peak = jnp.maximum(jnp.maximum(logits[0], logits[1]), jnp.maximum(logits[2], logits[3]))
+    powers = [jnp.exp(item - peak) for item in logits]
+    total = powers[0] + powers[1] + powers[2] + powers[3]
+    gates = [item / total for item in powers]
+    r.head_gates[...] = jnp.where(
+        lane == 0,
+        gates[0],
+        jnp.where(lane == 1, gates[1], jnp.where(lane == 2, gates[2], gates[3])),
+    )
+
+    query_gather.relay()
+    project_gather.start()
+    inner_gather.start()
+    query_gather.finish()
+    for part in range(6):
+        columns = slice(part * 256, part * 256 + 256)
+        r.mixture[:, columns] = product(r.acted[...], r.query[:, columns]).astype(bf16)
+    cot_gather.relay(1)
+
+    low_half = lane < HS
+    side = lane // HS
+    for j in range(MOA_TOP):
+        wanted = id_lanes[j] - side
+        chosen = jnp.zeros((tokens, 128), f32)
+        for pair in range(MOA_EXPERTS // 2):
+            block = r.mixture[:, pair * 128 : pair * 128 + 128].astype(f32)
+            chosen = chosen + jnp.where(wanted == 2 * pair, block, 0.0)
+        folded = chosen + pltpu.roll(chosen, HS, 1)
+        r.queries[j * tokens : (j + 1) * tokens, :] = (
+            jnp.where(low_half, folded, 0.0) * HS ** (-0.5)
+        ).astype(bf16)
+
+    direct_wait(keyval_view, r.direct_sems.at[0], r.direct_recvs.at[0], length)
+    chunk = 256
+
+    def attend(turn, carried):
+        rows = pl.ds(pl.multiple_of(turn * chunk, chunk), chunk)
+        scores = product(r.queries[rows, :], r.keyval[...], ((1,), (1,)))
+        top = jnp.max(scores, -1, keepdims=True)
+        weights = jnp.exp(scores - top)
+        mass = jnp.sum(weights, -1, keepdims=True)
+        seen = product(weights.astype(bf16), r.keyval[...]) / mass
+        r.heads[rows, :] = jnp.where(lanes_of((chunk, 128)) < HS, top + jnp.log(mass), seen)
+        return carried
+
+    lax.fori_loop(0, MOA_TOP * tokens // chunk, attend, 0)
+    project_gather.relay()
+
+    spread = []
+    for j in range(MOA_TOP):
+        head = r.heads[j * tokens : (j + 1) * tokens, :]
+        both = jnp.where(low_half, pltpu.roll(head, HS, 1), head)
+        spread.append(both * r.head_gates[:, j : j + 1])
+    for pair in range(MOA_EXPERTS // 2):
+        block = jnp.zeros((tokens, 128), f32)
+        for j in range(MOA_TOP):
+            block = jnp.where(id_lanes[j] - side == 2 * pair, spread[j], block)
+        r.mixture[:, pair * 128 : pair * 128 + 128] = block.astype(bf16)
+
+    project_gather.finish()
+    between = r.states[...].astype(f32) + product(r.mixture[...], r.project[...])
+    r.middle[...] = between
+    centred = between - jnp.mean(between, -1, keepdims=True)
+    inverse = lax.rsqrt(jnp.mean(centred * centred, -1, keepdims=True) + EPS)
+    entry = (centred * inverse * r.small[34:35, :] + r.small[35:36, :]).astype(bf16)
+    r.entering[ctx] = entry
+    entering_gather.start()
+    logits = product(r.small[16:32, :].astype(bf16), entry, ((1,), (1,)))[8:16]
+    peak = jnp.max(jnp.where(picked, logits, -1e30), 0, keepdims=True)
+    powers = jnp.where(picked, jnp.exp(jnp.where(picked, logits - peak, 0.0)), 0.0)
+    r.routes[ctx, 8:16, :] = powers / jnp.sum(powers, 0, keepdims=True)
+    route_sends = direct_send(r.routes.at[ctx], r.direct_sems.at[1], r.direct_recvs.at[1], length)
+    for copy in route_sends:
+        copy.start()
+
+    def selection(source, expert):
+        row = r.routes[source, pl.ds(EXP_DEV * ctx + expert, 1), :]
+        return rows_of((CAP, tokens)).astype(f32) == row
+
+    def slots(source):
+        return pl.ds(pl.multiple_of(source * CAP, CAP), CAP)
+
+    def first_half(source):
+        def one(expert, carried):
+            chosen = selection(source, expert).astype(f32).astype(bf16)
+            rows = product(chosen, r.entering[source]).astype(bf16)
+            r.slot_rows[expert, slots(source), :] = rows
+
+            def part(index, kept):
+                columns = pl.ds(pl.multiple_of(index * 512, 512), 512)
+                before = product(rows, r.inner[expert, :, columns])
+                value, gradient = gelu_parts(before)
+                r.active[expert, slots(source), columns] = value.astype(bf16)
+                r.slope[expert, slots(source), columns] = gradient.astype(bf16)
+                return kept
+
+            return lax.fori_loop(0, 4, part, carried)
+
+        lax.fori_loop(0, EXP_DEV, one, 0)
+
+    inner_gather.relay()
+    outer_gather.start()
+    direct_wait(lambda b: r.routes.at[b], r.direct_sems.at[1], r.direct_recvs.at[1], length)
+    entering_gather.relay(1)
+    inner_gather.relay_rest()
+    inner_gather.finish()
+
+    def step_of(step, carried):
+        for ahead in range(2, length):
+
+            @pl.when(step == ahead - 1)
+            def _():
+                entering_gather.relay(ahead)
+                if ahead < length - 1:
+                    pass
+
+        @pl.when(step == length - 2)
+        def _():
+            cot_gather.relay(2)
+
+        @pl.when(step == length - 1)
+        def _():
+            outer_gather.relay()
+
+        before_me = ctx - step >= 0
+        after_me = jnp.logical_and(ctx + step < length, step > 0)
+        count = before_me.astype(jnp.int32) + after_me.astype(jnp.int32)
+
+        def visit(turn, kept):
+            source = jnp.where(jnp.logical_and(turn == 0, before_me), ctx - step, ctx + step)
+            first_half(source)
+            return kept
+
+        lax.fori_loop(0, count, visit, 0)
+        return carried
+
+    lax.fori_loop(0, length, step_of, 0)
+    outer_gather.relay_rest()
+    cot_gather.relay(length - 1)
+    outer_gather.finish()
+
+    def second_half(turn, carried):
+        expert, part = turn // 2, turn % 2
+        rows = pl.ds(pl.multiple_of(part * 384, 384), 384)
+        r.result[expert, rows, :] = product(r.active[expert, rows, :], r.outer[expert]).astype(bf16)
+        return carried
+
+    lax.fori_loop(0, 2 * EXP_DEV, second_half, 0)
+
+    def score(source, carried):
+        lines = []
+        for expert in range(EXP_DEV):
+            chosen = selection(source, expert).astype(f32)
+            cot_rows = product(chosen.astype(bf16), r.cots[source]).astype(bf16)
+            r.slot_cot[expert, slots(source), :] = cot_rows
+            rows = r.result[expert, slots(source), :].astype(f32)
+            toward = jnp.sum(rows * r.small[36:37, :], -1, keepdims=True)
+            against = jnp.sum(rows * cot_rows.astype(f32), -1, keepdims=True)
+            lines.append(jnp.sum(chosen * toward, 0, keepdims=True))
+            lines.append(jnp.sum(chosen * against, 0, keepdims=True))
+        lines.append(jnp.zeros((8 - 2 * EXP_DEV, tokens), f32))
+        sheet = jnp.concatenate(lines, 0)
+
+        @pl.when(source == ctx)
+        def _():
+            r.scores_back[ctx] = sheet
+
+        @pl.when(source != ctx)
+        def _():
+            r.score_sent[source] = sheet
+            offset = (source - ctx + length) % length
+            remote(
+                r.score_sent.at[source],
+                r.scores_back.at[ctx],
+                r.direct_sems.at[2, offset - 1],
+                r.direct_recvs.at[2, offset - 1],
+                (source, me[1], me[2]),
+            ).start()
+
+        return carried
+
+    lax.fori_loop(0, length, score, 0)
+    direct_wait(lambda b: r.scores_back.at[b], r.direct_sems.at[2], r.direct_recvs.at[2], length)
+    for step in range(1, length):
+        target = moved(me, step, length)
+        remote(
+            r.score_sent.at[target[0]],
+            r.scores_back.at[ctx],
+            r.direct_sems.at[2, step - 1],
+            r.direct_recvs.at[2, step - 1],
+            target,
+        ).wait_send()
+    for copy in keyval_sends + route_sends:
+        copy.wait_send()
+    for item in (pack_gather, query_gather, project_gather, inner_gather, outer_gather):
+        item.drain()
+    cot_gather.drain()
+    entering_gather.drain()
+
+
+class PlaneReduce:
+    def __init__(self, piece, rows, halves, arrived, send, recv):
+        self.piece, self.rows, self.halves, self.arrived = piece, rows, halves, arrived
+        self.send, self.recv = send, recv
+        self.me, self.twin, self.beside, self.above, self.across = places()
+        self.chip, self.core, self.line = self.me[1] // 2, self.me[1] % 2, self.me[2]
+
+    def half(self, chip, core):
+        view, half = self.piece(chip, core), self.halves.at[chip]
+        return remote(view, half, self.send.at[chip], self.recv.at[chip], self.twin)
+
+    def shard(self, chip, line):
+        return self.piece(chip, self.core).at[pl.ds(line * self.rows, self.rows), :]
+
+    def start(self):
+        for chip in range(2):
+            self.half(chip, 1 - self.core).start()
+
+    def spread(self, slot, chip, line, device):
+        return remote(
+            self.shard(chip, line),
+            self.arrived.at[slot],
+            self.send.at[2 + slot],
+            self.recv.at[2 + slot],
+            device,
+        )
+
+    def sends(self):
+        return (
+            self.spread(0, 1 - self.chip, self.line, self.beside),
+            self.spread(1, self.chip, 1 - self.line, self.above),
+            self.spread(2, 1 - self.chip, 1 - self.line, self.across),
+        )
+
+    def add_halves(self):
+        for chip in range(2):
+            self.half(chip, self.core).wait_recv()
+            view = self.piece(chip, self.core)
+            both = view[...].astype(jnp.float32) + self.halves[chip].astype(jnp.float32)
+            view[...] = both.astype(jnp.bfloat16)
+        for copy in self.sends():
+            copy.start()
+
+    def total(self):
+        for copy in self.sends():
+            copy.wait_recv()
+        value = self.shard(self.chip, self.line)[...].astype(jnp.float32)
+        for slot in range(3):
+            value = value + self.arrived[slot].astype(jnp.float32)
+        return value
+
+    def drain(self):
+        for chip in range(2):
+            self.half(chip, 1 - self.core).wait_send()
+        for copy in self.sends():
+            copy.wait_send()
+
+
+class LineSum:
+    def __init__(self, length, value, parts, summed, reduce_sems, gather_sems):
+        self.length, self.value, self.parts, self.summed = length, value, parts, summed
+        self.reduce_sems, self.gather_sems = reduce_sems, gather_sems
+        self.me = places()[0]
+        self.share = value.shape[0] // length
+
+    def rows(self, block):
+        return pl.ds(pl.multiple_of(block * self.share, self.share), self.share)
+
+    def part(self, step):
+        target = moved(self.me, step, self.length)
+        send, recv = self.reduce_sems
+        return remote(
+            self.value.at[self.rows(target[0]), :],
+            self.parts.at[step - 1],
+            send.at[step - 1],
+            recv.at[step - 1],
+            target,
+        )
+
+    def start(self, value):
+        self.value[...] = value.astype(jnp.bfloat16)
+        for step in range(1, self.length):
+            self.part(step).start()
+
+    def view(self, block):
+        return self.summed.at[self.rows(block), :]
+
+    def share_out(self):
+        for step in range(1, self.length):
+            self.part(step).wait_recv()
+        value = self.value[self.rows(self.me[0]), :].astype(jnp.float32)
+        for step in range(1, self.length):
+            value = value + self.parts[step - 1].astype(jnp.float32)
+        self.view(self.me[0])[...] = value.astype(jnp.bfloat16)
+        for copy in direct_send(self.view(self.me[0]), *self.gather_sems, self.length):
+            copy.start()
+
+    def finish(self):
+        direct_wait(self.view, *self.gather_sems, self.length)
+        return self.summed[...]
+
+    def drain(self):
+        for step in range(1, self.length):
+            self.part(step).wait_send()
+        for copy in direct_send(self.view(self.me[0]), *self.gather_sems, self.length):
+            copy.wait_send()
+
+
+class ExpertReduce:
+    def __init__(self, inner, outer, half_in, half_out, side_in, side_out, last_in, last_out, send, recv):
+        self.arrays = (inner, outer)
+        self.halves = (half_in, half_out)
+        self.sides = (side_in, side_out)
+        self.lasts = (last_in, last_out)
+        self.counts = (64, 256)
+        self.send, self.recv = send, recv
+        self.me, self.twin, self.beside, self.above, unused = places()
+        self.chip, self.core, self.line = self.me[1] // 2, self.me[1] % 2, self.me[2]
+
+    def rows(self, which, chip, core, line, count):
+        size = self.counts[which]
+        start = pl.multiple_of(((chip * 2 + core) * 2 + line) * size, size)
+        return self.arrays[which].at[:, pl.ds(start, count * size), :]
+
+    def copy(self, source, target, slot, device):
+        return remote(source, target, self.send.at[slot], self.recv.at[slot], device)
+
+    def half(self, which, chip, core):
+        return self.copy(
+            self.rows(which, chip, core, 0, 2), self.halves[which].at[chip], 2 * which + chip, self.twin
+        )
+
+    def start(self, which):
+        for chip in range(2):
+            self.half(which, chip, 1 - self.core).start()
+
+    def side(self, which):
+        if which == 0:
+            source = self.rows(0, 1 - self.chip, self.core, 0, 2)
+            return [self.copy(source, self.sides[0], 4, self.beside)]
+        return [
+            self.copy(
+                self.rows(1, chip, self.core, 1 - self.line, 1), self.sides[1].at[chip], 5 + chip, self.above
+            )
+            for chip in range(2)
+        ]
+
+    def add(self, view, other):
+        for expert in range(EXP_DEV):
+            both = view[expert].astype(jnp.float32) + other[expert].astype(jnp.float32)
+            view[expert] = both.astype(jnp.bfloat16)
+
+    def add_halves(self, which):
+        def one(chip, carried):
+            self.half(which, chip, self.core).wait_recv()
+            self.add(self.rows(which, chip, self.core, 0, 2), self.halves[which].at[chip])
+            return carried
+
+        lax.fori_loop(0, 2, one, 0)
+        for copy in self.side(which):
+            copy.start()
+
+    def last(self, which):
+        if which == 0:
+            source = self.rows(0, self.chip, self.core, 1 - self.line, 1)
+            return self.copy(source, self.lasts[0], 7, self.above)
+        source = self.rows(1, 1 - self.chip, self.core, self.line, 1)
+        return self.copy(source, self.lasts[1], 8, self.beside)
+
+    def add_sides(self, which):
+        for copy in self.side(which):
+            copy.wait_recv()
+        if which == 0:
+            self.add(self.rows(0, self.chip, self.core, 0, 2), self.sides[0])
+        else:
+            for chip in range(2):
+                self.add(self.rows(1, chip, self.core, self.line, 1), self.sides[1].at[chip])
+        self.last(which).start()
+
+    def total(self, which, result):
+        self.last(which).wait_recv()
+        view = self.rows(which, self.chip, self.core, self.line, 1)
+        for expert in range(EXP_DEV):
+            both = view[expert].astype(jnp.float32) + self.lasts[which][expert].astype(jnp.float32)
+            result[expert] = both.astype(jnp.bfloat16)
+
+    def drain(self):
+        for which in range(2):
+            for chip in range(2):
+                self.half(which, chip, 1 - self.core).wait_send()
+            for copy in self.side(which):
+                copy.wait_send()
+            self.last(which).wait_send()
+
+
+def backward_part(length, r):
+    f32, bf16 = jnp.float32, jnp.bfloat16
+    tokens = r.states.shape[0]
+    me = places()[0]
+    ctx = me[0]
+    lane = lanes_of((tokens, 128))
+    low_half = lane < HS
+    side = lane // HS
+    id_lanes = [r.head_ids[:, j : j + 1] for j in range(MOA_TOP)]
+
+    def sems(row):
+        return r.direct_sems.at[row], r.direct_recvs.at[row]
+
+    def slots(source):
+        return pl.ds(pl.multiple_of(source * CAP, CAP), CAP)
+
+    def to_owner(view, target_ref, row, block):
+        slot = (block - ctx + length) % length - 1
+        send, recv = sems(row)
+        return remote(view, target_ref.at[slot], send.at[slot], recv.at[slot], (block, me[1], me[2]))
+
+    def from_all(target_ref, row):
+        send, recv = sems(row)
+        for step in range(1, length):
+            view = target_ref.at[step - 1]
+            source = moved(me, length - step, length)
+            remote(view, view, send.at[step - 1], recv.at[step - 1], source).wait_recv()
+
+    def sent_all(view_of, target_ref, row):
+        for step in range(1, length):
+            block = moved(me, step, length)[0]
+            to_owner(view_of(block), target_ref, row, block).wait_send()
+
+    r.gsmall[...] = jnp.zeros_like(r.gsmall)
+    mid = r.middle[...]
+    cot = r.cotangent[...]
+    halt_row = r.small[36:37, :]
+    reach = jnp.sum(mid * halt_row, -1, keepdims=True)
+    gap = jnp.sum(cot * (r.states[...].astype(f32) - mid), -1, keepdims=True)
+    turned = jnp.transpose(jnp.where(lane == 0, reach, gap))[0:8]
+    gates = r.routes[ctx, 8:16, :]
+    toward = jnp.concatenate(
+        [r.scores_back[d, 2 * e : 2 * e + 1, :] for d in range(length) for e in range(EXP_DEV)], 0
+    )
+    against = jnp.concatenate(
+        [r.scores_back[d, 2 * e + 1 : 2 * e + 2, :] for d in range(length) for e in range(EXP_DEV)], 0
+    )
+    halting = jax.nn.sigmoid(turned[0:1] + jnp.sum(gates * toward, 0, keepdims=True))
+    stop_grad = turned[1:2] - jnp.sum(gates * against, 0, keepdims=True)
+    mass, left = r.remaining[...], r.left_cot[...]
+    stopped = mass * halting
+    halt_grad = (stop_grad - left) * mass * halting * (1.0 - halting)
+    r.rows_out[0:1, :] = mass * (1.0 - halting)
+    r.rows_out[1:2, :] = stop_grad * halting + left * (1.0 - halting)
+    sheet = jnp.concatenate([1.0 - stopped, halt_grad, stopped, jnp.zeros((5, tokens), f32)], 0)
+    r.factors[ctx] = sheet
+    factor_sends = direct_send(r.factors.at[ctx], *sems(3), length)
+    for copy in factor_sends:
+        copy.start()
+    r.columns[...] = jnp.transpose(jnp.concatenate([sheet, jnp.zeros((120, tokens), f32)], 0))
+    gate_grad = (1.0 - stopped) * against + halt_grad * toward
+    pick_grad = gates * (gate_grad - jnp.sum(gates * gate_grad, 0, keepdims=True))
+    coarse = pick_grad.astype(bf16).astype(f32)
+    r.pick_grads[...] = jnp.concatenate([coarse, pick_grad - coarse], 0).astype(bf16)
+    sums = product(r.pick_grads[...], r.entering[ctx])
+    r.gsmall[24:32, :] = sums[0:8] + sums[8:16]
+    keep_col, halt_col = r.columns[:, 0:1], r.columns[:, 1:2]
+    r.flow[...] = keep_col * cot + halt_col * halt_row
+    r.gsmall[36:37, :] = jnp.sum(halt_col * mid, 0, keepdims=True)
+
+    def picks(block, expert):
+        row = r.routes[block, pl.ds(EXP_DEV * ctx + expert, 1), :]
+        return (rows_of((CAP, tokens)).astype(f32) == row).astype(f32)
+
+    def block_back(turn, carried):
+        offset = jnp.where(turn == 0, 0, jnp.where(turn == length - 1, 1, turn + 1))
+        block = (ctx + offset) % length
+
+        @pl.when(turn > 0)
+        def _():
+            slot = (ctx - block + length) % length - 1
+            view = r.factors.at[block]
+            send, recv = sems(3)
+            remote(view, view, send.at[slot], recv.at[slot], (block, me[1], me[2])).wait_recv()
+
+        def one(expert, kept):
+            chosen = picks(block, expert)
+            keep = jnp.sum(chosen * r.factors[block, 0:1, :], -1, keepdims=True)
+            halt = jnp.sum(chosen * r.factors[block, 1:2, :], -1, keepdims=True)
+            gate = jnp.sum(
+                chosen * r.routes[block, pl.ds(8 + EXP_DEV * ctx + expert, 1), :], -1, keepdims=True
+            )
+            rows = r.result[expert, slots(block), :].astype(f32) * gate
+            r.gsmall[36:37, :] += jnp.sum(halt * rows, 0, keepdims=True)
+            r.result[expert, slots(block), :] = rows.astype(bf16)
+            incoming = r.slot_cot[expert, slots(block), :].astype(f32)
+            rows_grad = (gate * (keep * incoming + halt * halt_row)).astype(bf16)
+            r.slot_cot[expert, slots(block), :] = rows_grad
+
+            def part(index, inside):
+                columns = pl.ds(pl.multiple_of(index * 512, 512), 512)
+                back = product(rows_grad, r.outer[expert, columns, :], ((1,), (1,)))
+                slope = r.slope[expert, slots(block), columns].astype(f32)
+                r.slope[expert, slots(block), columns] = (back * slope).astype(bf16)
+                return inside
+
+            lax.fori_loop(0, 4, part, 0)
+            sent = product(r.slope[expert, slots(block), :], r.inner[expert], ((1,), (1,)))
+            r.slot_back[expert] = sent.astype(bf16)
+            return kept
+
+        lax.fori_loop(0, EXP_DEV, one, 0)
+        spread = product(picks(block, 0).astype(bf16), r.slot_back[0], ((0,), (0,)))
+        spread = spread + product(picks(block, 1).astype(bf16), r.slot_back[1], ((0,), (0,)))
+        r.entering[block] = spread.astype(bf16)
+
+        @pl.when(turn > 0)
+        def _():
+            to_owner(r.entering.at[block], r.back_in, 4, block).start()
+
+        return carried
+
+    lax.fori_loop(0, length, block_back, 0)
+
+    def block_forward(turn, carried):
+        offset = jnp.where(turn == 0, 0, jnp.where(turn == length - 1, 1, turn + 1))
+        block = (ctx + offset) % length
+        spread = product(picks(block, 0).astype(bf16), r.result[0, slots(block), :], ((0,), (0,)))
+        spread = spread + product(
+            picks(block, 1).astype(bf16), r.result[1, slots(block), :], ((0,), (0,))
+        )
+        r.cots[block] = spread.astype(bf16)
+
+        @pl.when(turn > 0)
+        def _():
+            to_owner(r.cots.at[block], r.mix_in, 5, block).start()
+
+        return carried
+
+    lax.fori_loop(0, length, block_forward, 0)
+
+    experts = ExpertReduce(
+        r.inner, r.outer, r.half_in, r.half_out, r.side_in, r.side_out, r.last_in, r.last_out,
+        r.expert_send, r.expert_recv,
+    )
+
+    def outer_grad(turn, carried):
+        expert, part = turn // 4, turn % 4
+        columns = pl.ds(pl.multiple_of(part * 512, 512), 512)
+        value = product(r.active[expert, :, columns], r.slot_cot[expert], ((0,), (0,)))
+        r.outer[expert, columns, :] = value.astype(bf16)
+        return carried
+
+    lax.fori_loop(0, 4 * EXP_DEV, outer_grad, 0)
+    experts.start(1)
+
+    def inner_grad(turn, carried):
+        expert, part = turn // 4, turn % 4
+        columns = pl.ds(pl.multiple_of(part * 512, 512), 512)
+        value = product(r.slot_rows[expert], r.slope[expert, :, columns], ((0,), (0,)))
+        r.inner[expert, :, columns] = value.astype(bf16)
+        return carried
+
+    lax.fori_loop(0, 4 * EXP_DEV, inner_grad, 0)
+    experts.start(0)
+    experts.add_halves(1)
+    experts.add_halves(0)
+
+    from_all(r.back_in, 4)
+    mid = r.middle[...]
+    selector = r.small[24:32, :]
+    double = jnp.concatenate([selector, selector], 0).astype(bf16)
+    back = product(r.pick_grads[...], double, ((0,), (0,))) + r.entering[ctx].astype(f32)
+    for step in range(length - 1):
+        back = back + r.back_in[step].astype(f32)
+    centred = mid - jnp.mean(mid, -1, keepdims=True)
+    inverse = lax.rsqrt(jnp.mean(centred * centred, -1, keepdims=True) + EPS)
+    plain = centred * inverse
+    r.gsmall[34:35, :] = jnp.sum(back * plain, 0, keepdims=True)
+    r.gsmall[35:36, :] = jnp.sum(back, 0, keepdims=True)
+    scaled = back * r.small[34:35, :]
+    level = jnp.mean(scaled, -1, keepdims=True)
+    tilt = jnp.mean(scaled * plain, -1, keepdims=True)
+    flow = r.flow[...] + inverse * (scaled - level - plain * tilt)
+    r.flow[...] = flow
+    attn_grad = flow.astype(bf16)
+
+    def project_piece(chip, core):
+        column = pl.multiple_of((chip * 2 + core) * 512, 512)
+        return r.active.at[1, pl.ds(0, 384), pl.ds(column, 512)]
+
+    for part in range(4):
+        value = product(r.mixture[:, part * 384 : part * 384 + 384], attn_grad, ((0,), (0,)))
+        r.active[1, 0:384, part * 512 : part * 512 + 512] = value.astype(bf16)
+
+    def reducer(index, piece, rows, halves, arrived):
+        return PlaneReduce(piece, rows, halves, arrived, r.dense_send.at[index], r.dense_recv.at[index])
+
+    project_reduce = reducer(0, project_piece, 192, r.project_half, r.project_in)
+    project_reduce.start()
+
+    chosen = [jnp.zeros((tokens, 128), f32) for unused in range(MOA_TOP)]
+    for part in range(6):
+        value = product(attn_grad, r.project[part * 256 : part * 256 + 256, :], ((1,), (1,)))
+        for pair in range(2):
+            block = value[:, pair * 128 : pair * 128 + 128]
+            for j in range(MOA_TOP):
+                wanted = id_lanes[j] - side == 2 * (2 * part + pair)
+                chosen[j] = chosen[j] + jnp.where(wanted, block, 0.0)
+    gate_lanes = [r.head_gates[:, j : j + 1] for j in range(MOA_TOP)]
+    gate_grads = []
+    for j in range(MOA_TOP):
+        rows = slice(j * tokens, (j + 1) * tokens)
+        head = r.heads[rows, :]
+        folded = jnp.where(low_half, 0.0, chosen[j] + pltpu.roll(chosen[j], HS, 1))
+        gate_grads.append(jnp.sum(folded * head, -1, keepdims=True))
+        grads = (gate_lanes[j] * folded).astype(bf16)
+        r.heads_grad[rows, :] = grads
+        delta = jnp.sum(grads.astype(f32) * head, -1, keepdims=True)
+        pair = jnp.transpose(jnp.where(lane == 0, head[:, 0:1], delta))
+        r.stats[:, rows] = pair[0:8]
+    common = sum(g * v for g, v in zip(gate_lanes, gate_grads))
+    logit = jnp.zeros((tokens, 128), f32)
+    for j in range(MOA_TOP):
+        logit = jnp.where(lane == id_lanes[j], gate_lanes[j] * (gate_grads[j] - common), logit)
+    coarse = logit.astype(bf16)
+    fine = (logit - coarse.astype(f32)).astype(bf16)
+    sums = product(coarse, r.acted[...], ((0,), (0,))) + product(fine, r.acted[...], ((0,), (0,)))
+    r.gsmall[0:24, :] = sums[0:24]
+    chooser = r.small[...].astype(bf16)
+    r.acted_grad[...] = product(coarse, chooser) + product(fine, chooser)
+    project_reduce.add_halves()
+    experts.add_sides(1)
+    experts.add_sides(0)
+
+    r.kv_grad[...] = jnp.zeros_like(r.kv_grad)
+    chunk = 256
+
+    def attend_back(turn, carried):
+        rows = pl.ds(pl.multiple_of(turn * chunk, chunk), chunk)
+        query, grads, keyval = r.queries[rows, :], r.heads_grad[rows, :], r.keyval[...]
+        scores = product(keyval, query, ((1,), (1,)))
+        weights = jnp.exp(scores - r.stats[0:1, rows])
+        upward = product(keyval, grads, ((1,), (1,)))
+        score_grad = (weights * (upward - r.stats[1:2, rows])).astype(bf16)
+        r.kv_grad[...] += product(score_grad, query) + product(weights.astype(bf16), grads)
+        r.heads[rows, :] = product(score_grad, keyval, ((0,), (0,))) * HS ** (-0.5)
+        return carried
+
+    lax.fori_loop(0, MOA_TOP * tokens // chunk, attend_back, 0)
+
+    def send_keyval(turn, carried):
+        block = (ctx + turn) % length
+        rows = pl.ds(pl.multiple_of(block * tokens, tokens), tokens)
+
+        @pl.when(turn > 0)
+        def _():
+            r.heads_grad[rows, :] = r.kv_grad[rows, :].astype(bf16)
+            to_owner(r.heads_grad.at[rows, :], r.kv_in, 6, block).start()
+
+        return carried
+
+    lax.fori_loop(0, length, send_keyval, 0)
+    spread = []
+    for j in range(MOA_TOP):
+        piece = r.heads[j * tokens : (j + 1) * tokens, :]
+        spread.append(jnp.where(low_half, piece, pltpu.roll(piece, HS, 1)))
+    for pair in range(MOA_EXPERTS // 2):
+        block = jnp.zeros((tokens, 128), f32)
+        for j in range(MOA_TOP):
+            block = jnp.where(id_lanes[j] - side == 2 * pair, spread[j], block)
+        r.mixture[:, pair * 128 : pair * 128 + 128] = block.astype(bf16)
+    for part in range(4):
+        columns = slice(part * 384, part * 384 + 384)
+        value = product(r.acted[...], r.mixture[:, columns], ((0,), (0,)))
+        r.active[0, 0:512, columns] = value.astype(bf16)
+
+    def wide_piece(first, width):
+        def piece(chip, core):
+            start = pl.multiple_of((chip * 2 + core) * 128, 128)
+            return r.active.at[0, pl.ds(start, 128), pl.ds(first, width)]
+
+        return piece
+
+    query_reduce = reducer(1, wide_piece(0, 1536), 64, r.query_half, r.query_in)
+    query_reduce.start()
+    r.acted_grad[...] += product(r.mixture[...], r.query[...], ((1,), (1,)))
+    project_line = LineSum(length, r.project_value, r.project_parts, r.project_sum, sems(7), sems(8))
+    project_line.start(project_reduce.total())
+    query_reduce.add_halves()
+
+    own_rows = pl.ds(pl.multiple_of(ctx * tokens, tokens), tokens)
+    from_all(r.kv_in, 6)
+    keyval_grad = r.kv_grad[own_rows, :]
+    for step in range(length - 1):
+        keyval_grad = keyval_grad + r.kv_in[step].astype(f32)
+    keyval_grad = keyval_grad.astype(bf16)
+    back = r.acted_grad[...] + product(keyval_grad, r.packed[:, 0:128], ((1,), (1,)))
+    values = r.states[...].astype(f32)
+    centred = values - jnp.mean(values, -1, keepdims=True)
+    inverse = lax.rsqrt(jnp.mean(centred * centred, -1, keepdims=True) + EPS)
+    plain = centred * inverse
+    r.gsmall[32:33, :] = jnp.sum(back * plain, 0, keepdims=True)
+    r.gsmall[33:34, :] = jnp.sum(back, 0, keepdims=True)
+    r.active[0, 0:512, 1536:1664] = product(r.acted[...], keyval_grad, ((0,), (0,))).astype(bf16)
+    r.active[0, 0:512, 1664:1792] = jnp.transpose(r.gsmall[...]).astype(bf16)
+    small_reduce = reducer(2, wide_piece(1536, 256), 64, r.small_half, r.small_in)
+    small_reduce.start()
+    scaled = back * r.small[32:33, :]
+    level = jnp.mean(scaled, -1, keepdims=True)
+    tilt = jnp.mean(scaled * plain, -1, keepdims=True)
+    r.grad_states[...] = (
+        r.flow[...] + inverse * (scaled - level - plain * tilt) + r.columns[:, 2:3] * r.cotangent[...]
+    )
+    small_reduce.add_halves()
+    project_line.share_out()
+    query_line = LineSum(length, r.query_value, r.query_parts, r.query_sum, sems(9), sems(10))
+    query_line.start(query_reduce.total())
+    small_line = LineSum(length, r.small_value, r.small_parts, r.small_sum, sems(11), sems(12))
+    small_line.start(small_reduce.total())
+
+    experts.total(1, r.grad_outer)
+    experts.total(0, r.grad_inner)
+    from_all(r.mix_in, 5)
+    final = r.middle[...] + r.cots[ctx].astype(f32)
+    for step in range(length - 1):
+        final = final + r.mix_in[step].astype(f32)
+    r.new_states[...] = (
+        r.columns[:, 2:3] * r.states[...].astype(f32) + r.columns[:, 0:1] * final
+    ).astype(bf16)
+    query_line.share_out()
+    small_line.share_out()
+    r.grad_project[...] = project_line.finish()
+    r.grad_query[...] = query_line.finish()
+    r.grad_small[...] = small_line.finish()
+
+    for copy in factor_sends:
+        copy.wait_send()
+    sent_all(lambda b: r.entering.at[b], r.back_in, 4)
+    sent_all(lambda b: r.cots.at[b], r.mix_in, 5)
+    sent_all(
+        lambda b: r.heads_grad.at[pl.ds(pl.multiple_of(b * tokens, tokens), tokens), :], r.kv_in, 6
+    )
+    for item in (project_reduce, query_reduce, small_reduce, experts):
+        item.drain()
+    for item in (project_line, query_line, small_line):
+        item.drain()
+
+
+def whole_kernel(length, names, *refs):
+    r = SimpleNamespace(**dict(zip(names, refs)))
+    forward_part(length, r)
+    backward_part(length, r)
+
+
+def fast_body(
+    states,
+    remaining,
+    moa_ids,
+    ffn_ids,
+    out_cotangent,
+    left_cotangent,
+    query_weight,
+    keyval_weight,
+    project_weight,
+    chooser,
+    selector,
+    gain_one,
+    bias_one,
+    gain_two,
+    bias_two,
+    halt_weight,
+    expert_in,
+    expert_out,
+):
+    f32, bf16 = jnp.float32, jnp.bfloat16
+    length = lax.axis_size("ctx")
+    tokens = states.shape[1]
+    rows = length * CAP
+    wide = MOA_EXPERTS * HS
+    flat = jnp.stack([gain_one, bias_one, gain_two, bias_two, halt_weight], 1)
+    pack = jnp.concatenate(
+        [keyval_weight, chooser, selector, flat, jnp.zeros((flat.shape[0], 91), bf16)], 1
+    )
+    inputs = dict(
+        states=states[0],
+        cotangent=out_cotangent[0],
+        head_ids=moa_ids[0],
+        route_ids=ffn_ids[0],
+        remaining=remaining,
+        left_cot=left_cotangent,
+        pack=pack,
+        query_part=query_weight,
+        project_part=project_weight,
+        inner_part=expert_in,
+        outer_part=expert_out,
+    )
+    in_place = ("query_part", "project_part", "inner_part", "outer_part")
+    shape = jax.ShapeDtypeStruct
+    outputs = dict(
+        new_states=shape((tokens, D), bf16),
+        rows_out=shape((8, tokens), f32),
+        grad_states=shape((tokens, D), f32),
+        grad_query=shape((64, wide), bf16),
+        grad_project=shape((192, D), bf16),
+        grad_small=shape((64, 256), bf16),
+        grad_inner=shape((EXP_DEV, 64, FF), bf16),
+        grad_outer=shape((EXP_DEV, 256, D), bf16),
+    )
+    vmem, dma = pltpu.VMEM, pltpu.SemaphoreType.DMA
+    scratch = dict(
+        slot_rows=vmem((EXP_DEV, rows, D), bf16),
+        active=vmem((EXP_DEV, rows, FF), bf16),
+        slope=vmem((EXP_DEV, rows, FF), bf16),
+        result=vmem((EXP_DEV, rows, D), bf16),
+        slot_cot=vmem((EXP_DEV, rows, D), bf16),
+        inner=vmem((EXP_DEV, D, FF), bf16),
+        outer=vmem((EXP_DEV, FF, D), bf16),
+        query=vmem((D, wide), bf16),
+        project=vmem((wide, D), bf16),
+        packed=vmem((D, 256), bf16),
+        acted=vmem((tokens, D), bf16),
+        mixture=vmem((tokens, wide), bf16),
+        queries=vmem((MOA_TOP * tokens, 128), bf16),
+        heads=vmem((MOA_TOP * tokens, 128), f32),
+        keyval=vmem((length * tokens, 128), bf16),
+        head_gates=vmem((tokens, 128), f32),
+        middle=vmem((tokens, D), f32),
+        entering=vmem((length, tokens, D), bf16),
+        cots=vmem((length, tokens, D), bf16),
+        routes=vmem((length, 16, tokens), f32),
+        scores_back=vmem((length, 8, tokens), f32),
+        small=vmem((128, D), f32),
+        score_sent=vmem((length, 8, tokens), f32),
+        factors=vmem((length, 8, tokens), f32),
+        columns=vmem((tokens, 128), f32),
+        pick_grads=vmem((16, tokens), bf16),
+        gsmall=vmem((128, D), f32),
+        flow=vmem((tokens, D), f32),
+        slot_back=vmem((EXP_DEV, CAP, D), bf16),
+        back_in=vmem((length - 1, tokens, D), bf16),
+        mix_in=vmem((length - 1, tokens, D), bf16),
+        half_in=vmem((2, EXP_DEV, 128, FF), bf16),
+        half_out=vmem((2, EXP_DEV, 512, D), bf16),
+        side_in=vmem((EXP_DEV, 128, FF), bf16),
+        side_out=vmem((2, EXP_DEV, 256, D), bf16),
+        last_in=vmem((EXP_DEV, 64, FF), bf16),
+        last_out=vmem((EXP_DEV, 256, D), bf16),
+        heads_grad=vmem((MOA_TOP * tokens, 128), bf16),
+        stats=vmem((8, MOA_TOP * tokens), f32),
+        acted_grad=vmem((tokens, D), f32),
+        kv_grad=vmem((length * tokens, 128), f32),
+        kv_in=vmem((length - 1, tokens, 128), bf16),
+        project_half=vmem((2, 384, D), bf16),
+        project_in=vmem((3, 192, D), bf16),
+        query_half=vmem((2, 128, wide), bf16),
+        query_in=vmem((3, 64, wide), bf16),
+        small_half=vmem((2, 128, 256), bf16),
+        small_in=vmem((3, 64, 256), bf16),
+        project_value=vmem((192, D), bf16),
+        project_parts=vmem((length - 1, 192 // length, D), bf16),
+        project_sum=vmem((192, D), bf16),
+        query_value=vmem((64, wide), bf16),
+        query_parts=vmem((length - 1, 64 // length, wide), bf16),
+        query_sum=vmem((64, wide), bf16),
+        small_value=vmem((64, 256), bf16),
+        small_parts=vmem((length - 1, 64 // length, 256), bf16),
+        small_sum=vmem((64, 256), bf16),
+        plane_send=dma((5, 9)),
+        plane_recv=dma((5, 9)),
+        plane_local=dma((5,)),
+        line_send=dma((2, 2, length)),
+        line_recv=dma((2, 2, length)),
+        direct_sems=dma((13, length)),
+        direct_recvs=dma((13, length)),
+        expert_send=dma((9,)),
+        expert_recv=dma((9,)),
+        dense_send=dma((3, 5)),
+        dense_recv=dma((3, 5)),
+    )
+    in_vmem = pl.BlockSpec(memory_space=pltpu.VMEM)
+    anywhere = pl.BlockSpec(memory_space=pl.ANY)
+    names = (*inputs, *outputs, *scratch)
+    results = pl.pallas_call(
+        partial(whole_kernel, length, names),
+        out_shape=tuple(outputs.values()),
+        in_specs=[anywhere if name in in_place else in_vmem for name in inputs],
+        out_specs=[in_vmem] * len(outputs),
+        scratch_shapes=list(scratch.values()),
+        compiler_params=pltpu.CompilerParams(
+            collective_id=0, has_side_effects=True, vmem_limit_bytes=LIMIT_MIB * 2**20
+        ),
+        name="layer_step",
+    )(*inputs.values())
+    o = SimpleNamespace(**dict(zip(outputs, results)))
+    small = o.grad_small.astype(f32)
+    return (
+        o.new_states[None],
+        o.rows_out[0:1],
+        o.grad_states[None],
+        o.rows_out[1:2],
+        o.grad_query.astype(f32),
+        small[:, 0:128],
+        o.grad_project.astype(f32),
+        small[:, 128:152],
+        small[:, 152:160],
+        small[:, 160],
+        small[:, 161],
+        small[:, 162],
+        small[:, 163],
+        small[:, 164],
+        o.grad_inner.astype(f32),
+        o.grad_outer.astype(f32),
+    )
+
+
 def solution(mesh):
     in_specs = (
         P(("seq", "wsh"), "ctx", None),
@@ -423,4 +1615,5 @@
         P("ctx", ("seq", "wsh"), None),
         P("ctx", ("seq", "wsh"), None),
     )
+    body = fast_body if mesh.shape["ctx"] == 4 else general_body
     return jax.shard_map(body, mesh=mesh, in_specs=in_specs, out_specs=out_specs, check_vma=False)

time: 797 us -> 226 us (0.28)
  waiting for transfers between devices: 316 us -> 0 us
  Pallas kernels: 0 us -> 204 us
  blocking collectives: 153 us -> 0 us
  matrix products: 117 us -> 0 us
  local copies, waits for them, and re-layouts: 107 us -> 16.6 us
  other arithmetic: 61.8 us -> 4.55 us
  starting transfers between devices: 17.3 us -> 0 us
  between operations: 17.2 us -> 0.7 us
    pallas_call x0 -> x1, Pallas kernels: none -> 204 us  [fast_body(): pl.pallas_call(partial(whole_kernel, length, names), out_shape=tuple(outp...]
    reduce_scatter x5 -> x0, waiting for transfers between devices: 175 us -> none  [the longest x1 52.8 us: body(): lax.psum_scatter(inner_grad.astype(jnp.bfloat16), ('seq', 'wsh'), scatter...]
    dot_general x48 -> x0, matrix products: 117 us -> none  [the longest x1 33 us: body(): jnp.einsum('nekd,edf->nekf', arrived_rows, inner_full, preferred_element_...]
    all_to_all x3 -> x0, waiting for transfers between devices: 68.6 us -> none  [the longest x1 33.8 us: body(): lax.all_to_all(outgoing, 'ctx', split_axis=0, concat_axis=0, tiled=True)]
    all_gather x4 -> x0, blocking collectives: 64 us -> none  [the longest x1 17.7 us: body(): lax.all_gather(selector, ('seq', 'wsh'), axis=0, tiled=True)]
    gather x6 -> x0, local copies, waits for them, and re-layouts: 45.9 us -> none  [the longest x1 23 us: body(): mix_sel_grad = jnp.take_along_axis(mix_grad, head_ids[:, :, None], axis=1)]
    all_to_all x1 -> x0, blocking collectives: 40.2 us -> none  [body(): lax.all_to_all(grad_outgoing, 'ctx', split_axis=0, concat_axis=0, tiled=T...]
    unnamed x14 -> x0, waiting for transfers between devices: 35.9 us -> none
  transfers between devices with their start and end apart: 23 -> 0, of which waited for: 14 -> 0; matrix products, arithmetic and copies ran while one was open for 26% -> 0% of each run, Pallas kernels for 0% -> 0%
where the time goes in v2:
time: 226 us
  Pallas kernels  204 us (90%)
  local copies, waits for them, and re-layouts  16.6 us (7%)
  other arithmetic  4.55 us (2%)
    pallas_call x1, Pallas kernels, fast_body(): pl.pallas_call(partial(whole_kernel, length, names), out_shape=tuple(outp...  204 us
    unnamed x38, local copies, waits for them, and re-layouts  10.3 us

profile of v2, /device:TPU:0, one launch (start us, length us, event | category | flops | bytes accessed | tf_op | source)
XLA Modules:
  0.0 225.6 jit_solution(13419249465565768971)
XLA Ops:
  0.6 0.0 copy-start.8
  0.7 1.5 copy.45
  2.2 0.0 copy-done.8
  2.2 0.0 copy-start.7
  2.2 0.8 copy.46
  3.0 0.0 copy-done.7
  3.0 0.0 copy-start.9
  3.0 0.1 copy.47
  3.1 0.6 copy-done.9
  3.7 0.1 copy.48
  3.8 0.0 copy-start.10
  3.8 0.7 copy-done.10
  4.4 0.1 copy.49
  4.6 0.0 copy-start.11
  4.6 0.7 copy-done.11
  5.2 0.1 copy.50
  5.3 0.0 copy-start.12
  5.3 0.7 copy-done.12
  6.0 0.1 copy.51
  6.1 0.0 copy-start.13
  6.1 0.7 copy-done.13
  6.8 0.1 copy.52
  6.9 0.0 copy-start.14
  6.9 0.7 copy-done.14
  7.5 0.0 copy-start.6
  7.5 0.1 copy.53
  7.6 0.6 copy-done.6
  8.2 0.7 concatenate.3.refs_6_
  9.0 203.8 %layer_step.1 = (bf16[384,512]{1,0:T(8,128)(2,1)}, f32[8,384]{1,0:T(8,128)}, f32[384,512]{1,0:T(8,128)}, bf16[64,1536]{1,0:T(8,128)(2,1)}, bf16[192,512]{1,0:T(8...) custom-call(bf16[384,512]{1,0:T(8,128)(2,1)} %bitcast.15, ...), custom_call_target="tpu_custom_call" | custom-call | tf_op jit(solution)/shard_map/layer_step/pallas_call | solution.py:1546
  212.7 0.0 copy-start.2
  212.7 0.8 convert_element_type.16
  213.6 0.8 slice_reduce_fusion
  214.4 0.7 slice.41
  215.1 0.7 copy.54
  215.8 0.8 slice.42
  216.5 0.7 copy.55
  217.2 1.3 slice.40
  218.5 1.4 fusion
  219.9 0.0 copy-done.2
  219.9 0.0 copy-start.1
  219.9 1.1 convert_element_type.18
  221.0 0.1 copy-done.1
  221.0 0.0 copy-start.5
  221.0 1.1 convert_element_type.19
  222.1 0.0 copy-done.5
  222.1 0.0 copy-start.4
  222.1 0.0 copy-start.3
  222.1 0.8 convert_element_type.15
  222.9 0.0 copy-start
  222.9 0.3 copy-done.4
  223.2 0.8 convert_element_type.17
  224.0 0.0 copy-done.3
  224.0 0.7 copy.58
  224.7 0.0 copy-done
  224.7 0.9 copy.59
  (1 shorter events, 0.0 us)
Async XLA Ops:
  0.6 1.5 copy-start.8
  2.2 0.8 copy-start.7
  3.0 0.7 copy-start.9
  3.8 0.7 copy-start.10
  4.6 0.7 copy-start.11
  5.3 0.7 copy-start.12
  6.1 0.7 copy-start.13
  6.9 0.7 copy-start.14
  7.5 0.7 copy-start.6
  212.7 7.2 %copy-start.2 = (bf16[2,64,2048]{2,1,0:T(8,128)(2,1)S(1)}, bf16[2,64,2048]{2,1,0:T(8,128)(2,1)}, u32[]{:S(2)}) copy-start(bf16[2,64,2048]{2,1,0:T(8,128)(2,1)} %get-tuple-element.30) | copy-start | bytes 1572868
  219.9 1.1 copy-start.1
  221.0 1.1 copy-start.5
  222.1 1.0 copy-start.4
  222.1 1.8 copy-start.3
  222.9 1.8 copy-start

commit v3 on v2

--- a/solution.py
+++ b/solution.py
@@ -429,6 +429,11 @@
     return ((place[0] + offset) % length, place[1], place[2])
 
 
+def plane_peer(place, step):
+    shard = (shard_of(place) + step) % 8
+    return (place[0], shard // 2, shard % 2)
+
+
 class PlaneGather:
     def __init__(self, shard, full, halves, send, recv, local):
         self.shard, self.full, self.halves = shard, full, halves
@@ -507,6 +512,25 @@
             self.pair(self.halves(across, 1), 8, self.twin).wait_send()
 
 
+class PlaneShare:
+    def __init__(self, blocks, send, recv):
+        self.blocks, self.send, self.recv = blocks, send, recv
+        self.me = places()[0]
+        self.shard = shard_of(self.me)
+
+    def copy(self, shard, step, device):
+        view = self.blocks.at[shard]
+        return remote(view, view, self.send.at[step - 1], self.recv.at[step - 1], device)
+
+    def sends(self):
+        return [self.copy(self.shard, step, plane_peer(self.me, step)) for step in range(1, 8)]
+
+    def wait(self):
+        for step in range(1, 8):
+            source = plane_peer(self.me, 8 - step)
+            self.copy(shard_of(source), step, source).wait_recv()
+
+
 class LineGather:
     def __init__(self, length, blocks, send, recv):
         self.length, self.blocks, self.send, self.recv = length, blocks, send, recv
@@ -587,13 +611,44 @@
     return values * share, share + values * bell * SPREAD
 
 
+def picks(r, block, expert):
+    tokens = r.states.shape[0]
+    row = r.routes[block, pl.ds(EXP_DEV * lax.axis_index("ctx") + expert, 1), :]
+    return (rows_of((CAP, tokens)).astype(jnp.float32) == row).astype(jnp.float32)
+
+
+def slots(block):
+    return pl.ds(pl.multiple_of(block * CAP, CAP), CAP)
+
+
+def to_owner(length, r, view, target, row, block):
+    me = places()[0]
+    slot = (block - me[0] + length) % length - 1
+    send, recv = r.direct_sems.at[row, slot], r.direct_recvs.at[row, slot]
+    return remote(view, target.at[slot], send, recv, (block, me[1], me[2]))
+
+
+def give_back(length, r, block):
+    total = 0.0
+    for expert in range(EXP_DEV):
+        chosen = picks(r, block, expert).astype(jnp.bfloat16)
+        total = total + product(chosen, r.result[expert, slots(block), :], ((0,), (0,)))
+    r.cots[block] = total.astype(jnp.bfloat16)
+
+
+def returns(length, r):
+    return (
+        LineReturn(length, r.cots, r.mix_in, r.return_send.at[0], r.return_recv.at[0]),
+        LineReturn(length, r.entering, r.back_in, r.return_send.at[1], r.return_recv.at[1]),
+    )
+
+
 def forward_part(length, r):
     f32, bf16 = jnp.float32, jnp.bfloat16
     tokens = r.states.shape[0]
     me, twin, beside, above, across = places()
     ctx = me[0]
-    experts = EXP_DEV * length
-    peers = [twin, beside, above, across] + [moved(me, k, length) for k in range(1, length)]
+    peers = [plane_peer(me, k) for k in range(1, 8)] + [moved(me, k, length) for k in range(1, length)]
     barrier = pltpu.get_barrier_semaphore()
     for peer in peers:
         pl.semaphore_signal(barrier, inc=1, device_id=peer, device_id_type=MESH)
@@ -606,31 +661,45 @@
     def rows_view(ref, rows):
         return lambda shard: ref.at[pl.ds(shard * rows, rows), :]
 
-    pack_gather = gather(0, r.pack, rows_view(r.packed, 64))
-    query_gather = gather(1, r.query_part, rows_view(r.query, 64))
-    project_gather = gather(2, r.project_part, rows_view(r.project, 192))
+    def half_view(ref, rows):
+        return lambda shard, half: ref.at[pl.ds(shard * rows + half * (rows // 2), rows // 2), :]
+
+    pack_share = PlaneShare(r.packs, r.pack_send, r.pack_recv)
+    query_gather = gather(0, r.query_part, rows_view(r.query, 64), half_view(r.query, 64))
+    project_gather = gather(1, r.project_part, rows_view(r.project, 192), half_view(r.project, 192))
     inner_gather = gather(
-        3,
+        2,
         r.inner_part,
         lambda shard: r.inner.at[:, pl.ds(shard * 64, 64), :],
         lambda shard, half: r.inner.at[half, pl.ds(shard * 64, 64), :],
     )
-    outer_gather = gather(
-        4,
-        r.outer_part,
-        lambda shard: r.outer.at[:, pl.ds(shard * 256, 256), :],
-        lambda shard, half: r.outer.at[half, pl.ds(shard * 256, 256), :],
-    )
+    outer_gathers = [
+        gather(
+            3 + k, r.outer_part.at[k], rows_view(r.outer.at[k], 256), half_view(r.outer.at[k], 256)
+        )
+        for k in range(EXP_DEV)
+    ]
     cot_gather = LineGather(length, lambda b: r.cots.at[b], r.line_send.at[0], r.line_recv.at[0])
     entering_gather = LineGather(length, lambda b: r.entering.at[b], r.line_send.at[1], r.line_recv.at[1])
 
     def keyval_view(block):
         return r.keyval.at[pl.ds(block * tokens, tokens), :]
 
+    fetch = pltpu.make_async_copy(r.cotangent_part, r.cotangent, r.plane_local.at[5])
+    fetch.start()
+    shard = shard_of(me)
+    r.packs[shard, 0:64, :] = r.keyval_part[...]
+    rows = [r.chooser_part[...].astype(f32), r.selector_part[...].astype(f32), r.vectors[...].astype(f32)]
+    rows = jnp.concatenate([*rows, jnp.zeros((8, 64), f32)], 0)
+    r.packs[shard, 64:112, :] = jnp.concatenate([rows, jnp.zeros((48, 64), f32)], 1).astype(bf16)
+    pl.semaphore_wait(barrier, len(peers))
+    pack_sends = pack_share.sends()
+    for copy in pack_sends:
+        copy.start()
+    query_gather.start()
+    project_gather.start()
+    fetch.wait()
     r.cots[ctx] = r.cotangent[...].astype(bf16)
-    pl.semaphore_wait(barrier, len(peers))
-    pack_gather.start()
-    query_gather.start()
     cot_gather.start()
 
     values = r.states[...].astype(f32)
@@ -639,9 +708,7 @@
     r.flow[...] = centred * inverse
 
     lane = lanes_of((tokens, 128))
-    ids = r.route_ids[...].astype(f32)
-    both = jnp.where(lane == 0, ids[:, 0:1], ids[:, 1:2])
-    turned = jnp.transpose(both)[0:8]
+    turned = r.route_ids[...].astype(f32)
     expert_row = rows_of((8, tokens)).astype(f32)
     picked = jnp.logical_or(expert_row == turned[0:1], expert_row == turned[1:2])
     marks = jnp.concatenate([picked.astype(f32), jnp.zeros((8, tokens), f32)], 0).astype(bf16)
@@ -649,20 +716,27 @@
     ranks = product(marks, earlier)[0:8]
     r.routes[ctx, 0:8, :] = jnp.where(picked, ranks, -1.0)
 
-    pack_gather.relay()
-    pack_gather.finish()
-    r.small[...] = jnp.transpose(r.packed[:, 128:256].astype(f32))
+    ids = jnp.concatenate([r.head_ids[...].astype(f32), jnp.zeros((124, tokens), f32)], 0)
+    r.id_columns[...] = jnp.transpose(ids).astype(jnp.int32)
+    r.small[48:128, :] = jnp.zeros((80, D), f32)
+    pack_share.wait()
+    for pair in range(4):
+        sides = [r.packs[2 * pair + k, 64:112, :].astype(f32) for k in range(2)]
+        both = jnp.where(lanes_of((48, 128)) < 64, sides[0], pltpu.roll(sides[1], 64, 1))
+        r.small[0:48, pair * 128 : pair * 128 + 128] = both
+    keyval_weight = r.packs[:, 0:64, :].reshape(D, 128)
     shaped = (r.flow[...] * r.small[32:33, :] + r.small[33:34, :]).astype(bf16)
     r.acted[...] = shaped
-    sides = product(shaped, r.packed[...])
-    keyval_view(ctx)[...] = sides[:, 0:128].astype(bf16)
+    keyval_view(ctx)[...] = product(shaped, keyval_weight).astype(bf16)
     keyval_sends = direct_send(keyval_view(ctx), r.direct_sems.at[0], r.direct_recvs.at[0], length)
     for copy in keyval_sends:
         copy.start()
-
-    id_lanes = [r.head_ids[:, j : j + 1] for j in range(MOA_TOP)]
+    query_gather.relay()
+
+    id_lanes = [r.id_columns[:, j : j + 1] for j in range(MOA_TOP)]
+    choice = product(shaped, r.small[...].astype(bf16), ((1,), (1,)))
     logits = [
-        jnp.sum(jnp.where(lane == id_lanes[j], sides[:, 128:256], 0.0), -1, keepdims=True)
+        jnp.sum(jnp.where(lane == id_lanes[j], choice, 0.0), -1, keepdims=True)
         for j in range(MOA_TOP)
     ]
     peak = jnp.maximum(jnp.maximum(logits[0], logits[1]), jnp.maximum(logits[2], logits[3]))
@@ -675,9 +749,10 @@
         jnp.where(lane == 1, gates[1], jnp.where(lane == 2, gates[2], gates[3])),
     )
 
-    query_gather.relay()
-    project_gather.start()
+    query_gather.relay_rest()
+    project_gather.relay()
     inner_gather.start()
+    outer_gathers[0].start()
     query_gather.finish()
     for part in range(6):
         columns = slice(part * 256, part * 256 + 256)
@@ -697,6 +772,7 @@
             jnp.where(low_half, folded, 0.0) * HS ** (-0.5)
         ).astype(bf16)
 
+    project_gather.relay_rest()
     direct_wait(keyval_view, r.direct_sems.at[0], r.direct_recvs.at[0], length)
     chunk = 256
 
@@ -711,7 +787,6 @@
         return carried
 
     lax.fori_loop(0, MOA_TOP * tokens // chunk, attend, 0)
-    project_gather.relay()
 
     spread = []
     for j in range(MOA_TOP):
@@ -740,16 +815,9 @@
     for copy in route_sends:
         copy.start()
 
-    def selection(source, expert):
-        row = r.routes[source, pl.ds(EXP_DEV * ctx + expert, 1), :]
-        return rows_of((CAP, tokens)).astype(f32) == row
-
-    def slots(source):
-        return pl.ds(pl.multiple_of(source * CAP, CAP), CAP)
-
     def first_half(source):
         def one(expert, carried):
-            chosen = selection(source, expert).astype(f32).astype(bf16)
+            chosen = picks(r, source, expert).astype(bf16)
             rows = product(chosen, r.entering[source]).astype(bf16)
             r.slot_rows[expert, slots(source), :] = rows
 
@@ -765,64 +833,28 @@
 
         lax.fori_loop(0, EXP_DEV, one, 0)
 
-    inner_gather.relay()
-    outer_gather.start()
-    direct_wait(lambda b: r.routes.at[b], r.direct_sems.at[1], r.direct_recvs.at[1], length)
-    entering_gather.relay(1)
-    inner_gather.relay_rest()
-    inner_gather.finish()
-
-    def step_of(step, carried):
-        for ahead in range(2, length):
-
-            @pl.when(step == ahead - 1)
-            def _():
-                entering_gather.relay(ahead)
-                if ahead < length - 1:
-                    pass
-
-        @pl.when(step == length - 2)
-        def _():
-            cot_gather.relay(2)
-
-        @pl.when(step == length - 1)
-        def _():
-            outer_gather.relay()
-
-        before_me = ctx - step >= 0
-        after_me = jnp.logical_and(ctx + step < length, step > 0)
-        count = before_me.astype(jnp.int32) + after_me.astype(jnp.int32)
-
-        def visit(turn, kept):
-            source = jnp.where(jnp.logical_and(turn == 0, before_me), ctx - step, ctx + step)
-            first_half(source)
-            return kept
-
-        lax.fori_loop(0, count, visit, 0)
-        return carried
-
-    lax.fori_loop(0, length, step_of, 0)
-    outer_gather.relay_rest()
-    cot_gather.relay(length - 1)
-    outer_gather.finish()
-
-    def second_half(turn, carried):
-        expert, part = turn // 2, turn % 2
-        rows = pl.ds(pl.multiple_of(part * 384, 384), 384)
-        r.result[expert, rows, :] = product(r.active[expert, rows, :], r.outer[expert]).astype(bf16)
-        return carried
-
-    lax.fori_loop(0, 2 * EXP_DEV, second_half, 0)
+    def second_half(first, count):
+        rows = pl.ds(pl.multiple_of(first * CAP, CAP), count * CAP)
+
+        def one(expert, carried):
+            value = product(r.active[expert, rows, :], r.outer[expert])
+            r.result[expert, rows, :] = value.astype(bf16)
+            return carried
+
+        lax.fori_loop(0, EXP_DEV, one, 0)
 
     def score(source, carried):
         lines = []
         for expert in range(EXP_DEV):
-            chosen = selection(source, expert).astype(f32)
+            chosen = picks(r, source, expert)
             cot_rows = product(chosen.astype(bf16), r.cots[source]).astype(bf16)
             r.slot_cot[expert, slots(source), :] = cot_rows
             rows = r.result[expert, slots(source), :].astype(f32)
             toward = jnp.sum(rows * r.small[36:37, :], -1, keepdims=True)
             against = jnp.sum(rows * cot_rows.astype(f32), -1, keepdims=True)
+            gate_row = r.routes[source, pl.ds(8 + EXP_DEV * ctx + expert, 1), :]
+            gate = jnp.sum(chosen * gate_row, -1, keepdims=True)
+            r.result[expert, slots(source), :] = (rows * gate).astype(bf16)
             lines.append(jnp.sum(chosen * toward, 0, keepdims=True))
             lines.append(jnp.sum(chosen * against, 0, keepdims=True))
         lines.append(jnp.zeros((8 - 2 * EXP_DEV, tokens), f32))
@@ -846,7 +878,52 @@
 
         return carried
 
-    lax.fori_loop(0, length, score, 0)
+    lower = ctx < length // 2
+    last = jnp.where(lower, length - 1, 0)
+    at_end = jnp.logical_or(ctx == 0, ctx == length - 1)
+
+    def arrival(turn):
+        along = jnp.where(lower, turn, length - 1 - turn)
+        around = jnp.where(turn == 0, ctx, jnp.where(turn == 1, ctx - 1, ctx + 1))
+        return jnp.where(at_end, along, around)
+
+    inner_gather.relay()
+    outer_gathers[1].start()
+    direct_wait(lambda b: r.routes.at[b], r.direct_sems.at[1], r.direct_recvs.at[1], length)
+    entering_gather.relay(1)
+    inner_gather.relay_rest()
+    inner_gather.finish()
+    outer_gathers[0].relay()
+
+    def near(turn, carried):
+        @pl.when(turn == 1)
+        def _():
+            entering_gather.relay(2)
+            cot_gather.relay(2)
+
+        @pl.when(turn == 2)
+        def _():
+            outer_gathers[1].relay()
+            outer_gathers[0].relay_rest()
+
+        first_half(arrival(turn))
+        return carried
+
+    lax.fori_loop(0, length - 1, near, 0)
+    outer_gathers[1].relay_rest()
+    for item in outer_gathers:
+        item.finish()
+    second_half(jnp.where(lower, 0, 1), length - 1)
+    lax.fori_loop(0, length - 1, lambda turn, carried: score(arrival(turn), carried), 0)
+    entering_gather.relay(length - 1)
+    first_half(last)
+    second_half(last, 1)
+    cot_gather.relay(length - 1)
+    score(last, 0)
+    cot_gather.drain()
+    mixed, unused = returns(length, r)
+    for index in range(2):
+        give_back(length, r, mixed.far + index)
     direct_wait(lambda b: r.scores_back.at[b], r.direct_sems.at[2], r.direct_recvs.at[2], length)
     for step in range(1, length):
         target = moved(me, step, length)
@@ -859,10 +936,67 @@
         ).wait_send()
     for copy in keyval_sends + route_sends:
         copy.wait_send()
-    for item in (pack_gather, query_gather, project_gather, inner_gather, outer_gather):
+    for copy in pack_sends:
+        copy.wait_send()
+    for item in (query_gather, project_gather, inner_gather, *outer_gathers):
         item.drain()
-    cot_gather.drain()
     entering_gather.drain()
+
+
+class LineReturn:
+    def __init__(self, length, parts, arrived, send, recv):
+        self.length, self.parts, self.arrived = length, parts, arrived
+        self.send, self.recv = send, recv
+        self.me = places()[0]
+        ctx = self.me[0]
+        self.at_end = jnp.logical_or(ctx == 0, ctx == length - 1)
+        self.inside = jnp.logical_not(self.at_end)
+        self.next = (ctx + 1 - 2 * (ctx % 2), self.me[1], self.me[2])
+        self.far = (1 - ctx // 2) * 2
+
+    def copy(self, block, place, slot, device):
+        return remote(
+            self.parts.at[block], self.arrived.at[place], self.send.at[slot], self.recv.at[slot], device
+        )
+
+    def hand(self, index):
+        return self.copy(self.far + index, index, index, self.next)
+
+    def near(self):
+        return self.copy(self.next[0], 2, 2, self.next)
+
+    def across(self, index):
+        block = self.far + index
+        return self.copy(block, 3, 3 + index, (block, self.me[1], self.me[2]))
+
+    def start_far(self, index):
+        pl.when(self.at_end)(lambda: self.hand(index).start())
+
+    def pass_on(self, index):
+        @pl.when(self.inside)
+        def _():
+            self.hand(index).wait_recv()
+            block = self.far + index
+            both = self.parts[block].astype(jnp.float32) + self.arrived[index].astype(jnp.float32)
+            self.parts[block] = both.astype(jnp.bfloat16)
+            self.across(index).start()
+
+    def start_near(self):
+        self.near().start()
+
+    def wait(self):
+        self.near().wait_recv()
+        self.across(self.me[0] % 2).wait_recv()
+
+    def total(self):
+        own = self.parts[self.me[0]].astype(jnp.float32)
+        return own + self.arrived[2].astype(jnp.float32) + self.arrived[3].astype(jnp.float32)
+
+    def drain(self):
+        self.near().wait_send()
+        for index in range(2):
+            pl.when(self.at_end)(lambda i=index: self.hand(i).wait_send())
+            pl.when(self.inside)(lambda i=index: self.across(i).wait_send())
 
 
 class PlaneReduce:
@@ -1068,18 +1202,10 @@
     lane = lanes_of((tokens, 128))
     low_half = lane < HS
     side = lane // HS
-    id_lanes = [r.head_ids[:, j : j + 1] for j in range(MOA_TOP)]
+    id_lanes = [r.id_columns[:, j : j + 1] for j in range(MOA_TOP)]
 
     def sems(row):
         return r.direct_sems.at[row], r.direct_recvs.at[row]
-
-    def slots(source):
-        return pl.ds(pl.multiple_of(source * CAP, CAP), CAP)
-
-    def to_owner(view, target_ref, row, block):
-        slot = (block - ctx + length) % length - 1
-        send, recv = sems(row)
-        return remote(view, target_ref.at[slot], send.at[slot], recv.at[slot], (block, me[1], me[2]))
 
     def from_all(target_ref, row):
         send, recv = sems(row)
@@ -1091,7 +1217,7 @@
     def sent_all(view_of, target_ref, row):
         for step in range(1, length):
             block = moved(me, step, length)[0]
-            to_owner(view_of(block), target_ref, row, block).wait_send()
+            to_owner(length, r, view_of(block), target_ref, row, block).wait_send()
 
     r.gsmall[...] = jnp.zeros_like(r.gsmall)
     mid = r.middle[...]
@@ -1119,6 +1245,9 @@
     factor_sends = direct_send(r.factors.at[ctx], *sems(3), length)
     for copy in factor_sends:
         copy.start()
+    mixed, backs = returns(length, r)
+    for index in range(2):
+        mixed.start_far(index)
     r.columns[...] = jnp.transpose(jnp.concatenate([sheet, jnp.zeros((120, tokens), f32)], 0))
     gate_grad = (1.0 - stopped) * against + halt_grad * toward
     pick_grad = gates * (gate_grad - jnp.sum(gates * gate_grad, 0, keepdims=True))
@@ -1128,78 +1257,82 @@
     r.gsmall[24:32, :] = sums[0:8] + sums[8:16]
     keep_col, halt_col = r.columns[:, 0:1], r.columns[:, 1:2]
     r.flow[...] = keep_col * cot + halt_col * halt_row
+    r.grad_states[...] = r.columns[:, 2:3] * cot
     r.gsmall[36:37, :] = jnp.sum(halt_col * mid, 0, keepdims=True)
 
-    def picks(block, expert):
-        row = r.routes[block, pl.ds(EXP_DEV * ctx + expert, 1), :]
-        return (rows_of((CAP, tokens)).astype(f32) == row).astype(f32)
-
-    def block_back(turn, carried):
-        offset = jnp.where(turn == 0, 0, jnp.where(turn == length - 1, 1, turn + 1))
-        block = (ctx + offset) % length
-
-        @pl.when(turn > 0)
+    def rows_back(block):
+        @pl.when(block != ctx)
         def _():
             slot = (ctx - block + length) % length - 1
             view = r.factors.at[block]
             send, recv = sems(3)
             remote(view, view, send.at[slot], recv.at[slot], (block, me[1], me[2])).wait_recv()
 
-        def one(expert, kept):
-            chosen = picks(block, expert)
+        for expert in range(EXP_DEV):
+            chosen = picks(r, block, expert)
             keep = jnp.sum(chosen * r.factors[block, 0:1, :], -1, keepdims=True)
             halt = jnp.sum(chosen * r.factors[block, 1:2, :], -1, keepdims=True)
-            gate = jnp.sum(
-                chosen * r.routes[block, pl.ds(8 + EXP_DEV * ctx + expert, 1), :], -1, keepdims=True
-            )
-            rows = r.result[expert, slots(block), :].astype(f32) * gate
+            gate_row = r.routes[block, pl.ds(8 + EXP_DEV * ctx + expert, 1), :]
+            gate = jnp.sum(chosen * gate_row, -1, keepdims=True)
+            rows = r.result[expert, slots(block), :].astype(f32)
             r.gsmall[36:37, :] += jnp.sum(halt * rows, 0, keepdims=True)
-            r.result[expert, slots(block), :] = rows.astype(bf16)
             incoming = r.slot_cot[expert, slots(block), :].astype(f32)
             rows_grad = (gate * (keep * incoming + halt * halt_row)).astype(bf16)
             r.slot_cot[expert, slots(block), :] = rows_grad
 
+    side_blocks = length // 2
+    side_rows = side_blocks * CAP
+
+    def side_back(turn, carried):
+        half = jnp.where(turn == 0, 1 - ctx // side_blocks, ctx // side_blocks)
+
+        def prepare(index, kept):
+            rows_back(half * side_blocks + index)
+            return kept
+
+        lax.fori_loop(0, side_blocks, prepare, 0)
+        rows = pl.ds(pl.multiple_of(half * side_rows, side_rows), side_rows)
+
+        def one(expert, kept):
             def part(index, inside):
                 columns = pl.ds(pl.multiple_of(index * 512, 512), 512)
-                back = product(rows_grad, r.outer[expert, columns, :], ((1,), (1,)))
-                slope = r.slope[expert, slots(block), columns].astype(f32)
-                r.slope[expert, slots(block), columns] = (back * slope).astype(bf16)
+                back = product(r.slot_cot[expert, rows, :], r.outer[expert, columns, :], ((1,), (1,)))
+                slope = r.slope[expert, rows, columns].astype(f32)
+                r.slope[expert, rows, columns] = (back * slope).astype(bf16)
                 return inside
 
             lax.fori_loop(0, 4, part, 0)
-            sent = product(r.slope[expert, slots(block), :], r.inner[expert], ((1,), (1,)))
+            sent = product(r.slope[expert, rows, :], r.inner[expert], ((1,), (1,)))
             r.slot_back[expert] = sent.astype(bf16)
             return kept
 
         lax.fori_loop(0, EXP_DEV, one, 0)
-        spread = product(picks(block, 0).astype(bf16), r.slot_back[0], ((0,), (0,)))
-        spread = spread + product(picks(block, 1).astype(bf16), r.slot_back[1], ((0,), (0,)))
-        r.entering[block] = spread.astype(bf16)
-
-        @pl.when(turn > 0)
+
+        def send(index, kept):
+            block = half * side_blocks + index
+            total = 0.0
+            for expert in range(EXP_DEV):
+                chosen = picks(r, block, expert).astype(bf16)
+                total = total + product(chosen, r.slot_back[expert, slots(index), :], ((0,), (0,)))
+            r.entering[block] = total.astype(bf16)
+            return kept
+
+        lax.fori_loop(0, side_blocks, send, 0)
+
+        @pl.when(turn == 0)
         def _():
-            to_owner(r.entering.at[block], r.back_in, 4, block).start()
+            for index in range(2):
+                backs.start_far(index)
+            mixed.pass_on(0)
 
         return carried
 
-    lax.fori_loop(0, length, block_back, 0)
-
-    def block_forward(turn, carried):
-        offset = jnp.where(turn == 0, 0, jnp.where(turn == length - 1, 1, turn + 1))
-        block = (ctx + offset) % length
-        spread = product(picks(block, 0).astype(bf16), r.result[0, slots(block), :], ((0,), (0,)))
-        spread = spread + product(
-            picks(block, 1).astype(bf16), r.result[1, slots(block), :], ((0,), (0,))
-        )
-        r.cots[block] = spread.astype(bf16)
-
-        @pl.when(turn > 0)
-        def _():
-            to_owner(r.cots.at[block], r.mix_in, 5, block).start()
-
-        return carried
-
-    lax.fori_loop(0, length, block_forward, 0)
+    lax.fori_loop(0, 2, side_back, 0)
+    backs.start_near()
+    mixed.pass_on(1)
+    give_back(length, r, backs.next[0])
+    mixed.start_near()
+    give_back(length, r, ctx)
 
     experts = ExpertReduce(
         r.inner, r.outer, r.half_in, r.half_out, r.side_in, r.side_out, r.last_in, r.last_out,
@@ -1215,6 +1348,7 @@
 
     lax.fori_loop(0, 4 * EXP_DEV, outer_grad, 0)
     experts.start(1)
+    backs.pass_on(0)
 
     def inner_grad(turn, carried):
         expert, part = turn // 4, turn % 4
@@ -1226,15 +1360,14 @@
     lax.fori_loop(0, 4 * EXP_DEV, inner_grad, 0)
     experts.start(0)
     experts.add_halves(1)
+    backs.pass_on(1)
     experts.add_halves(0)
 
-    from_all(r.back_in, 4)
+    backs.wait()
     mid = r.middle[...]
     selector = r.small[24:32, :]
     double = jnp.concatenate([selector, selector], 0).astype(bf16)
-    back = product(r.pick_grads[...], double, ((0,), (0,))) + r.entering[ctx].astype(f32)
-    for step in range(length - 1):
-        back = back + r.back_in[step].astype(f32)
+    back = product(r.pick_grads[...], double, ((0,), (0,))) + backs.total()
     centred = mid - jnp.mean(mid, -1, keepdims=True)
     inverse = lax.rsqrt(jnp.mean(centred * centred, -1, keepdims=True) + EPS)
     plain = centred * inverse
@@ -1290,26 +1423,44 @@
     sums = product(coarse, r.acted[...], ((0,), (0,))) + product(fine, r.acted[...], ((0,), (0,)))
     r.gsmall[0:24, :] = sums[0:24]
     chooser = r.small[...].astype(bf16)
-    r.acted_grad[...] = product(coarse, chooser) + product(fine, chooser)
+    r.cotangent[...] = product(coarse, chooser) + product(fine, chooser)
     project_reduce.add_halves()
-    experts.add_sides(1)
-    experts.add_sides(0)
 
     r.kv_grad[...] = jnp.zeros_like(r.kv_grad)
     chunk = 256
 
+    half_keys = length * tokens // 2
+
     def attend_back(turn, carried):
-        rows = pl.ds(pl.multiple_of(turn * chunk, chunk), chunk)
-        query, grads, keyval = r.queries[rows, :], r.heads_grad[rows, :], r.keyval[...]
+        @pl.when(turn == 4)
+        def _():
+            experts.add_sides(1)
+
+        @pl.when(turn == 8)
+        def _():
+            experts.add_sides(0)
+
+        rows = pl.ds(pl.multiple_of((turn // 2) * chunk, chunk), chunk)
+        keys = pl.ds(pl.multiple_of((turn % 2) * half_keys, half_keys), half_keys)
+        query, grads, keyval = r.queries[rows, :], r.heads_grad[rows, :], r.keyval[keys, :]
         scores = product(keyval, query, ((1,), (1,)))
         weights = jnp.exp(scores - r.stats[0:1, rows])
         upward = product(keyval, grads, ((1,), (1,)))
         score_grad = (weights * (upward - r.stats[1:2, rows])).astype(bf16)
-        r.kv_grad[...] += product(score_grad, query) + product(weights.astype(bf16), grads)
-        r.heads[rows, :] = product(score_grad, keyval, ((0,), (0,))) * HS ** (-0.5)
+        r.kv_grad[keys, :] += product(score_grad, query) + product(weights.astype(bf16), grads)
+        down = product(score_grad, keyval, ((0,), (0,))) * HS ** (-0.5)
+
+        @pl.when(turn % 2 == 0)
+        def _():
+            r.heads[rows, :] = down
+
+        @pl.when(turn % 2 == 1)
+        def _():
+            r.heads[rows, :] += down
+
         return carried
 
-    lax.fori_loop(0, MOA_TOP * tokens // chunk, attend_back, 0)
+    lax.fori_loop(0, 2 * MOA_TOP * tokens // chunk, attend_back, 0)
 
     def send_keyval(turn, carried):
         block = (ctx + turn) % length
@@ -1318,7 +1469,7 @@
         @pl.when(turn > 0)
         def _():
             r.heads_grad[rows, :] = r.kv_grad[rows, :].astype(bf16)
-            to_owner(r.heads_grad.at[rows, :], r.kv_in, 6, block).start()
+            to_owner(length, r, r.heads_grad.at[rows, :], r.kv_in, 6, block).start()
 
         return carried
 
@@ -1346,7 +1497,7 @@
 
     query_reduce = reducer(1, wide_piece(0, 1536), 64, r.query_half, r.query_in)
     query_reduce.start()
-    r.acted_grad[...] += product(r.mixture[...], r.query[...], ((1,), (1,)))
+    r.cotangent[...] += product(r.mixture[...], r.query[...], ((1,), (1,)))
     project_line = LineSum(length, r.project_value, r.project_parts, r.project_sum, sems(7), sems(8))
     project_line.start(project_reduce.total())
     query_reduce.add_halves()
@@ -1357,7 +1508,7 @@
     for step in range(length - 1):
         keyval_grad = keyval_grad + r.kv_in[step].astype(f32)
     keyval_grad = keyval_grad.astype(bf16)
-    back = r.acted_grad[...] + product(keyval_grad, r.packed[:, 0:128], ((1,), (1,)))
+    back = r.cotangent[...] + product(keyval_grad, r.packs[:, 0:64, :].reshape(D, 128), ((1,), (1,)))
     values = r.states[...].astype(f32)
     centred = values - jnp.mean(values, -1, keepdims=True)
     inverse = lax.rsqrt(jnp.mean(centred * centred, -1, keepdims=True) + EPS)
@@ -1372,7 +1523,7 @@
     level = jnp.mean(scaled, -1, keepdims=True)
     tilt = jnp.mean(scaled * plain, -1, keepdims=True)
     r.grad_states[...] = (
-        r.flow[...] + inverse * (scaled - level - plain * tilt) + r.columns[:, 2:3] * r.cotangent[...]
+        r.grad_states[...] + r.flow[...] + inverse * (scaled - level - plain * tilt)
     )
     small_reduce.add_halves()
     project_line.share_out()
@@ -1383,10 +1534,8 @@
 
     experts.total(1, r.grad_outer)
     experts.total(0, r.grad_inner)
-    from_all(r.mix_in, 5)
-    final = r.middle[...] + r.cots[ctx].astype(f32)
-    for step in range(length - 1):
-        final = final + r.mix_in[step].astype(f32)
+    mixed.wait()
+    final = r.middle[...] + mixed.total()
     r.new_states[...] = (
         r.columns[:, 2:3] * r.states[...].astype(f32) + r.columns[:, 0:1] * final
     ).astype(bf16)
@@ -1398,8 +1547,8 @@
 
     for copy in factor_sends:
         copy.wait_send()
-    sent_all(lambda b: r.entering.at[b], r.back_in, 4)
-    sent_all(lambda b: r.cots.at[b], r.mix_in, 5)
+    mixed.drain()
+    backs.drain()
     sent_all(
         lambda b: r.heads_grad.at[pl.ds(pl.multiple_of(b * tokens, tokens), tokens), :], r.kv_in, 6
     )
@@ -1413,6 +1562,56 @@
     r = SimpleNamespace(**dict(zip(names, refs)))
     forward_part(length, r)
     backward_part(length, r)
+
+
+def write_kernel(
+    new_states, rows_out, grad_states, grad_query, grad_project, grad_small, grad_inner, grad_outer, *outs
+):
+    f32 = jnp.float32
+    outs[0][0] = new_states[...]
+    outs[1][...] = rows_out[0:1, :]
+    outs[2][0] = grad_states[...]
+    outs[3][...] = rows_out[1:2, :]
+    outs[4][...] = grad_query[...].astype(f32)
+    outs[5][...] = grad_small[:, 0:128].astype(f32)
+    outs[6][...] = grad_project[...].astype(f32)
+    turned = jnp.transpose(grad_small[:, 128:256].astype(f32))
+    outs[7][...] = turned[0:24]
+    outs[8][...] = turned[24:32]
+    for index in range(5):
+        outs[9 + index][...] = turned[32 + index : 33 + index]
+    outs[14][...] = grad_inner[...].astype(f32)
+    outs[15][...] = grad_outer[...].astype(f32)
+
+
+def write_out(tokens, *results):
+    f32, bf16 = jnp.float32, jnp.bfloat16
+    shape = jax.ShapeDtypeStruct
+    outs = (
+        shape((1, tokens, D), bf16),
+        shape((1, tokens), f32),
+        shape((1, tokens, D), f32),
+        shape((1, tokens), f32),
+        shape((64, MOA_EXPERTS * HS), f32),
+        shape((64, 128), f32),
+        shape((192, D), f32),
+        shape((MOA_EXPERTS, 64), f32),
+        shape((8, 64), f32),
+        *[shape((1, 64), f32)] * 5,
+        shape((EXP_DEV, 64, FF), f32),
+        shape((EXP_DEV, 256, D), f32),
+    )
+    in_vmem = pl.BlockSpec(memory_space=pltpu.VMEM)
+    final = pl.pallas_call(
+        write_kernel,
+        out_shape=outs,
+        in_specs=[in_vmem] * len(results),
+        out_specs=[in_vmem] * len(outs),
+        compiler_params=pltpu.CompilerParams(vmem_limit_bytes=LIMIT_MIB * 2**20),
+        name="write_out",
+    )(*results)
+    vectors = [item.reshape(64) for item in final[9:14]]
+    return (*final[0:7], final[7].T, final[8].T, *vectors, *final[14:16])
 
 
 def fast_body(
@@ -1440,24 +1639,27 @@
     tokens = states.shape[1]
     rows = length * CAP
     wide = MOA_EXPERTS * HS
-    flat = jnp.stack([gain_one, bias_one, gain_two, bias_two, halt_weight], 1)
-    pack = jnp.concatenate(
-        [keyval_weight, chooser, selector, flat, jnp.zeros((flat.shape[0], 91), bf16)], 1
+    nothing = jnp.zeros_like(gain_one)
+    vectors = jnp.stack(
+        [gain_one, bias_one, gain_two, bias_two, halt_weight, nothing, nothing, nothing], 0
     )
     inputs = dict(
         states=states[0],
-        cotangent=out_cotangent[0],
-        head_ids=moa_ids[0],
-        route_ids=ffn_ids[0],
+        cotangent_part=out_cotangent[0],
+        head_ids=moa_ids[0].T,
+        route_ids=ffn_ids[0].T,
         remaining=remaining,
         left_cot=left_cotangent,
-        pack=pack,
+        keyval_part=keyval_weight,
+        chooser_part=chooser.T,
+        selector_part=selector.T,
+        vectors=vectors,
         query_part=query_weight,
         project_part=project_weight,
         inner_part=expert_in,
         outer_part=expert_out,
     )
-    in_place = ("query_part", "project_part", "inner_part", "outer_part")
+    in_place = ("cotangent_part", "query_part", "project_part", "inner_part", "outer_part")
     shape = jax.ShapeDtypeStruct
     outputs = dict(
         new_states=shape((tokens, D), bf16),
@@ -1480,7 +1682,9 @@
         outer=vmem((EXP_DEV, FF, D), bf16),
         query=vmem((D, wide), bf16),
         project=vmem((wide, D), bf16),
-        packed=vmem((D, 256), bf16),
+        packs=vmem((8, 112, 128), bf16),
+        id_columns=vmem((tokens, 128), jnp.int32),
+        cotangent=vmem((tokens, D), f32),
         acted=vmem((tokens, D), bf16),
         mixture=vmem((tokens, wide), bf16),
         queries=vmem((MOA_TOP * tokens, 128), bf16),
@@ -1499,9 +1703,9 @@
         pick_grads=vmem((16, tokens), bf16),
         gsmall=vmem((128, D), f32),
         flow=vmem((tokens, D), f32),
-        slot_back=vmem((EXP_DEV, CAP, D), bf16),
-        back_in=vmem((length - 1, tokens, D), bf16),
-        mix_in=vmem((length - 1, tokens, D), bf16),
+        slot_back=vmem((EXP_DEV, rows // 2, D), bf16),
+        back_in=vmem((4, tokens, D), bf16),
+        mix_in=vmem((4, tokens, D), bf16),
         half_in=vmem((2, EXP_DEV, 128, FF), bf16),
         half_out=vmem((2, EXP_DEV, 512, D), bf16),
         side_in=vmem((EXP_DEV, 128, FF), bf16),
@@ -1510,7 +1714,6 @@
         last_out=vmem((EXP_DEV, 256, D), bf16),
         heads_grad=vmem((MOA_TOP * tokens, 128), bf16),
         stats=vmem((8, MOA_TOP * tokens), f32),
-        acted_grad=vmem((tokens, D), f32),
         kv_grad=vmem((length * tokens, 128), f32),
         kv_in=vmem((length - 1, tokens, 128), bf16),
         project_half=vmem((2, 384, D), bf16),
@@ -1528,13 +1731,17 @@
         small_value=vmem((64, 256), bf16),
         small_parts=vmem((length - 1, 64 // length, 256), bf16),
         small_sum=vmem((64, 256), bf16),
+        pack_send=dma((7,)),
+        pack_recv=dma((7,)),
         plane_send=dma((5, 9)),
         plane_recv=dma((5, 9)),
-        plane_local=dma((5,)),
+        plane_local=dma((6,)),
         line_send=dma((2, 2, length)),
         line_recv=dma((2, 2, length)),
         direct_sems=dma((13, length)),
         direct_recvs=dma((13, length)),
+        return_send=dma((2, 5)),
+        return_recv=dma((2, 5)),
         expert_send=dma((9,)),
         expert_recv=dma((9,)),
         dense_send=dma((3, 5)),
@@ -1554,26 +1761,7 @@
         ),
         name="layer_step",
     )(*inputs.values())
-    o = SimpleNamespace(**dict(zip(outputs, results)))
-    small = o.grad_small.astype(f32)
-    return (
-        o.new_states[None],
-        o.rows_out[0:1],
-        o.grad_states[None],
-        o.rows_out[1:2],
-        o.grad_query.astype(f32),
-        small[:, 0:128],
-        o.grad_project.astype(f32),
-        small[:, 128:152],
-        small[:, 152:160],
-        small[:, 160],
-        small[:, 161],
-        small[:, 162],
-        small[:, 163],
-        small[:, 164],
-        o.grad_inner.astype(f32),
-        o.grad_outer.astype(f32),
-    )
+    return write_out(tokens, *results)
 
 
 def solution(mesh):

time: 226 us -> 194 us (0.86)
  local copies, waits for them, and re-layouts: 16.6 us -> 1.27 us
  Pallas kernels: 204 us -> 192 us
  other arithmetic: 4.55 us -> 0 us
    pallas_call x1, Pallas kernels: 204 us -> 188 us  [fast_body(): pl.pallas_call(partial(whole_kernel, length, names), out_shape=tuple(outp...]
    unnamed x38 -> x10, local copies, waits for them, and re-layouts: 10.3 us -> 0.66 us
    slice x5 -> x0, local copies, waits for them, and re-layouts: 4.99 us -> none  [the longest x1 1.35 us: fast_body(): o.rows_out[1:2]]
    convert_element_type x5 -> x0, other arithmetic: 4.55 us -> none  [the longest x1 1.1 us: fast_body(): o.grad_outer.astype(f32)]
    pallas_call x0 -> x1, Pallas kernels: none -> 3.87 us  [write_out(): pl.pallas_call(write_kernel, out_shape=outs, in_specs=[in_vmem] * len(res...]
where the time goes in v3:
time: 194 us
  Pallas kernels  192 us (99%)
    pallas_call x1, Pallas kernels, fast_body(): pl.pallas_call(partial(whole_kernel, length, names), out_shape=tuple(outp...  188 us

profile of v3, /device:TPU:0, one launch (start us, length us, event | category | flops | bytes accessed | tf_op | source)
XLA Modules:
  0.0 194.1 jit_solution(3421966447731122310)
XLA Ops:
  0.6 0.0 copy-start.3
  0.7 0.0 copy-start.4
  0.7 0.0 copy-start
  0.7 0.0 copy-start.1
  0.7 0.0 copy-start.2
  0.7 0.6 copy-done.3
  1.3 0.0 copy-done.4
  1.3 0.0 copy-done
  1.3 0.0 copy-done.1
  1.4 0.0 copy-done.2
  1.4 0.6 stack.27.refs_9_
  2.0 188.3 %layer_step.1 = (bf16[384,512]{1,0:T(8,128)(2,1)}, f32[8,384]{1,0:T(8,128)}, f32[384,512]{1,0:T(8,128)}, bf16[64,1536]{1,0:T(8,128)(2,1)}, bf16[192,512]{1,0:T(8...) custom-call(bf16[384,512]{1,0:T(8,128)(2,1)} %bitcast.23, ...), custom_call_target="tpu_custom_call" | custom-call | tf_op jit(solution)/shard_map/layer_step/pallas_call | solution.py:1753
  190.2 3.9 %write_out.1 = (bf16[1,384,512]{2,1,0:T(8,128)(2,1)}, f32[1,384]{1,0:T(1,128)}, f32[1,384,512]{2,1,0:T(8,128)}, f32[1,384]{1,0:T(1,128)}, f32[64,1536]{1,0:T(8,1...) custom-call(bf16[384,512]{1,0:T(8,128)(2,1)} %get-tuple-element.40.n, ...), custom_call_target="tpu_custom_call" | custom-call | tf_op jit(solution)/shard_map/write_out/pallas_call | solution.py:1605
  (2 shorter events, 0.0 us)
Async XLA Ops:
  0.6 0.7 copy-start.3
  0.7 0.7 copy-start.4
  0.7 0.7 copy-start
  0.7 0.7 copy-start.1
  0.7 0.7 copy-start.2

commit v4 on v3

--- a/solution.py
+++ b/solution.py
@@ -392,7 +392,7 @@
 
 MESH = pl.DeviceIdType.MESH
 CAP = 192
-LIMIT_MIB = 63
+LIMIT_MIB = 62
 KEEP = 0.7071067811865476
 SPREAD = 0.3989422804014327
 ERF_P = 0.3275911
@@ -705,7 +705,7 @@
     values = r.states[...].astype(f32)
     centred = values - jnp.mean(values, -1, keepdims=True)
     inverse = lax.rsqrt(jnp.mean(centred * centred, -1, keepdims=True) + EPS)
-    r.flow[...] = centred * inverse
+    r.grad_states[...] = centred * inverse
 
     lane = lanes_of((tokens, 128))
     turned = r.route_ids[...].astype(f32)
@@ -725,7 +725,7 @@
         both = jnp.where(lanes_of((48, 128)) < 64, sides[0], pltpu.roll(sides[1], 64, 1))
         r.small[0:48, pair * 128 : pair * 128 + 128] = both
     keyval_weight = r.packs[:, 0:64, :].reshape(D, 128)
-    shaped = (r.flow[...] * r.small[32:33, :] + r.small[33:34, :]).astype(bf16)
+    shaped = (r.grad_states[...] * r.small[32:33, :] + r.small[33:34, :]).astype(bf16)
     r.acted[...] = shaped
     keyval_view(ctx)[...] = product(shaped, keyval_weight).astype(bf16)
     keyval_sends = direct_send(keyval_view(ctx), r.direct_sems.at[0], r.direct_recvs.at[0], length)
@@ -743,10 +743,10 @@
     powers = [jnp.exp(item - peak) for item in logits]
     total = powers[0] + powers[1] + powers[2] + powers[3]
     gates = [item / total for item in powers]
-    r.head_gates[...] = jnp.where(
-        lane == 0,
+    r.columns[...] = jnp.where(
+        lane == 8,
         gates[0],
-        jnp.where(lane == 1, gates[1], jnp.where(lane == 2, gates[2], gates[3])),
+        jnp.where(lane == 9, gates[1], jnp.where(lane == 10, gates[2], gates[3])),
     )
 
     query_gather.relay_rest()
@@ -792,7 +792,7 @@
     for j in range(MOA_TOP):
         head = r.heads[j * tokens : (j + 1) * tokens, :]
         both = jnp.where(low_half, pltpu.roll(head, HS, 1), head)
-        spread.append(both * r.head_gates[:, j : j + 1])
+        spread.append(both * r.columns[:, 8 + j : 9 + j])
     for pair in range(MOA_EXPERTS // 2):
         block = jnp.zeros((tokens, 128), f32)
         for j in range(MOA_TOP):
@@ -802,6 +802,8 @@
     project_gather.finish()
     between = r.states[...].astype(f32) + product(r.mixture[...], r.project[...])
     r.middle[...] = between
+    reach = jnp.sum(between * r.small[36:37, :], -1, keepdims=True)
+    gap = jnp.sum(r.cotangent[...] * (r.states[...].astype(f32) - between), -1, keepdims=True)
     centred = between - jnp.mean(between, -1, keepdims=True)
     inverse = lax.rsqrt(jnp.mean(centred * centred, -1, keepdims=True) + EPS)
     entry = (centred * inverse * r.small[34:35, :] + r.small[35:36, :]).astype(bf16)
@@ -811,6 +813,9 @@
     peak = jnp.max(jnp.where(picked, logits, -1e30), 0, keepdims=True)
     powers = jnp.where(picked, jnp.exp(jnp.where(picked, logits - peak, 0.0)), 0.0)
     r.routes[ctx, 8:16, :] = powers / jnp.sum(powers, 0, keepdims=True)
+    r.routes[ctx, 16:24, :] = jnp.transpose(jnp.where(lane == 0, reach, gap))[0:8]
+    r.routes[ctx, 18:19, :] = r.remaining[...]
+    r.routes[ctx, 19:20, :] = r.left_cot[...]
     route_sends = direct_send(r.routes.at[ctx], r.direct_sems.at[1], r.direct_recvs.at[1], length)
     for copy in route_sends:
         copy.start()
@@ -860,22 +865,7 @@
         lines.append(jnp.zeros((8 - 2 * EXP_DEV, tokens), f32))
         sheet = jnp.concatenate(lines, 0)
 
-        @pl.when(source == ctx)
-        def _():
-            r.scores_back[ctx] = sheet
-
-        @pl.when(source != ctx)
-        def _():
-            r.score_sent[source] = sheet
-            offset = (source - ctx + length) % length
-            remote(
-                r.score_sent.at[source],
-                r.scores_back.at[ctx],
-                r.direct_sems.at[2, offset - 1],
-                r.direct_recvs.at[2, offset - 1],
-                (source, me[1], me[2]),
-            ).start()
-
+        r.scores[ctx, source] = sheet
         return carried
 
     lower = ctx < length // 2
@@ -921,20 +911,14 @@
     cot_gather.relay(length - 1)
     score(last, 0)
     cot_gather.drain()
+    score_sends = direct_send(r.scores.at[ctx], r.direct_sems.at[2], r.direct_recvs.at[2], length)
+    for copy in score_sends:
+        copy.start()
     mixed, unused = returns(length, r)
     for index in range(2):
         give_back(length, r, mixed.far + index)
-    direct_wait(lambda b: r.scores_back.at[b], r.direct_sems.at[2], r.direct_recvs.at[2], length)
-    for step in range(1, length):
-        target = moved(me, step, length)
-        remote(
-            r.score_sent.at[target[0]],
-            r.scores_back.at[ctx],
-            r.direct_sems.at[2, step - 1],
-            r.direct_recvs.at[2, step - 1],
-            target,
-        ).wait_send()
-    for copy in keyval_sends + route_sends:
+    direct_wait(lambda b: r.scores.at[b], r.direct_sems.at[2], r.direct_recvs.at[2], length)
+    for copy in keyval_sends + route_sends + score_sends:
         copy.wait_send()
     for copy in pack_sends:
         copy.wait_send()
@@ -1118,80 +1102,74 @@
         self.me, self.twin, self.beside, self.above, unused = places()
         self.chip, self.core, self.line = self.me[1] // 2, self.me[1] % 2, self.me[2]
 
-    def rows(self, which, chip, core, line, count):
+    def rows(self, which, expert, chip, core, line, count):
         size = self.counts[which]
         start = pl.multiple_of(((chip * 2 + core) * 2 + line) * size, size)
-        return self.arrays[which].at[:, pl.ds(start, count * size), :]
-
-    def copy(self, source, target, slot, device):
-        return remote(source, target, self.send.at[slot], self.recv.at[slot], device)
-
-    def half(self, which, chip, core):
-        return self.copy(
-            self.rows(which, chip, core, 0, 2), self.halves[which].at[chip], 2 * which + chip, self.twin
-        )
+        return self.arrays[which].at[expert, pl.ds(start, count * size), :]
+
+    def copy(self, source, target, which, expert, slot, device):
+        unit = 2 * which + expert
+        return remote(source, target, self.send.at[unit, slot], self.recv.at[unit, slot], device)
+
+    def half(self, which, expert, chip, core):
+        source = self.rows(which, expert, chip, core, 0, 2)
+        return self.copy(source, self.halves[which].at[chip, expert], which, expert, chip, self.twin)
 
     def start(self, which):
-        for chip in range(2):
-            self.half(which, chip, 1 - self.core).start()
-
-    def side(self, which):
-        if which == 0:
-            source = self.rows(0, 1 - self.chip, self.core, 0, 2)
-            return [self.copy(source, self.sides[0], 4, self.beside)]
-        return [
-            self.copy(
-                self.rows(1, chip, self.core, 1 - self.line, 1), self.sides[1].at[chip], 5 + chip, self.above
-            )
-            for chip in range(2)
-        ]
+        for expert in range(EXP_DEV):
+            for chip in range(2):
+                self.half(which, expert, chip, 1 - self.core).start()
+
+    def side(self, which, expert, index):
+        if expert == 0:
+            source, device = self.rows(which, 0, 1 - self.chip, self.core, index, 1), self.beside
+        else:
+            source, device = self.rows(which, 1, index, self.core, 1 - self.line, 1), self.above
+        return self.copy(source, self.sides[which].at[expert, index], which, expert, 2 + index, device)
 
     def add(self, view, other):
+        view[...] = (view[...].astype(jnp.float32) + other[...].astype(jnp.float32)).astype(jnp.bfloat16)
+
+    def add_halves(self, which):
         for expert in range(EXP_DEV):
-            both = view[expert].astype(jnp.float32) + other[expert].astype(jnp.float32)
-            view[expert] = both.astype(jnp.bfloat16)
-
-    def add_halves(self, which):
-        def one(chip, carried):
-            self.half(which, chip, self.core).wait_recv()
-            self.add(self.rows(which, chip, self.core, 0, 2), self.halves[which].at[chip])
-            return carried
-
-        lax.fori_loop(0, 2, one, 0)
-        for copy in self.side(which):
-            copy.start()
-
-    def last(self, which):
-        if which == 0:
-            source = self.rows(0, self.chip, self.core, 1 - self.line, 1)
-            return self.copy(source, self.lasts[0], 7, self.above)
-        source = self.rows(1, 1 - self.chip, self.core, self.line, 1)
-        return self.copy(source, self.lasts[1], 8, self.beside)
+            for chip in range(2):
+                self.half(which, expert, chip, self.core).wait_recv()
+                self.add(self.rows(which, expert, chip, self.core, 0, 2), self.halves[which].at[chip, expert])
+            for index in range(2):
+                self.side(which, expert, index).start()
+
+    def last(self, which, expert):
+        if expert == 0:
+            source, device = self.rows(which, 0, self.chip, self.core, 1 - self.line, 1), self.above
+        else:
+            source, device = self.rows(which, 1, 1 - self.chip, self.core, self.line, 1), self.beside
+        return self.copy(source, self.lasts[which].at[expert], which, expert, 4, device)
 
     def add_sides(self, which):
-        for copy in self.side(which):
-            copy.wait_recv()
-        if which == 0:
-            self.add(self.rows(0, self.chip, self.core, 0, 2), self.sides[0])
-        else:
-            for chip in range(2):
-                self.add(self.rows(1, chip, self.core, self.line, 1), self.sides[1].at[chip])
-        self.last(which).start()
+        for expert in range(EXP_DEV):
+            for index in range(2):
+                self.side(which, expert, index).wait_recv()
+                chip, line = (self.chip, index) if expert == 0 else (index, self.line)
+                self.add(
+                    self.rows(which, expert, chip, self.core, line, 1), self.sides[which].at[expert, index]
+                )
+            self.last(which, expert).start()
 
     def total(self, which, result):
-        self.last(which).wait_recv()
-        view = self.rows(which, self.chip, self.core, self.line, 1)
         for expert in range(EXP_DEV):
-            both = view[expert].astype(jnp.float32) + self.lasts[which][expert].astype(jnp.float32)
+            self.last(which, expert).wait_recv()
+            view = self.rows(which, expert, self.chip, self.core, self.line, 1)
+            both = view[...].astype(jnp.float32) + self.lasts[which][expert].astype(jnp.float32)
             result[expert] = both.astype(jnp.bfloat16)
 
     def drain(self):
         for which in range(2):
-            for chip in range(2):
-                self.half(which, chip, 1 - self.core).wait_send()
-            for copy in self.side(which):
-                copy.wait_send()
-            self.last(which).wait_send()
+            for expert in range(EXP_DEV):
+                for chip in range(2):
+                    self.half(which, expert, chip, 1 - self.core).wait_send()
+                for index in range(2):
+                    self.side(which, expert, index).wait_send()
+                self.last(which, expert).wait_send()
 
 
 def backward_part(length, r):
@@ -1221,53 +1199,47 @@
 
     r.gsmall[...] = jnp.zeros_like(r.gsmall)
     mid = r.middle[...]
-    cot = r.cotangent[...]
     halt_row = r.small[36:37, :]
-    reach = jnp.sum(mid * halt_row, -1, keepdims=True)
-    gap = jnp.sum(cot * (r.states[...].astype(f32) - mid), -1, keepdims=True)
-    turned = jnp.transpose(jnp.where(lane == 0, reach, gap))[0:8]
-    gates = r.routes[ctx, 8:16, :]
-    toward = jnp.concatenate(
-        [r.scores_back[d, 2 * e : 2 * e + 1, :] for d in range(length) for e in range(EXP_DEV)], 0
-    )
-    against = jnp.concatenate(
-        [r.scores_back[d, 2 * e + 1 : 2 * e + 2, :] for d in range(length) for e in range(EXP_DEV)], 0
-    )
-    halting = jax.nn.sigmoid(turned[0:1] + jnp.sum(gates * toward, 0, keepdims=True))
-    stop_grad = turned[1:2] - jnp.sum(gates * against, 0, keepdims=True)
-    mass, left = r.remaining[...], r.left_cot[...]
-    stopped = mass * halting
-    halt_grad = (stop_grad - left) * mass * halting * (1.0 - halting)
+
+    def scalars(block):
+        gates = r.routes[block, 8:16, :]
+        lines = [
+            [r.scores[d, block, 2 * e + k : 2 * e + k + 1, :] for d in range(length) for e in range(EXP_DEV)]
+            for k in range(2)
+        ]
+        toward, against = (jnp.concatenate(item, 0) for item in lines)
+        own = r.routes[block, 16:24, :]
+        halting = jax.nn.sigmoid(own[0:1] + jnp.sum(gates * toward, 0, keepdims=True))
+        stop_grad = own[1:2] - jnp.sum(gates * against, 0, keepdims=True)
+        mass, left = own[2:3], own[3:4]
+        stopped = mass * halting
+        halt_grad = (stop_grad - left) * mass * halting * (1.0 - halting)
+        sheet = jnp.concatenate([1.0 - stopped, halt_grad, stopped, jnp.zeros((5, tokens), f32)], 0)
+        r.factors[block] = sheet
+        return gates, toward, against, halting, stop_grad, mass, left, stopped, halt_grad, sheet
+
+    def other(step, carried):
+        scalars((ctx + step) % length)
+        return carried
+
+    lax.fori_loop(1, length, other, 0)
+    gates, toward, against, halting, stop_grad, mass, left, stopped, halt_grad, sheet = scalars(ctx)
+    mixed, backs = returns(length, r)
+    mixed.start_far(0)
     r.rows_out[0:1, :] = mass * (1.0 - halting)
     r.rows_out[1:2, :] = stop_grad * halting + left * (1.0 - halting)
-    sheet = jnp.concatenate([1.0 - stopped, halt_grad, stopped, jnp.zeros((5, tokens), f32)], 0)
-    r.factors[ctx] = sheet
-    factor_sends = direct_send(r.factors.at[ctx], *sems(3), length)
-    for copy in factor_sends:
-        copy.start()
-    mixed, backs = returns(length, r)
-    for index in range(2):
-        mixed.start_far(index)
-    r.columns[...] = jnp.transpose(jnp.concatenate([sheet, jnp.zeros((120, tokens), f32)], 0))
+    turned = jnp.transpose(jnp.concatenate([sheet, jnp.zeros((120, tokens), f32)], 0))
+    r.columns[...] = jnp.where(lane < 8, turned, r.columns[...])
     gate_grad = (1.0 - stopped) * against + halt_grad * toward
     pick_grad = gates * (gate_grad - jnp.sum(gates * gate_grad, 0, keepdims=True))
     coarse = pick_grad.astype(bf16).astype(f32)
     r.pick_grads[...] = jnp.concatenate([coarse, pick_grad - coarse], 0).astype(bf16)
     sums = product(r.pick_grads[...], r.entering[ctx])
     r.gsmall[24:32, :] = sums[0:8] + sums[8:16]
-    keep_col, halt_col = r.columns[:, 0:1], r.columns[:, 1:2]
-    r.flow[...] = keep_col * cot + halt_col * halt_row
-    r.grad_states[...] = r.columns[:, 2:3] * cot
+    halt_col = r.columns[:, 1:2]
     r.gsmall[36:37, :] = jnp.sum(halt_col * mid, 0, keepdims=True)
 
     def rows_back(block):
-        @pl.when(block != ctx)
-        def _():
-            slot = (ctx - block + length) % length - 1
-            view = r.factors.at[block]
-            send, recv = sems(3)
-            remote(view, view, send.at[slot], recv.at[slot], (block, me[1], me[2])).wait_recv()
-
         for expert in range(EXP_DEV):
             chosen = picks(r, block, expert)
             keep = jnp.sum(chosen * r.factors[block, 0:1, :], -1, keepdims=True)
@@ -1283,61 +1255,46 @@
     side_blocks = length // 2
     side_rows = side_blocks * CAP
 
-    def side_back(turn, carried):
-        half = jnp.where(turn == 0, 1 - ctx // side_blocks, ctx // side_blocks)
-
-        def prepare(index, kept):
-            rows_back(half * side_blocks + index)
-            return kept
-
-        lax.fori_loop(0, side_blocks, prepare, 0)
-        rows = pl.ds(pl.multiple_of(half * side_rows, side_rows), side_rows)
-
-        def one(expert, kept):
-            def part(index, inside):
-                columns = pl.ds(pl.multiple_of(index * 512, 512), 512)
-                back = product(r.slot_cot[expert, rows, :], r.outer[expert, columns, :], ((1,), (1,)))
-                slope = r.slope[expert, rows, columns].astype(f32)
-                r.slope[expert, rows, columns] = (back * slope).astype(bf16)
-                return inside
-
-            lax.fori_loop(0, 4, part, 0)
+    def prepare(turn, carried):
+        rows_back((ctx + turn) % length)
+        return carried
+
+    def rows_of_half(half):
+        return pl.ds(pl.multiple_of(half * side_rows, side_rows), side_rows)
+
+    def hidden_back(half):
+        rows = rows_of_half(half)
+
+        def part(turn, carried):
+            expert, index = turn // 2, turn % 2
+            columns = pl.ds(pl.multiple_of(index * 1024, 1024), 1024)
+            back = product(r.slot_cot[expert, rows, :], r.outer[expert, columns, :], ((1,), (1,)))
+            slope = r.slope[expert, rows, columns].astype(f32)
+            r.slope[expert, rows, columns] = (back * slope).astype(bf16)
+            return carried
+
+        lax.fori_loop(0, 2 * EXP_DEV, part, 0)
+
+    def entering_back(half):
+        rows = rows_of_half(half)
+
+        def one(expert, carried):
             sent = product(r.slope[expert, rows, :], r.inner[expert], ((1,), (1,)))
             r.slot_back[expert] = sent.astype(bf16)
-            return kept
+            return carried
 
         lax.fori_loop(0, EXP_DEV, one, 0)
 
-        def send(index, kept):
+        def gather_up(index, carried):
             block = half * side_blocks + index
             total = 0.0
             for expert in range(EXP_DEV):
                 chosen = picks(r, block, expert).astype(bf16)
                 total = total + product(chosen, r.slot_back[expert, slots(index), :], ((0,), (0,)))
             r.entering[block] = total.astype(bf16)
-            return kept
-
-        lax.fori_loop(0, side_blocks, send, 0)
-
-        @pl.when(turn == 0)
-        def _():
-            for index in range(2):
-                backs.start_far(index)
-            mixed.pass_on(0)
-
-        return carried
-
-    lax.fori_loop(0, 2, side_back, 0)
-    backs.start_near()
-    mixed.pass_on(1)
-    give_back(length, r, backs.next[0])
-    mixed.start_near()
-    give_back(length, r, ctx)
-
-    experts = ExpertReduce(
-        r.inner, r.outer, r.half_in, r.half_out, r.side_in, r.side_out, r.last_in, r.last_out,
-        r.expert_send, r.expert_recv,
-    )
+            return carried
+
+        lax.fori_loop(0, side_blocks, gather_up, 0)
 
     def outer_grad(turn, carried):
         expert, part = turn // 4, turn % 4
@@ -1346,10 +1303,6 @@
         r.outer[expert, columns, :] = value.astype(bf16)
         return carried
 
-    lax.fori_loop(0, 4 * EXP_DEV, outer_grad, 0)
-    experts.start(1)
-    backs.pass_on(0)
-
     def inner_grad(turn, carried):
         expert, part = turn // 4, turn % 4
         columns = pl.ds(pl.multiple_of(part * 512, 512), 512)
@@ -1357,11 +1310,33 @@
         r.inner[expert, :, columns] = value.astype(bf16)
         return carried
 
+    near, far = ctx // side_blocks, 1 - ctx // side_blocks
+    experts = ExpertReduce(
+        r.inner, r.outer, r.half_in, r.half_out, r.side_in, r.side_out, r.last_in, r.last_out,
+        r.expert_send, r.expert_recv,
+    )
+    lax.fori_loop(0, length, prepare, 0)
+    hidden_back(far)
+    entering_back(far)
+    for index in range(2):
+        backs.start_far(index)
+    hidden_back(near)
+    lax.fori_loop(0, 4 * EXP_DEV, outer_grad, 0)
+    experts.start(1)
+    entering_back(near)
+    backs.start_near()
+    mixed.start_far(1)
+    experts.add_halves(1)
+    give_back(length, r, backs.next[0])
+    mixed.start_near()
+    give_back(length, r, ctx)
+    backs.pass_on(0)
     lax.fori_loop(0, 4 * EXP_DEV, inner_grad, 0)
     experts.start(0)
-    experts.add_halves(1)
     backs.pass_on(1)
+    mixed.pass_on(0)
     experts.add_halves(0)
+    experts.add_sides(1)
 
     backs.wait()
     mid = r.middle[...]
@@ -1376,8 +1351,10 @@
     scaled = back * r.small[34:35, :]
     level = jnp.mean(scaled, -1, keepdims=True)
     tilt = jnp.mean(scaled * plain, -1, keepdims=True)
-    flow = r.flow[...] + inverse * (scaled - level - plain * tilt)
-    r.flow[...] = flow
+    cot = r.cotangent[...]
+    flow = r.columns[:, 0:1] * cot + r.columns[:, 1:2] * halt_row
+    flow = flow + inverse * (scaled - level - plain * tilt)
+    r.grad_states[...] = flow + r.columns[:, 2:3] * cot
     attn_grad = flow.astype(bf16)
 
     def project_piece(chip, core):
@@ -1402,7 +1379,7 @@
             for j in range(MOA_TOP):
                 wanted = id_lanes[j] - side == 2 * (2 * part + pair)
                 chosen[j] = chosen[j] + jnp.where(wanted, block, 0.0)
-    gate_lanes = [r.head_gates[:, j : j + 1] for j in range(MOA_TOP)]
+    gate_lanes = [r.columns[:, 8 + j : 9 + j] for j in range(MOA_TOP)]
     gate_grads = []
     for j in range(MOA_TOP):
         rows = slice(j * tokens, (j + 1) * tokens)
@@ -1425,6 +1402,8 @@
     chooser = r.small[...].astype(bf16)
     r.cotangent[...] = product(coarse, chooser) + product(fine, chooser)
     project_reduce.add_halves()
+    mixed.pass_on(1)
+    experts.add_sides(0)
 
     r.kv_grad[...] = jnp.zeros_like(r.kv_grad)
     chunk = 256
@@ -1432,14 +1411,6 @@
     half_keys = length * tokens // 2
 
     def attend_back(turn, carried):
-        @pl.when(turn == 4)
-        def _():
-            experts.add_sides(1)
-
-        @pl.when(turn == 8)
-        def _():
-            experts.add_sides(0)
-
         rows = pl.ds(pl.multiple_of((turn // 2) * chunk, chunk), chunk)
         keys = pl.ds(pl.multiple_of((turn % 2) * half_keys, half_keys), half_keys)
         query, grads, keyval = r.queries[rows, :], r.heads_grad[rows, :], r.keyval[keys, :]
@@ -1523,7 +1494,7 @@
     level = jnp.mean(scaled, -1, keepdims=True)
     tilt = jnp.mean(scaled * plain, -1, keepdims=True)
     r.grad_states[...] = (
-        r.grad_states[...] + r.flow[...] + inverse * (scaled - level - plain * tilt)
+        r.grad_states[...] + inverse * (scaled - level - plain * tilt)
     )
     small_reduce.add_halves()
     project_line.share_out()
@@ -1545,8 +1516,6 @@
     r.grad_query[...] = query_line.finish()
     r.grad_small[...] = small_line.finish()
 
-    for copy in factor_sends:
-        copy.wait_send()
     mixed.drain()
     backs.drain()
     sent_all(
@@ -1690,26 +1659,23 @@
         queries=vmem((MOA_TOP * tokens, 128), bf16),
         heads=vmem((MOA_TOP * tokens, 128), f32),
         keyval=vmem((length * tokens, 128), bf16),
-        head_gates=vmem((tokens, 128), f32),
         middle=vmem((tokens, D), f32),
         entering=vmem((length, tokens, D), bf16),
         cots=vmem((length, tokens, D), bf16),
-        routes=vmem((length, 16, tokens), f32),
-        scores_back=vmem((length, 8, tokens), f32),
+        routes=vmem((length, 24, tokens), f32),
+        scores=vmem((length, length, 8, tokens), f32),
         small=vmem((128, D), f32),
-        score_sent=vmem((length, 8, tokens), f32),
         factors=vmem((length, 8, tokens), f32),
         columns=vmem((tokens, 128), f32),
         pick_grads=vmem((16, tokens), bf16),
         gsmall=vmem((128, D), f32),
-        flow=vmem((tokens, D), f32),
         slot_back=vmem((EXP_DEV, rows // 2, D), bf16),
         back_in=vmem((4, tokens, D), bf16),
         mix_in=vmem((4, tokens, D), bf16),
         half_in=vmem((2, EXP_DEV, 128, FF), bf16),
         half_out=vmem((2, EXP_DEV, 512, D), bf16),
-        side_in=vmem((EXP_DEV, 128, FF), bf16),
-        side_out=vmem((2, EXP_DEV, 256, D), bf16),
+        side_in=vmem((EXP_DEV, 2, 64, FF), bf16),
+        side_out=vmem((EXP_DEV, 2, 256, D), bf16),
         last_in=vmem((EXP_DEV, 64, FF), bf16),
         last_out=vmem((EXP_DEV, 256, D), bf16),
         heads_grad=vmem((MOA_TOP * tokens, 128), bf16),
@@ -1742,8 +1708,8 @@
         direct_recvs=dma((13, length)),
         return_send=dma((2, 5)),
         return_recv=dma((2, 5)),
-        expert_send=dma((9,)),
-        expert_recv=dma((9,)),
+        expert_send=dma((4, 5)),
+        expert_recv=dma((4, 5)),
         dense_send=dma((3, 5)),
         dense_recv=dma((3, 5)),
     )

time: 194 us -> 180 us (0.928)
  Pallas kernels: 192 us -> 178 us
    pallas_call x1, Pallas kernels: 188 us -> 174 us  [fast_body(): pl.pallas_call(partial(whole_kernel, length, names), out_shape=tuple(outp...]
where the time goes in v4:
time: 180 us
  Pallas kernels  178 us (99%)
    pallas_call x1, Pallas kernels, fast_body(): pl.pallas_call(partial(whole_kernel, length, names), out_shape=tuple(outp...  174 us
    pallas_call x1, Pallas kernels, write_out(): pl.pallas_call(write_kernel, out_shape=outs, in_specs=[in_vmem] * len(res...  3.87 us

profile of v4, /device:TPU:0, one launch (start us, length us, event | category | flops | bytes accessed | tf_op | source)
XLA Modules:
  0.0 179.7 jit_solution(5637338840579212137)
XLA Ops:
  0.6 0.0 copy-start.3
  0.7 0.0 copy-start.4
  0.7 0.0 copy-start
  0.7 0.0 copy-start.1
  0.7 0.0 copy-start.2
  0.7 0.6 copy-done.3
  1.3 0.0 copy-done.4
  1.3 0.0 copy-done
  1.3 0.0 copy-done.1
  1.4 0.0 copy-done.2
  1.4 0.6 stack.27.refs_9_
  2.0 173.8 %layer_step.1 = (bf16[384,512]{1,0:T(8,128)(2,1)}, f32[8,384]{1,0:T(8,128)}, f32[384,512]{1,0:T(8,128)}, bf16[64,1536]{1,0:T(8,128)(2,1)}, bf16[192,512]{1,0:T(8...) custom-call(bf16[384,512]{1,0:T(8,128)(2,1)} %bitcast.23, ...), custom_call_target="tpu_custom_call" | custom-call | tf_op jit(solution)/shard_map/layer_step/pallas_call | solution.py:1719
  175.8 3.9 %write_out.1 = (bf16[1,384,512]{2,1,0:T(8,128)(2,1)}, f32[1,384]{1,0:T(1,128)}, f32[1,384,512]{2,1,0:T(8,128)}, f32[1,384]{1,0:T(1,128)}, f32[64,1536]{1,0:T(8,1...) custom-call(bf16[384,512]{1,0:T(8,128)(2,1)} %get-tuple-element.40.n, ...), custom_call_target="tpu_custom_call" | custom-call | tf_op jit(solution)/shard_map/write_out/pallas_call | solution.py:1574
  (2 shorter events, 0.0 us)
Async XLA Ops:
  0.6 0.7 copy-start.3
  0.7 0.7 copy-start.4
  0.7 0.7 copy-start
  0.7 0.7 copy-start.1
  0.7 0.7 copy-start.2

commit v5 on v4

--- a/solution.py
+++ b/solution.py
@@ -1406,13 +1406,13 @@
     experts.add_sides(0)
 
     r.kv_grad[...] = jnp.zeros_like(r.kv_grad)
-    chunk = 256
-
-    half_keys = length * tokens // 2
+    chunk = 512
+
+    half_keys = tokens
 
     def attend_back(turn, carried):
-        rows = pl.ds(pl.multiple_of((turn // 2) * chunk, chunk), chunk)
-        keys = pl.ds(pl.multiple_of((turn % 2) * half_keys, half_keys), half_keys)
+        rows = pl.ds(pl.multiple_of((turn // length) * chunk, chunk), chunk)
+        keys = pl.ds(pl.multiple_of((turn % length) * half_keys, half_keys), half_keys)
         query, grads, keyval = r.queries[rows, :], r.heads_grad[rows, :], r.keyval[keys, :]
         scores = product(keyval, query, ((1,), (1,)))
         weights = jnp.exp(scores - r.stats[0:1, rows])
@@ -1421,17 +1421,17 @@
         r.kv_grad[keys, :] += product(score_grad, query) + product(weights.astype(bf16), grads)
         down = product(score_grad, keyval, ((0,), (0,))) * HS ** (-0.5)
 
-        @pl.when(turn % 2 == 0)
+        @pl.when(turn % length == 0)
         def _():
             r.heads[rows, :] = down
 
-        @pl.when(turn % 2 == 1)
+        @pl.when(turn % length > 0)
         def _():
             r.heads[rows, :] += down
 
         return carried
 
-    lax.fori_loop(0, 2 * MOA_TOP * tokens // chunk, attend_back, 0)
+    lax.fori_loop(0, length * MOA_TOP * tokens // chunk, attend_back, 0)
 
     def send_keyval(turn, carried):
         block = (ctx + turn) % length

time: 180 us -> 180 us (level)
  no operation moved by 1% of the time
where the time goes in v5:
time: 180 us; the launch traced here: 179 us
  Pallas kernels  177 us (98%)
    pallas_call x1, Pallas kernels, fast_body(): pl.pallas_call(partial(whole_kernel, length, names), out_shape=tuple(outp...  174 us
    pallas_call x1, Pallas kernels, write_out(): pl.pallas_call(write_kernel, out_shape=outs, in_specs=[in_vmem] * len(res...  3.87 us

profile of v5, /device:TPU:0, one launch (start us, length us, event | category | flops | bytes accessed | tf_op | source)
XLA Modules:
  0.0 179.5 jit_solution(3789887638203178261)
XLA Ops:
  0.6 0.0 copy-start.3
  0.7 0.0 copy-start.4
  0.7 0.0 copy-start
  0.7 0.0 copy-start.1
  0.7 0.0 copy-start.2
  0.7 0.6 copy-done.3
  1.3 0.0 copy-done.4
  1.3 0.0 copy-done
  1.3 0.0 copy-done.1
  1.4 0.0 copy-done.2
  1.4 0.6 stack.27.refs_9_
  2.0 173.6 %layer_step.1 = (bf16[384,512]{1,0:T(8,128)(2,1)}, f32[8,384]{1,0:T(8,128)}, f32[384,512]{1,0:T(8,128)}, bf16[64,1536]{1,0:T(8,128)(2,1)}, bf16[192,512]{1,0:T(8...) custom-call(bf16[384,512]{1,0:T(8,128)(2,1)} %bitcast.23, ...), custom_call_target="tpu_custom_call" | custom-call | tf_op jit(solution)/shard_map/layer_step/pallas_call | solution.py:1719
  175.6 3.9 %write_out.1 = (bf16[1,384,512]{2,1,0:T(8,128)(2,1)}, f32[1,384]{1,0:T(1,128)}, f32[1,384,512]{2,1,0:T(8,128)}, f32[1,384]{1,0:T(1,128)}, f32[64,1536]{1,0:T(8,1...) custom-call(bf16[384,512]{1,0:T(8,128)(2,1)} %get-tuple-element.40.n, ...), custom_call_target="tpu_custom_call" | custom-call | tf_op jit(solution)/shard_map/write_out/pallas_call | solution.py:1574
  (2 shorter events, 0.0 us)
Async XLA Ops:
  0.6 0.7 copy-start.3
  0.7 0.7 copy-start.4
  0.7 0.7 copy-start
  0.7 0.7 copy-start.1
  0.7 0.7 copy-start.2
